TPU v7x, 256 devices: a whole 4x4x8 slice. The times are simulated.
256 devices in a mesh: src: 16 (over y_lo, x, core), rec: 16 (over y_hi, z).
Axes of the slice: x: 4, y: 4 (y_hi: 2, y_lo: 2; y = y_hi * 2 + y_lo), z: 8, core: 2. Of those that a mesh axis runs over, the one named last changes fastest.
Arguments:
- kernel: bfloat16 [2, 32, 4096, 4096], P(None, None, 'src', 'rec'), may hold values from -0.09375 to 0.09375
- focusing: float32 [64, 4096, 128], P(None, ('rec', 'src')), may hold values from -6 to 6
- first_arrival: float32 [64, 4096, 128], P(None, ('rec', 'src')), may hold values from -6 to 6
- onset: int32 [64, 4096], replicated, may hold values from 32 to 127
Outputs:
- upgoing: float32 [64, 4096, 128], P(None, ('src', 'rec'))
- downgoing: float32 [64, 4096, 128], P(None, ('rec', 'src'))
All inputs are finite; a program needn't handle non-finite values.
Results may differ from a plain program's by a relative error of at most 0.0029.
Values may be sent and summed in bfloat16 or wider, within the bound.
No kernel may reach another device: no remote copies, remote signals or barrier semaphores. Data moves between devices by JAX's collectives and lax.ppermute only.
A program may use at most 128 MiB of HBM per device.

v0:
```python
import functools

import numpy as np
import jax
import jax.numpy as jnp
from jax import lax
from jax.experimental import pallas as pl
from jax.experimental.pallas import tpu as pltpu
from jax.sharding import Mesh, PartitionSpec as P

HIGH = lax.Precision.HIGHEST
F32 = jnp.float32
BF16 = jnp.bfloat16
UNROLL = 8
NX, NZ = 4, 8
PAIRS = [(a, b) for a in range(2) for b in range(NX)]


def table(count, samples, flipped):
    steps = np.arange(samples)
    if flipped:
        steps = samples - 1 - steps
    waves = np.arange(count) + 1
    angle = (waves[:, None] * steps[None, :] % samples) * (2.0 * np.pi / samples)
    return np.concatenate([np.cos(angle), -np.sin(angle)]).astype(np.float32)


def local(body, outs, args, scratch=(), limit=4, source=None):
    vmem = pl.BlockSpec(memory_space=pltpu.VMEM)
    extra = []
    if source is not None:
        extra = [pltpu.with_memory_space_constraint(source, pltpu.HBM)]
    return pl.pallas_call(
        body,
        in_specs=[pl.BlockSpec(memory_space=pltpu.HBM)] * len(extra) + [vmem] * len(args),
        out_specs=[vmem] * len(outs),
        out_shape=[pltpu.VMEM(shape, dtype) for shape, dtype in outs],
        scratch_shapes=list(scratch),
        compiler_params=pltpu.CompilerParams(vmem_limit_bytes=limit << 20),
    )(*extra, *[pltpu.with_memory_space_constraint(arg, pltpu.VMEM) for arg in args])


def src_at(dyl, dx, dc):
    yl, x, c = lax.axis_index("yl"), lax.axis_index("x"), lax.axis_index("c")
    return ((yl + dyl) & 1) * (2 * NX) + ((x + dx) & (NX - 1)) * 2 + ((c + dc) & 1)


def rec_at(dyh, dz):
    yh, z = lax.axis_index("yh"), lax.axis_index("z")
    return ((yh + dyh) & 1) * NZ + ((z + dz) & (NZ - 1))


def to_spec(forward, trace):
    dims = (((1,), (1,)), ((), ()))
    both = lax.dot_general(forward, trace, dims, precision=HIGH, preferred_element_type=F32)
    half = both.shape[0] // 2
    return jnp.concatenate([both[:half], both[half:]], axis=1)


def from_spec(packed, inverse):
    half = packed.shape[1] // 2
    stacked = jnp.concatenate([packed[:, :half], packed[:, half:]], axis=0)
    dims = (((0,), (0,)), ((), ()))
    return lax.dot_general(stacked, inverse, dims, precision=HIGH, preferred_element_type=F32)


def spectra_body(forward, traces, out, buf):
    for n in range(traces.shape[1]):
        buf[:, n, :] = to_spec(forward[...], traces[:, n, :])
    out[...] = buf[...].astype(BF16)


def middle_body(forward, inverse, onset, plus, minus, share, taken, upgoing, out, total, buf):
    total[...] = plus[...].astype(F32) + minus[...].astype(F32) + share[...] + taken[...]
    points, width, samples = upgoing.shape
    time = lax.broadcasted_iota(jnp.int32, (points, samples), 1)
    for n in range(width):
        trace = from_spec(total[:, n, :], inverse[...])
        trace = jnp.where(time < onset[:, n : n + 1], trace, 0.0)
        upgoing[:, n, :] = trace
        buf[:, n, :] = to_spec(forward[...], trace)
    out[...] = buf[...].astype(BF16)


def last_body(inverse, onset, first, kept, taken, downgoing, total):
    total[...] = kept[...] + taken[...].astype(F32)
    points, width, samples = downgoing.shape
    time = lax.broadcasted_iota(jnp.int32, (points, samples), 1)
    for n in range(width):
        trace = from_spec(total[:, n, :], inverse[...])
        trace = jnp.where(time < onset[:, n : n + 1], trace, 0.0)
        downgoing[:, n, :] = first[:, n, :] - trace


def cross(direct, turned, sign):
    half = turned.shape[1] // 2
    lane = lax.broadcasted_iota(jnp.int32, turned.shape, 1)
    swapped = pltpu.roll(turned, half, 1)
    return direct + jnp.where(lane < half, -sign * swapped, sign * swapped)


def stream(kernel, held_kernel, arrived, prepare, one):
    groups = kernel.shape[1] // UNROLL

    def fetch(i):
        part = pl.ds(i * UNROLL, UNROLL)
        return pltpu.make_async_copy(kernel.at[:, part], held_kernel.at[:, part], arrived.at[i])

    for i in range(groups):
        fetch(i).start()
    prepare()

    def step(i, carry):
        fetch(i).wait()
        for u in range(UNROLL):
            one(i * UNROLL + u, u)
        return carry

    lax.fori_loop(0, groups, step, 0)


def pack_body(*refs):
    for i, ref in enumerate(refs[:-1]):
        refs[-1][i] = ref[...]


def pick_body(plus, minus, out_p, out_m):
    out_p[...] = plus[0]
    out_m[...] = minus[1]


def unpack(refs, spec, places):
    places = list(places)
    for ref in refs:
        if len(ref.shape) == 3:
            spec[:, places.pop(0)] = ref[...]
        else:
            for i in range(ref.shape[0]):
                spec[:, places.pop(0)] = ref[i]


def conv_body(source, *refs, spots, pieces):
    ins, outs, (spec, kernel, arrived) = refs[:pieces], refs[pieces:-3], refs[-3:]
    width, lanes = ins[0].shape[-2:]
    order = [(s, dz) for s in range(2) for dz in range(NZ)]
    firsts = [pl.multiple_of(rec_at(1 - s, dz) * width, width) for s, dz in order]
    size = len(order) * width

    def prepare():
        unpack(ins, spec, [src_at(*spot) for spot in spots])

    def one(kk, u):
        rhs = spec[kk].reshape(len(spots) * width, lanes)
        rows = [kernel[c, kk, pl.ds(first, width), :] for c in range(2) for first in firsts]
        both = jnp.dot(jnp.concatenate(rows, axis=0), rhs, preferred_element_type=F32)
        out = cross(both[:size], both[size:], 1.0)
        for j in range(len(order)):
            outs[j][kk] = out[j * width : (j + 1) * width].astype(outs[j].dtype)

    stream(source, kernel, arrived, prepare, one)


def corr_body(source, *refs, spots, pieces):
    ins, (away, stay, spec, total, kernel, arrived) = refs[:pieces], refs[pieces:]
    width, lanes = ins[0].shape[-2:]
    near = [src_at(a, b, 0) for a, b in PAIRS]
    far = [src_at(a, b, 1) for a, b in PAIRS]

    def prepare():
        unpack(ins, spec, [rec_at(*spot) for spot in spots])

    def one(kk, u):
        turned = spec[kk].reshape(len(spots) * width, lanes).T
        real, imag = [jnp.dot(turned, kernel[c, kk], preferred_element_type=F32) for c in range(2)]
        half = lanes // 2
        out = jnp.concatenate([real[:half] + imag[half:], real[half:] - imag[:half]], axis=0).T
        total[u] = out.reshape(-1, width, lanes)
        for j in range(len(PAIRS)):
            stay[j, kk] = total[u, near[j]]
            away[j, kk] = total[u, far[j]].astype(BF16)

    stream(source, kernel, arrived, prepare, one)


def hop_body(taken, share, out):
    out[...] = (taken[...].astype(F32) + share[...]).astype(BF16)


def meet_body(one_way, other_way, share, out):
    out[...] = one_way[...].astype(F32) + other_way[...].astype(F32) + share[...]


def held(stay, taken, s, b):
    j = PAIRS.index((1 - s, b))
    return stay[j] + taken[j].astype(F32)


def lead_x_body(stay, taken, out_p, out_m):
    out_p[...] = held(stay, taken, 0, 2).astype(BF16)
    out_m[...] = held(stay, taken, 1, 2).astype(BF16)


def turn_x_body(plus, minus, stay, taken, out_p, out_m):
    out_p[0] = (plus[...].astype(F32) + held(stay, taken, 0, 1)).astype(BF16)
    out_p[1] = held(stay, taken, 1, 1).astype(BF16)
    out_m[0] = held(stay, taken, 0, 3).astype(BF16)
    out_m[1] = (minus[...].astype(F32) + held(stay, taken, 1, 3)).astype(BF16)


def meet_x_body(plus, minus, stay, taken, send, keep):
    send[...] = (plus[0].astype(F32) + minus[0].astype(F32) + held(stay, taken, 0, 0)).astype(BF16)
    keep[...] = plus[1].astype(F32) + minus[1].astype(F32) + held(stay, taken, 1, 0)


def move(value, axis, step):
    size = lax.axis_size(axis)
    return lax.ppermute(value, axis, [(i, (i + step) % size) for i in range(size)])


def per_device(kernel, focusing, first_arrival, onset):
    points, width, samples = focusing.shape
    count = kernel.shape[1]
    lanes = 2 * points
    forward = jnp.asarray(table(count, samples, False))
    inverse = forward * (2.0 / samples)
    rinverse = jnp.asarray(table(count, samples, True)) * (2.0 / samples)
    src, rec = src_at(0, 0, 0), rec_at(0, 0)
    one, two = (count, width, lanes), (2, count, width, lanes)
    limits_up = lax.dynamic_slice_in_dim(onset, (src * 2 * NZ + rec) * width, width, 1)
    limits_down = lax.dynamic_slice_in_dim(onset, (rec * 4 * NX + src) * width, width, 1)
    buf = pltpu.VMEM(one, F32)
    bulk = [
        pltpu.VMEM(kernel.shape, BF16),
        pltpu.SemaphoreType.DMA((count // UNROLL,)),
    ]

    (own,) = local(spectra_body, [(one, BF16)], [forward, focusing], [buf])
    near = {(0, 0): own}
    near[0, -1] = move(own, "x", 1)
    near[0, 1] = move(own, "x", -1)
    near[1, 0] = move(own, "yl", 1)
    near[0, 2] = move(near[0, -1], "x", 1)
    near[1, 1] = move(near[1, 0], "x", -1)
    near[1, -1] = move(near[1, 0], "x", 1)
    near[1, 2] = move(near[1, 1], "x", -1)
    groups = [[(0, 0), (1, 0), (0, -1), (0, 1)], [(1, 1), (1, -1), (0, 2), (1, 2)]]
    pieces = list(near.values())
    spots = [key + (0,) for key in near] + [key + (1,) for group in groups for key in group]
    for group in groups:
        (packed,) = local(pack_body, [((len(group),) + one, BF16)], [near[key] for key in group])
        pieces.append(move(packed, "c", 1))
    full = (len(spots), width, lanes)

    leads = [(0, 4), (0, 5), (1, 3), (1, 4)]
    order = [(s, dz) for s in range(2) for dz in range(NZ)]
    outs = local(
        functools.partial(conv_body, spots=spots, pieces=len(pieces)),
        [(one, BF16 if key in leads else F32) for key in order],
        pieces,
        [pltpu.VMEM((count,) + full, BF16)] + bulk,
        14,
        kernel,
    )
    share = dict(zip(order, outs))
    sums = {}
    for s in range(2):
        for sign, tag in ((1, "p"), (-1, "m")):
            hops = NZ // 2 - (tag == "mp"[s])
            value = share[s, sign * hops % NZ]
            for i in range(1, hops + 1):
                value = move(value, "z", sign)
                if i < hops:
                    left = share[s, sign * (hops - i) % NZ]
                    (value,) = local(hop_body, [(one, BF16)], [value, left])
            sums[s, tag] = value
    (send,) = local(meet_body, [(one, F32)], [sums[0, "p"], sums[0, "m"], share[0, 0]])
    taken = move(send, "yh", 1)
    upgoing, mine = local(
        middle_body,
        [(focusing.shape, F32), (one, BF16)],
        [forward, inverse, limits_up, sums[1, "p"], sums[1, "m"], share[1, 0], taken],
        [buf, buf],
    )

    (pair,) = local(pack_body, [(two, BF16)], [mine, move(mine, "yh", 1)])
    plus = minus = pair
    pieces, spots = [pair], [(0, 0), (1, 0)]
    for i in range(1, NZ // 2):
        plus, minus = move(plus, "z", 1), move(minus, "z", -1)
        pieces += [plus, minus]
        spots += [(s, dz) for dz in (-i, i) for s in range(2)]
    plus, minus = local(pick_body, [(one, BF16)] * 2, [plus, minus])
    pieces += [move(plus, "z", 1), move(minus, "z", -1)]
    spots += [(s, NZ // 2) for s in range(2)]
    away, stay = local(
        functools.partial(corr_body, spots=spots, pieces=len(pieces)),
        [((len(PAIRS),) + one, BF16), ((len(PAIRS),) + one, F32)],
        pieces,
        [pltpu.VMEM((count,) + full, BF16), pltpu.VMEM((UNROLL,) + full, F32)] + bulk,
        18,
        kernel,
    )
    taken = move(away, "c", 1)
    plus, minus = local(lead_x_body, [(one, BF16)] * 2, [stay, taken])
    plus, minus = move(plus, "x", 1), move(minus, "x", -1)
    plus, minus = local(turn_x_body, [(two, BF16)] * 2, [plus, minus, stay, taken])
    plus, minus = move(plus, "x", 1), move(minus, "x", -1)
    send, keep = local(meet_x_body, [(one, BF16), (one, F32)], [plus, minus, stay, taken])
    (downgoing,) = local(
        last_body,
        [(focusing.shape, F32)],
        [rinverse, limits_down, first_arrival, keep, move(send, "yl", 1)],
        [buf],
    )
    return upgoing, downgoing


def solution(mesh):
    fine = Mesh(mesh.devices.reshape(2, NX, 2, 2, NZ), ("yl", "x", "c", "yh", "z"))
    src, rec = ("yl", "x", "c"), ("yh", "z")
    in_specs = (P(None, None, src, rec), P(None, rec + src, None), P(None, rec + src, None), P())
    out_specs = (P(None, src + rec, None), P(None, rec + src, None))

    return jax.shard_map(
        per_device, mesh=fine, in_specs=in_specs, out_specs=out_specs, check_vma=False
    )
```

profile of v0, /device:TPU:32, one launch (start us, length us, event | category | flops | bytes accessed | tf_op | source)
XLA Modules:
  0.0 140.6 jit_solution(17138646081549424383)
XLA Ops:
  6.7 2.2 %collective-permute-done.2.refs_1_.refs_3_ = bf16[32,16,128]{2,1,0:T(8,128)(2,1)S(1)} collective-permute-done((bf16[32,16,128]{2,1,0:T(8,128)(2,1)S(1)}, bf16[32,16,128]{2,1,0:T(8,128)(2,1)S(1)}, u32[]{:S(2)}, u32[]{:S(2)}) %collective-permute-start.2) | collective-permute-done | bytes 131104 | tf_op jit(solution)/shard_map/ppermute | solution.py:217
  8.8 2.8 %collective-permute-start.4 = (bf16[32,16,128]{2,1,0:T(8,128)(2,1)S(1)}, bf16[32,16,128]{2,1,0:T(8,128)(2,1)S(1)}, u32[]{:S(2)}, u32[]{:S(2)}) collective-permute-start(bf16[32,16,128]{2,1,0:T(8,128)(2,1)S(1)} %collective-permute-done.2.refs_1_.refs_3_), channel_id=1, source_target_pairs={{0,96},{32,0},{64,32},{96,64},{1,97},{33,1},{65,33},{97,65},{2,98}... | collective-permute-start | bytes 393224 | tf_op jit(solution)/shard_map/ppermute | solution.py:217
  14.9 3.7 %collective-permute-start.6 = (bf16[32,16,128]{2,1,0:T(8,128)(2,1)S(1)}, bf16[32,16,128]{2,1,0:T(8,128)(2,1)S(1)}, u32[]{:S(2)}, u32[]{:S(2)}) collective-permute-start(bf16[32,16,128]{2,1,0:T(8,128)(2,1)S(1)} %collective-permute-done.4.refs_0_.refs_5_), channel_id=1, source_target_pairs={{0,96},{32,0},{64,32},{96,64},{1,97},{33,1},{65,33},{97,65},{2,98}... | collective-permute-start | bytes 393224 | tf_op jit(solution)/shard_map/ppermute | solution.py:217
  23.2 5.0 %shard_map.80 = (f32[32,16,128]{2,1,0:T(8,128)S(1)}, f32[32,16,128]{2,1,0:T(8,128)S(1)}, f32[32,16,128]{2,1,0:T(8,128)S(1)}, f32[32,16,128]{2,1,0:T(8,128)S(1)},...) custom-call(bf16[2,32,256,256]{3,2,1,0:T(8,128)(2,1)} %source.3, ...), custom_call_target="tpu_custom_call" | custom-call | tf_op jit(solution)/shard_map/pallas_call | solution.py:33
  28.2 2.0 %collective-permute-start.16 = (bf16[32,16,128]{2,1,0:T(8,128)(2,1)S(1)}, bf16[32,16,128]{2,1,0:T(8,128)(2,1)S(1)}, u32[]{:S(2)}, u32[]{:S(2)}) collective-permute-start(bf16[32,16,128]{2,1,0:T(8,128)(2,1)S(1)} %get-tuple-element.38), channel_id=1, source_target_pairs={{0,1},{1,2},{2,3},{3,4},{4,5},{5,6},{6,7},{7,0},{8,9},{9,10},{10,1... | collective-permute-start | bytes 393224 | tf_op jit(solution)/shard_map/ppermute | solution.py:217
  30.3 3.5 %collective-permute-done.16.taken = bf16[32,16,128]{2,1,0:T(8,128)(2,1)S(1)} collective-permute-done((bf16[32,16,128]{2,1,0:T(8,128)(2,1)S(1)}, bf16[32,16,128]{2,1,0:T(8,128)(2,1)S(1)}, u32[]{:S(2)}, u32[]{:S(2)}) %collective-permute-start.16) | collective-permute-done | bytes 131104 | tf_op jit(solution)/shard_map/ppermute | solution.py:217
  33.9 2.0 %collective-permute-start.17 = (bf16[32,16,128]{2,1,0:T(8,128)(2,1)S(1)}, bf16[32,16,128]{2,1,0:T(8,128)(2,1)S(1)}, u32[]{:S(2)}, u32[]{:S(2)}) collective-permute-start(bf16[32,16,128]{2,1,0:T(8,128)(2,1)S(1)} %shard_map.86), channel_id=1, source_target_pairs={{0,1},{1,2},{2,3},{3,4},{4,5},{5,6},{6,7},{7,0},{8,9},{9,10},{10,1... | collective-permute-start | bytes 393224 | tf_op jit(solution)/shard_map/ppermute | solution.py:217
  35.9 2.4 %collective-permute-start.12 = (bf16[32,16,128]{2,1,0:T(8,128)(2,1)S(1)}, bf16[32,16,128]{2,1,0:T(8,128)(2,1)S(1)}, u32[]{:S(2)}, u32[]{:S(2)}) collective-permute-start(bf16[32,16,128]{2,1,0:T(8,128)(2,1)S(1)} %get-tuple-element.33), channel_id=1, source_target_pairs={{0,7},{1,0},{2,1},{3,2},{4,3},{5,4},{6,5},{7,6},{8,15},{9,8},{10,9... | collective-permute-start | bytes 393224 | tf_op jit(solution)/shard_map/ppermute | solution.py:217
  38.3 3.2 %collective-permute-start.21 = (bf16[32,16,128]{2,1,0:T(8,128)(2,1)S(1)}, bf16[32,16,128]{2,1,0:T(8,128)(2,1)S(1)}, u32[]{:S(2)}, u32[]{:S(2)}) collective-permute-start(bf16[32,16,128]{2,1,0:T(8,128)(2,1)S(1)} %shard_map.89), channel_id=1, source_target_pairs={{0,7},{1,0},{2,1},{3,2},{4,3},{5,4},{6,5},{7,6},{8,15},{9,8},{10,9... | collective-permute-start | bytes 393224 | tf_op jit(solution)/shard_map/ppermute | solution.py:217
  41.8 3.1 %collective-permute-start.9 = (bf16[32,16,128]{2,1,0:T(8,128)(2,1)S(1)}, bf16[32,16,128]{2,1,0:T(8,128)(2,1)S(1)}, u32[]{:S(2)}, u32[]{:S(2)}) collective-permute-start(bf16[32,16,128]{2,1,0:T(8,128)(2,1)S(1)} %get-tuple-element.30), channel_id=1, source_target_pairs={{0,1},{1,2},{2,3},{3,4},{4,5},{5,6},{6,7},{7,0},{8,9},{9,10},{10,1... | collective-permute-start | bytes 393224 | tf_op jit(solution)/shard_map/ppermute | solution.py:217
  45.2 3.8 %collective-permute-start.22 = (bf16[32,16,128]{2,1,0:T(8,128)(2,1)S(1)}, bf16[32,16,128]{2,1,0:T(8,128)(2,1)S(1)}, u32[]{:S(2)}, u32[]{:S(2)}) collective-permute-start(bf16[32,16,128]{2,1,0:T(8,128)(2,1)S(1)} %shard_map.90), channel_id=1, source_target_pairs={{0,7},{1,0},{2,1},{3,2},{4,3},{5,4},{6,5},{7,6},{8,15},{9,8},{10,9... | collective-permute-start | bytes 393224 | tf_op jit(solution)/shard_map/ppermute | solution.py:217
  49.7 2.2 %collective-permute-start.10 = (bf16[32,16,128]{2,1,0:T(8,128)(2,1)S(1)}, bf16[32,16,128]{2,1,0:T(8,128)(2,1)S(1)}, u32[]{:S(2)}, u32[]{:S(2)}) collective-permute-start(bf16[32,16,128]{2,1,0:T(8,128)(2,1)S(1)} %shard_map.81), channel_id=1, source_target_pairs={{0,1},{1,2},{2,3},{3,4},{4,5},{5,6},{6,7},{7,0},{8,9},{9,10},{10,1... | collective-permute-start | bytes 393224 | tf_op jit(solution)/shard_map/ppermute | solution.py:217
  54.2 3.3 %collective-permute-start.23 = (f32[32,16,128]{2,1,0:T(8,128)S(1)}, f32[32,16,128]{2,1,0:T(8,128)S(1)}, u32[]{:S(2)}, u32[]{:S(2)}) collective-permute-start(f32[32,16,128]{2,1,0:T(8,128)S(1)} %shard_map.91), channel_id=1, source_target_pairs={{0,8},{8,0},{1,9},{9,1},{2,10},{10,2},{3,11},{11,3},{4,12},{12,4},... | collective-permute-start | bytes 786440 | tf_op jit(solution)/shard_map/ppermute | solution.py:217
  57.5 2.0 %collective-permute-start.11 = (bf16[32,16,128]{2,1,0:T(8,128)(2,1)S(1)}, bf16[32,16,128]{2,1,0:T(8,128)(2,1)S(1)}, u32[]{:S(2)}, u32[]{:S(2)}) collective-permute-start(bf16[32,16,128]{2,1,0:T(8,128)(2,1)S(1)} %shard_map.82), channel_id=1, source_target_pairs={{0,1},{1,2},{2,3},{3,4},{4,5},{5,6},{6,7},{7,0},{8,9},{9,10},{10,1... | collective-permute-start | bytes 393224 | tf_op jit(solution)/shard_map/ppermute | solution.py:217
  64.6 2.7 %shard_map.92 = (f32[64,16,128]{2,1,0:T(8,128)S(1)}, bf16[32,16,128]{2,1,0:T(8,128)(2,1)S(1)}) custom-call(f32[64,128]{1,0:T(8,128)S(1)} %copy-done.3, f32[64,128]{1,0:T(8,128)S(1)} %copy-done.4, s32[64,16]{1,0:T(8,128)S(1)} %get-tuple-element.59.onset, bf16[32,16,128]{2,1,0:T(8,128)(2,1)S(1)} %collective-permute-done.11.plus, ...), custom_call_target="tpu_custom_call" | custom-call | tf_op jit(solution)/shard_map/pallas_call | solution.py:33
  67.2 2.3 %collective-permute-start.24 = (bf16[32,16,128]{2,1,0:T(8,128)(2,1)S(1)}, bf16[32,16,128]{2,1,0:T(8,128)(2,1)S(1)}, u32[]{:S(2)}, u32[]{:S(2)}) collective-permute-start(bf16[32,16,128]{2,1,0:T(8,128)(2,1)S(1)} %get-tuple-element.47.refs_0_), channel_id=1, source_target_pairs={{0,8},{8,0},{1,9},{9,1},{2,10},{10,2},{3,11},{11,3},{4,12},{12,4},... | collective-permute-start | bytes 393224 | tf_op jit(solution)/shard_map/ppermute | solution.py:217
  69.6 4.2 %collective-permute-done.24.refs_1_ = bf16[32,16,128]{2,1,0:T(8,128)(2,1)S(1)} collective-permute-done((bf16[32,16,128]{2,1,0:T(8,128)(2,1)S(1)}, bf16[32,16,128]{2,1,0:T(8,128)(2,1)S(1)}, u32[]{:S(2)}, u32[]{:S(2)}) %collective-permute-start.24) | collective-permute-done | bytes 131104 | tf_op jit(solution)/shard_map/ppermute | solution.py:217
  73.8 3.1 %collective-permute-start.25 = (bf16[2,32,16,128]{3,2,1,0:T(8,128)(2,1)S(1)}, bf16[2,32,16,128]{3,2,1,0:T(8,128)(2,1)S(1)}, u32[]{:S(2)}, u32[]{:S(2)}) collective-permute-start(bf16[2,32,16,128]{3,2,1,0:T(8,128)(2,1)S(1)} %shard_map.93.refs_0_), channel_id=1, source_target_pairs={{0,1},{1,2},{2,3},{3,4},{4,5},{5,6},{6,7},{7,0},{8,9},{9,10},{10,1... | collective-permute-start | bytes 786440 | tf_op jit(solution)/shard_map/ppermute | solution.py:217
  76.9 6.4 %collective-permute-done.25.refs_1_ = bf16[2,32,16,128]{3,2,1,0:T(8,128)(2,1)S(1)} collective-permute-done((bf16[2,32,16,128]{3,2,1,0:T(8,128)(2,1)S(1)}, bf16[2,32,16,128]{3,2,1,0:T(8,128)(2,1)S(1)}, u32[]{:S(2)}, u32[]{:S(2)}) %collective-permute-start.25) | collective-permute-done | bytes 262176 | tf_op jit(solution)/shard_map/ppermute | solution.py:217
  86.3 6.0 %collective-permute-done.27.refs_3_ = bf16[2,32,16,128]{3,2,1,0:T(8,128)(2,1)S(1)} collective-permute-done((bf16[2,32,16,128]{3,2,1,0:T(8,128)(2,1)S(1)}, bf16[2,32,16,128]{3,2,1,0:T(8,128)(2,1)S(1)}, u32[]{:S(2)}, u32[]{:S(2)}) %collective-permute-start.27) | collective-permute-done | bytes 262176 | tf_op jit(solution)/shard_map/ppermute | solution.py:217
  92.3 3.0 %collective-permute-start.30 = (bf16[2,32,16,128]{3,2,1,0:T(8,128)(2,1)S(1)}, bf16[2,32,16,128]{3,2,1,0:T(8,128)(2,1)S(1)}, u32[]{:S(2)}, u32[]{:S(2)}) collective-permute-start(bf16[2,32,16,128]{3,2,1,0:T(8,128)(2,1)S(1)} %collective-permute-done.28.refs_4_), channel_id=1, source_target_pairs={{0,7},{1,0},{2,1},{3,2},{4,3},{5,4},{6,5},{7,6},{8,15},{9,8},{10,9... | collective-permute-start | bytes 786440 | tf_op jit(solution)/shard_map/ppermute | solution.py:217
  95.2 4.3 %collective-permute-done.29.plus.refs_5_ = bf16[2,32,16,128]{3,2,1,0:T(8,128)(2,1)S(1)} collective-permute-done((bf16[2,32,16,128]{3,2,1,0:T(8,128)(2,1)S(1)}, bf16[2,32,16,128]{3,2,1,0:T(8,128)(2,1)S(1)}, u32[]{:S(2)}, u32[]{:S(2)}) %collective-permute-start.29) | collective-permute-done | bytes 262176 | tf_op jit(solution)/shard_map/ppermute | solution.py:217
  101.3 2.2 %collective-permute-start.31 = (bf16[32,16,128]{2,1,0:T(8,128)(2,1)S(1)}, bf16[32,16,128]{2,1,0:T(8,128)(2,1)S(1)}, u32[]{:S(2)}, u32[]{:S(2)}) collective-permute-start(bf16[32,16,128]{2,1,0:T(8,128)(2,1)S(1)} %get-tuple-element.48), channel_id=1, source_target_pairs={{0,1},{1,2},{2,3},{3,4},{4,5},{5,6},{6,7},{7,0},{8,9},{9,10},{10,1... | collective-permute-start | bytes 393224 | tf_op jit(solution)/shard_map/ppermute | solution.py:217
  103.5 2.8 %collective-permute-done.31.refs_7_ = bf16[32,16,128]{2,1,0:T(8,128)(2,1)S(1)} collective-permute-done((bf16[32,16,128]{2,1,0:T(8,128)(2,1)S(1)}, bf16[32,16,128]{2,1,0:T(8,128)(2,1)S(1)}, u32[]{:S(2)}, u32[]{:S(2)}) %collective-permute-start.31) | collective-permute-done | bytes 131104 | tf_op jit(solution)/shard_map/ppermute | solution.py:217
  106.3 3.0 %collective-permute-done.32.refs_8_ = bf16[32,16,128]{2,1,0:T(8,128)(2,1)S(1)} collective-permute-done((bf16[32,16,128]{2,1,0:T(8,128)(2,1)S(1)}, bf16[32,16,128]{2,1,0:T(8,128)(2,1)S(1)}, u32[]{:S(2)}, u32[]{:S(2)}) %collective-permute-start.32) | collective-permute-done | bytes 131104 | tf_op jit(solution)/shard_map/ppermute | solution.py:217
  109.4 4.5 %shard_map.95 = (bf16[8,32,16,128]{3,2,1,0:T(8,128)(2,1)S(1)}, f32[8,32,16,128]{3,2,1,0:T(8,128)S(1)}) custom-call(bf16[2,32,256,256]{3,2,1,0:T(8,128)(2,1)} %source.3, bf16[2,32,16,128]{3,2,1,0:T(8,128)(2,1)S(1)} %shard_map.93.refs_0_, bf16[2,32,16,128]{3,2,1,0:T(8,128)(2,1)S(1)} %collective-permute-done.25.refs_1_, ...), custom_call_target="tpu_custom_call" | custom-call | tf_op jit(solution)/shard_map/pallas_call | solution.py:33
  113.9 2.6 %collective-permute-done.33.taken = bf16[8,32,16,128]{3,2,1,0:T(8,128)(2,1)S(1)} collective-permute-done((bf16[8,32,16,128]{3,2,1,0:T(8,128)(2,1)S(1)}, bf16[8,32,16,128]{3,2,1,0:T(8,128)(2,1)S(1)}, u32[]{:S(2)}, u32[]{:S(2)}) %collective-permute-start.33) | collective-permute-done | bytes 1048608 | tf_op jit(solution)/shard_map/ppermute | solution.py:217
  117.0 3.5 %collective-permute-start.35 = (bf16[32,16,128]{2,1,0:T(8,128)(2,1)S(1)}, bf16[32,16,128]{2,1,0:T(8,128)(2,1)S(1)}, u32[]{:S(2)}, u32[]{:S(2)}) collective-permute-start(bf16[32,16,128]{2,1,0:T(8,128)(2,1)S(1)} %get-tuple-element.53), channel_id=1, source_target_pairs={{0,96},{32,0},{64,32},{96,64},{1,97},{33,1},{65,33},{97,65},{2,98}... | collective-permute-start | bytes 393224 | tf_op jit(solution)/shard_map/ppermute | solution.py:217
  120.5 3.7 %collective-permute-done.34.plus = bf16[32,16,128]{2,1,0:T(8,128)(2,1)S(1)} collective-permute-done((bf16[32,16,128]{2,1,0:T(8,128)(2,1)S(1)}, bf16[32,16,128]{2,1,0:T(8,128)(2,1)S(1)}, u32[]{:S(2)}, u32[]{:S(2)}) %collective-permute-start.34) | collective-permute-done | bytes 131104 | tf_op jit(solution)/shard_map/ppermute | solution.py:217
  125.5 2.1 %collective-permute-start.37 = (bf16[2,32,16,128]{3,2,1,0:T(8,128)(2,1)S(1)}, bf16[2,32,16,128]{3,2,1,0:T(8,128)(2,1)S(1)}, u32[]{:S(2)}, u32[]{:S(2)}) collective-permute-start(bf16[2,32,16,128]{3,2,1,0:T(8,128)(2,1)S(1)} %get-tuple-element.55), channel_id=1, source_target_pairs={{0,96},{32,0},{64,32},{96,64},{1,97},{33,1},{65,33},{97,65},{2,98}... | collective-permute-start | bytes 786440 | tf_op jit(solution)/shard_map/ppermute | solution.py:217
  127.6 5.7 %collective-permute-done.36.plus = bf16[2,32,16,128]{3,2,1,0:T(8,128)(2,1)S(1)} collective-permute-done((bf16[2,32,16,128]{3,2,1,0:T(8,128)(2,1)S(1)}, bf16[2,32,16,128]{3,2,1,0:T(8,128)(2,1)S(1)}, u32[]{:S(2)}, u32[]{:S(2)}) %collective-permute-start.36) | collective-permute-done | bytes 262176 | tf_op jit(solution)/shard_map/ppermute | solution.py:217
  135.1 3.4 %collective-permute-done.38.taken = bf16[32,16,128]{2,1,0:T(8,128)(2,1)S(1)} collective-permute-done((bf16[32,16,128]{2,1,0:T(8,128)(2,1)S(1)}, bf16[32,16,128]{2,1,0:T(8,128)(2,1)S(1)}, u32[]{:S(2)}, u32[]{:S(2)}) %collective-permute-start.38) | collective-permute-done | bytes 131104 | tf_op jit(solution)/shard_map/ppermute | solution.py:217
  (84 shorter events, 33.0 us)
Async XLA Ops:
  3.5 5.3 %collective-permute-start.2 = (bf16[32,16,128]{2,1,0:T(8,128)(2,1)S(1)}, bf16[32,16,128]{2,1,0:T(8,128)(2,1)S(1)}, u32[]{:S(2)}, u32[]{:S(2)}) collective-permute-start(bf16[32,16,128]{2,1,0:T(8,128)(2,1)S(1)} %shard_map.77.refs_0_), channel_id=1, source_target_pairs={{0,128},{128,0},{1,129},{129,1},{2,130},{130,2},{3,131},{131,3},{4... | collective-permute-start | bytes 393224 | tf_op jit(solution)/shard_map/ppermute | solution.py:217
  5.2 8.4 %collective-permute-start = (bf16[32,16,128]{2,1,0:T(8,128)(2,1)S(1)}, bf16[32,16,128]{2,1,0:T(8,128)(2,1)S(1)}, u32[]{:S(2)}, u32[]{:S(2)}) collective-permute-start(bf16[32,16,128]{2,1,0:T(8,128)(2,1)S(1)} %shard_map.77.refs_0_), channel_id=1, source_target_pairs={{0,32},{32,64},{64,96},{96,0},{1,33},{33,65},{65,97},{97,1},{2,34}... | collective-permute-start | bytes 393224 | tf_op jit(solution)/shard_map/ppermute | solution.py:217
  8.8 6.1 %collective-permute-start.4 = (bf16[32,16,128]{2,1,0:T(8,128)(2,1)S(1)}, bf16[32,16,128]{2,1,0:T(8,128)(2,1)S(1)}, u32[]{:S(2)}, u32[]{:S(2)}) collective-permute-start(bf16[32,16,128]{2,1,0:T(8,128)(2,1)S(1)} %collective-permute-done.2.refs_1_.refs_3_), channel_id=1, source_target_pairs={{0,96},{32,0},{64,32},{96,64},{1,97},{33,1},{65,33},{97,65},{2,98}... | collective-permute-start | bytes 393224 | tf_op jit(solution)/shard_map/ppermute | solution.py:217
  11.6 7.0 %collective-permute-start.1 = (bf16[32,16,128]{2,1,0:T(8,128)(2,1)S(1)}, bf16[32,16,128]{2,1,0:T(8,128)(2,1)S(1)}, u32[]{:S(2)}, u32[]{:S(2)}) collective-permute-start(bf16[32,16,128]{2,1,0:T(8,128)(2,1)S(1)} %shard_map.77.refs_0_), channel_id=1, source_target_pairs={{0,96},{32,0},{64,32},{96,64},{1,97},{33,1},{65,33},{97,65},{2,98}... | collective-permute-start | bytes 393224 | tf_op jit(solution)/shard_map/ppermute | solution.py:217
  12.4 6.4 %collective-permute-start.5 = (bf16[32,16,128]{2,1,0:T(8,128)(2,1)S(1)}, bf16[32,16,128]{2,1,0:T(8,128)(2,1)S(1)}, u32[]{:S(2)}, u32[]{:S(2)}) collective-permute-start(bf16[32,16,128]{2,1,0:T(8,128)(2,1)S(1)} %collective-permute-done.2.refs_1_.refs_3_), channel_id=1, source_target_pairs={{0,32},{32,64},{64,96},{96,0},{1,33},{33,65},{65,97},{97,1},{2,34}... | collective-permute-start | bytes 393224 | tf_op jit(solution)/shard_map/ppermute | solution.py:217
  13.6 6.6 %collective-permute-start.3 = (bf16[32,16,128]{2,1,0:T(8,128)(2,1)S(1)}, bf16[32,16,128]{2,1,0:T(8,128)(2,1)S(1)}, u32[]{:S(2)}, u32[]{:S(2)}) collective-permute-start(bf16[32,16,128]{2,1,0:T(8,128)(2,1)S(1)} %collective-permute-done.refs_2_.refs_1_), channel_id=1, source_target_pairs={{0,32},{32,64},{64,96},{96,0},{1,33},{33,65},{65,97},{97,1},{2,34}... | collective-permute-start | bytes 393224 | tf_op jit(solution)/shard_map/ppermute | solution.py:217
  14.9 6.2 %collective-permute-start.6 = (bf16[32,16,128]{2,1,0:T(8,128)(2,1)S(1)}, bf16[32,16,128]{2,1,0:T(8,128)(2,1)S(1)}, u32[]{:S(2)}, u32[]{:S(2)}) collective-permute-start(bf16[32,16,128]{2,1,0:T(8,128)(2,1)S(1)} %collective-permute-done.4.refs_0_.refs_5_), channel_id=1, source_target_pairs={{0,96},{32,0},{64,32},{96,64},{1,97},{33,1},{65,33},{97,65},{2,98}... | collective-permute-start | bytes 393224 | tf_op jit(solution)/shard_map/ppermute | solution.py:217
  28.2 5.6 %collective-permute-start.16 = (bf16[32,16,128]{2,1,0:T(8,128)(2,1)S(1)}, bf16[32,16,128]{2,1,0:T(8,128)(2,1)S(1)}, u32[]{:S(2)}, u32[]{:S(2)}) collective-permute-start(bf16[32,16,128]{2,1,0:T(8,128)(2,1)S(1)} %get-tuple-element.38), channel_id=1, source_target_pairs={{0,1},{1,2},{2,3},{3,4},{4,5},{5,6},{6,7},{7,0},{8,9},{9,10},{10,1... | collective-permute-start | bytes 393224 | tf_op jit(solution)/shard_map/ppermute | solution.py:217
  30.2 8.0 %collective-permute-start.20 = (bf16[32,16,128]{2,1,0:T(8,128)(2,1)S(1)}, bf16[32,16,128]{2,1,0:T(8,128)(2,1)S(1)}, u32[]{:S(2)}, u32[]{:S(2)}) collective-permute-start(bf16[32,16,128]{2,1,0:T(8,128)(2,1)S(1)} %get-tuple-element.42), channel_id=1, source_target_pairs={{0,7},{1,0},{2,1},{3,2},{4,3},{5,4},{6,5},{7,6},{8,15},{9,8},{10,9... | collective-permute-start | bytes 393224 | tf_op jit(solution)/shard_map/ppermute | solution.py:217
  33.9 7.7 %collective-permute-start.17 = (bf16[32,16,128]{2,1,0:T(8,128)(2,1)S(1)}, bf16[32,16,128]{2,1,0:T(8,128)(2,1)S(1)}, u32[]{:S(2)}, u32[]{:S(2)}) collective-permute-start(bf16[32,16,128]{2,1,0:T(8,128)(2,1)S(1)} %shard_map.86), channel_id=1, source_target_pairs={{0,1},{1,2},{2,3},{3,4},{4,5},{5,6},{6,7},{7,0},{8,9},{9,10},{10,1... | collective-permute-start | bytes 393224 | tf_op jit(solution)/shard_map/ppermute | solution.py:217
  35.9 9.1 %collective-permute-start.12 = (bf16[32,16,128]{2,1,0:T(8,128)(2,1)S(1)}, bf16[32,16,128]{2,1,0:T(8,128)(2,1)S(1)}, u32[]{:S(2)}, u32[]{:S(2)}) collective-permute-start(bf16[32,16,128]{2,1,0:T(8,128)(2,1)S(1)} %get-tuple-element.33), channel_id=1, source_target_pairs={{0,7},{1,0},{2,1},{3,2},{4,3},{5,4},{6,5},{7,6},{8,15},{9,8},{10,9... | collective-permute-start | bytes 393224 | tf_op jit(solution)/shard_map/ppermute | solution.py:217
  38.3 6.8 %collective-permute-start.21 = (bf16[32,16,128]{2,1,0:T(8,128)(2,1)S(1)}, bf16[32,16,128]{2,1,0:T(8,128)(2,1)S(1)}, u32[]{:S(2)}, u32[]{:S(2)}) collective-permute-start(bf16[32,16,128]{2,1,0:T(8,128)(2,1)S(1)} %shard_map.89), channel_id=1, source_target_pairs={{0,7},{1,0},{2,1},{3,2},{4,3},{5,4},{6,5},{7,6},{8,15},{9,8},{10,9... | collective-permute-start | bytes 393224 | tf_op jit(solution)/shard_map/ppermute | solution.py:217
  41.6 7.4 %collective-permute-start.18 = (bf16[32,16,128]{2,1,0:T(8,128)(2,1)S(1)}, bf16[32,16,128]{2,1,0:T(8,128)(2,1)S(1)}, u32[]{:S(2)}, u32[]{:S(2)}) collective-permute-start(bf16[32,16,128]{2,1,0:T(8,128)(2,1)S(1)} %shard_map.87), channel_id=1, source_target_pairs={{0,1},{1,2},{2,3},{3,4},{4,5},{5,6},{6,7},{7,0},{8,9},{9,10},{10,1... | collective-permute-start | bytes 393224 | tf_op jit(solution)/shard_map/ppermute | solution.py:217
  41.8 7.9 %collective-permute-start.9 = (bf16[32,16,128]{2,1,0:T(8,128)(2,1)S(1)}, bf16[32,16,128]{2,1,0:T(8,128)(2,1)S(1)}, u32[]{:S(2)}, u32[]{:S(2)}) collective-permute-start(bf16[32,16,128]{2,1,0:T(8,128)(2,1)S(1)} %get-tuple-element.30), channel_id=1, source_target_pairs={{0,1},{1,2},{2,3},{3,4},{4,5},{5,6},{6,7},{7,0},{8,9},{9,10},{10,1... | collective-permute-start | bytes 393224 | tf_op jit(solution)/shard_map/ppermute | solution.py:217
  45.0 7.0 %collective-permute-start.13 = (bf16[32,16,128]{2,1,0:T(8,128)(2,1)S(1)}, bf16[32,16,128]{2,1,0:T(8,128)(2,1)S(1)}, u32[]{:S(2)}, u32[]{:S(2)}) collective-permute-start(bf16[32,16,128]{2,1,0:T(8,128)(2,1)S(1)} %shard_map.83), channel_id=1, source_target_pairs={{0,7},{1,0},{2,1},{3,2},{4,3},{5,4},{6,5},{7,6},{8,15},{9,8},{10,9... | collective-permute-start | bytes 393224 | tf_op jit(solution)/shard_map/ppermute | solution.py:217
  45.2 8.6 %collective-permute-start.22 = (bf16[32,16,128]{2,1,0:T(8,128)(2,1)S(1)}, bf16[32,16,128]{2,1,0:T(8,128)(2,1)S(1)}, u32[]{:S(2)}, u32[]{:S(2)}) collective-permute-start(bf16[32,16,128]{2,1,0:T(8,128)(2,1)S(1)} %shard_map.90), channel_id=1, source_target_pairs={{0,7},{1,0},{2,1},{3,2},{4,3},{5,4},{6,5},{7,6},{8,15},{9,8},{10,9... | collective-permute-start | bytes 393224 | tf_op jit(solution)/shard_map/ppermute | solution.py:217
  49.7 7.7 %collective-permute-start.10 = (bf16[32,16,128]{2,1,0:T(8,128)(2,1)S(1)}, bf16[32,16,128]{2,1,0:T(8,128)(2,1)S(1)}, u32[]{:S(2)}, u32[]{:S(2)}) collective-permute-start(bf16[32,16,128]{2,1,0:T(8,128)(2,1)S(1)} %shard_map.81), channel_id=1, source_target_pairs={{0,1},{1,2},{2,3},{3,4},{4,5},{5,6},{6,7},{7,0},{8,9},{9,10},{10,1... | collective-permute-start | bytes 393224 | tf_op jit(solution)/shard_map/ppermute | solution.py:217
  52.0 7.5 %collective-permute-start.14 = (bf16[32,16,128]{2,1,0:T(8,128)(2,1)S(1)}, bf16[32,16,128]{2,1,0:T(8,128)(2,1)S(1)}, u32[]{:S(2)}, u32[]{:S(2)}) collective-permute-start(bf16[32,16,128]{2,1,0:T(8,128)(2,1)S(1)} %shard_map.84), channel_id=1, source_target_pairs={{0,7},{1,0},{2,1},{3,2},{4,3},{5,4},{6,5},{7,6},{8,15},{9,8},{10,9... | collective-permute-start | bytes 393224 | tf_op jit(solution)/shard_map/ppermute | solution.py:217
  54.2 10.4 %collective-permute-start.23 = (f32[32,16,128]{2,1,0:T(8,128)S(1)}, f32[32,16,128]{2,1,0:T(8,128)S(1)}, u32[]{:S(2)}, u32[]{:S(2)}) collective-permute-start(f32[32,16,128]{2,1,0:T(8,128)S(1)} %shard_map.91), channel_id=1, source_target_pairs={{0,8},{8,0},{1,9},{9,1},{2,10},{10,2},{3,11},{11,3},{4,12},{12,4},... | collective-permute-start | bytes 786440 | tf_op jit(solution)/shard_map/ppermute | solution.py:217
  57.5 6.3 %collective-permute-start.11 = (bf16[32,16,128]{2,1,0:T(8,128)(2,1)S(1)}, bf16[32,16,128]{2,1,0:T(8,128)(2,1)S(1)}, u32[]{:S(2)}, u32[]{:S(2)}) collective-permute-start(bf16[32,16,128]{2,1,0:T(8,128)(2,1)S(1)} %shard_map.82), channel_id=1, source_target_pairs={{0,1},{1,2},{2,3},{3,4},{4,5},{5,6},{6,7},{7,0},{8,9},{9,10},{10,1... | collective-permute-start | bytes 393224 | tf_op jit(solution)/shard_map/ppermute | solution.py:217
  67.2 6.6 %collective-permute-start.24 = (bf16[32,16,128]{2,1,0:T(8,128)(2,1)S(1)}, bf16[32,16,128]{2,1,0:T(8,128)(2,1)S(1)}, u32[]{:S(2)}, u32[]{:S(2)}) collective-permute-start(bf16[32,16,128]{2,1,0:T(8,128)(2,1)S(1)} %get-tuple-element.47.refs_0_), channel_id=1, source_target_pairs={{0,8},{8,0},{1,9},{9,1},{2,10},{10,2},{3,11},{11,3},{4,12},{12,4},... | collective-permute-start | bytes 393224 | tf_op jit(solution)/shard_map/ppermute | solution.py:217
  73.8 9.5 %collective-permute-start.25 = (bf16[2,32,16,128]{3,2,1,0:T(8,128)(2,1)S(1)}, bf16[2,32,16,128]{3,2,1,0:T(8,128)(2,1)S(1)}, u32[]{:S(2)}, u32[]{:S(2)}) collective-permute-start(bf16[2,32,16,128]{3,2,1,0:T(8,128)(2,1)S(1)} %shard_map.93.refs_0_), channel_id=1, source_target_pairs={{0,1},{1,2},{2,3},{3,4},{4,5},{5,6},{6,7},{7,0},{8,9},{9,10},{10,1... | collective-permute-start | bytes 786440 | tf_op jit(solution)/shard_map/ppermute | solution.py:217
  76.9 8.5 %collective-permute-start.26 = (bf16[2,32,16,128]{3,2,1,0:T(8,128)(2,1)S(1)}, bf16[2,32,16,128]{3,2,1,0:T(8,128)(2,1)S(1)}, u32[]{:S(2)}, u32[]{:S(2)}) collective-permute-start(bf16[2,32,16,128]{3,2,1,0:T(8,128)(2,1)S(1)} %shard_map.93.refs_0_), channel_id=1, source_target_pairs={{0,7},{1,0},{2,1},{3,2},{4,3},{5,4},{6,5},{7,6},{8,15},{9,8},{10,9... | collective-permute-start | bytes 786440 | tf_op jit(solution)/shard_map/ppermute | solution.py:217
  83.3 9.0 %collective-permute-start.27 = (bf16[2,32,16,128]{3,2,1,0:T(8,128)(2,1)S(1)}, bf16[2,32,16,128]{3,2,1,0:T(8,128)(2,1)S(1)}, u32[]{:S(2)}, u32[]{:S(2)}) collective-permute-start(bf16[2,32,16,128]{3,2,1,0:T(8,128)(2,1)S(1)} %collective-permute-done.25.refs_1_), channel_id=1, source_target_pairs={{0,1},{1,2},{2,3},{3,4},{4,5},{5,6},{6,7},{7,0},{8,9},{9,10},{10,1... | collective-permute-start | bytes 786440 | tf_op jit(solution)/shard_map/ppermute | solution.py:217
  85.4 6.8 %collective-permute-start.28 = (bf16[2,32,16,128]{3,2,1,0:T(8,128)(2,1)S(1)}, bf16[2,32,16,128]{3,2,1,0:T(8,128)(2,1)S(1)}, u32[]{:S(2)}, u32[]{:S(2)}) collective-permute-start(bf16[2,32,16,128]{3,2,1,0:T(8,128)(2,1)S(1)} %collective-permute-done.26.refs_2_), channel_id=1, source_target_pairs={{0,7},{1,0},{2,1},{3,2},{4,3},{5,4},{6,5},{7,6},{8,15},{9,8},{10,9... | collective-permute-start | bytes 786440 | tf_op jit(solution)/shard_map/ppermute | solution.py:217
  92.3 7.3 %collective-permute-start.29 = (bf16[2,32,16,128]{3,2,1,0:T(8,128)(2,1)S(1)}, bf16[2,32,16,128]{3,2,1,0:T(8,128)(2,1)S(1)}, u32[]{:S(2)}, u32[]{:S(2)}) collective-permute-start(bf16[2,32,16,128]{3,2,1,0:T(8,128)(2,1)S(1)} %collective-permute-done.27.refs_3_), channel_id=1, source_target_pairs={{0,1},{1,2},{2,3},{3,4},{4,5},{5,6},{6,7},{7,0},{8,9},{9,10},{10,1... | collective-permute-start | bytes 786440 | tf_op jit(solution)/shard_map/ppermute | solution.py:217
  92.3 9.0 %collective-permute-start.30 = (bf16[2,32,16,128]{3,2,1,0:T(8,128)(2,1)S(1)}, bf16[2,32,16,128]{3,2,1,0:T(8,128)(2,1)S(1)}, u32[]{:S(2)}, u32[]{:S(2)}) collective-permute-start(bf16[2,32,16,128]{3,2,1,0:T(8,128)(2,1)S(1)} %collective-permute-done.28.refs_4_), channel_id=1, source_target_pairs={{0,7},{1,0},{2,1},{3,2},{4,3},{5,4},{6,5},{7,6},{8,15},{9,8},{10,9... | collective-permute-start | bytes 786440 | tf_op jit(solution)/shard_map/ppermute | solution.py:217
  103.5 5.9 %collective-permute-start.32 = (bf16[32,16,128]{2,1,0:T(8,128)(2,1)S(1)}, bf16[32,16,128]{2,1,0:T(8,128)(2,1)S(1)}, u32[]{:S(2)}, u32[]{:S(2)}) collective-permute-start(bf16[32,16,128]{2,1,0:T(8,128)(2,1)S(1)} %get-tuple-element.49), channel_id=1, source_target_pairs={{0,7},{1,0},{2,1},{3,2},{4,3},{5,4},{6,5},{7,6},{8,15},{9,8},{10,9... | collective-permute-start | bytes 393224 | tf_op jit(solution)/shard_map/ppermute | solution.py:217
  116.6 7.5 %collective-permute-start.34 = (bf16[32,16,128]{2,1,0:T(8,128)(2,1)S(1)}, bf16[32,16,128]{2,1,0:T(8,128)(2,1)S(1)}, u32[]{:S(2)}, u32[]{:S(2)}) collective-permute-start(bf16[32,16,128]{2,1,0:T(8,128)(2,1)S(1)} %get-tuple-element.52), channel_id=1, source_target_pairs={{0,32},{32,64},{64,96},{96,0},{1,33},{33,65},{65,97},{97,1},{2,34}... | collective-permute-start | bytes 393224 | tf_op jit(solution)/shard_map/ppermute | solution.py:217
  117.0 7.2 %collective-permute-start.35 = (bf16[32,16,128]{2,1,0:T(8,128)(2,1)S(1)}, bf16[32,16,128]{2,1,0:T(8,128)(2,1)S(1)}, u32[]{:S(2)}, u32[]{:S(2)}) collective-permute-start(bf16[32,16,128]{2,1,0:T(8,128)(2,1)S(1)} %get-tuple-element.53), channel_id=1, source_target_pairs={{0,96},{32,0},{64,32},{96,64},{1,97},{33,1},{65,33},{97,65},{2,98}... | collective-permute-start | bytes 393224 | tf_op jit(solution)/shard_map/ppermute | solution.py:217
  124.3 9.1 %collective-permute-start.36 = (bf16[2,32,16,128]{3,2,1,0:T(8,128)(2,1)S(1)}, bf16[2,32,16,128]{3,2,1,0:T(8,128)(2,1)S(1)}, u32[]{:S(2)}, u32[]{:S(2)}) collective-permute-start(bf16[2,32,16,128]{3,2,1,0:T(8,128)(2,1)S(1)} %get-tuple-element.54), channel_id=1, source_target_pairs={{0,32},{32,64},{64,96},{96,0},{1,33},{33,65},{65,97},{97,1},{2,34}... | collective-permute-start | bytes 786440 | tf_op jit(solution)/shard_map/ppermute | solution.py:217
  125.5 7.9 %collective-permute-start.37 = (bf16[2,32,16,128]{3,2,1,0:T(8,128)(2,1)S(1)}, bf16[2,32,16,128]{3,2,1,0:T(8,128)(2,1)S(1)}, u32[]{:S(2)}, u32[]{:S(2)}) collective-permute-start(bf16[2,32,16,128]{3,2,1,0:T(8,128)(2,1)S(1)} %get-tuple-element.55), channel_id=1, source_target_pairs={{0,96},{32,0},{64,32},{96,64},{1,97},{33,1},{65,33},{97,65},{2,98}... | collective-permute-start | bytes 786440 | tf_op jit(solution)/shard_map/ppermute | solution.py:217
  (13 other events, 186.3 us)
where the time goes:
time: 141 us
  waiting for transfers between devices  60.4 us (43%)
  starting transfers between devices  59.9 us (42%)
  Pallas kernels  15.2 us (11%)
  local copies, waits for them, and re-layouts  4.25 us (3%)
    ppermute x39, waiting for transfers between devices, move(): lax.ppermute(value, axis, [(i, (i + step) % size) for i in range(size)])  60.4 us
    ppermute x39, starting transfers between devices, move(): lax.ppermute(value, axis, [(i, (i + step) % size) for i in range(size)])  59.9 us
    pallas_call x23, Pallas kernels, local(): pl.pallas_call(body, in_specs=[pl.BlockSpec(memory_space=pltpu.HBM)] * le...  15.2 us
    unnamed x14, local copies, waits for them, and re-layouts  3.4 us
  transfers between devices with their start and end apart: 39, of which 24 were waited for; matrix products, arithmetic and copies ran while one was open for 1% of the time, Pallas kernels for 0%

commit v1 on v0

--- a/solution.py
+++ b/solution.py
@@ -70,8 +70,9 @@
     out[...] = buf[...].astype(BF16)
 
 
-def middle_body(forward, inverse, onset, plus, minus, share, taken, upgoing, out, total, buf):
-    total[...] = plus[...].astype(F32) + minus[...].astype(F32) + share[...] + taken[...]
+def middle_body(forward, inverse, onset, plus, minus, share, far, upgoing, out, total, buf):
+    ring = plus[...].astype(F32) + minus[...].astype(F32)
+    total[...] = ring + (share[...] + far[0].astype(F32))
     points, width, samples = upgoing.shape
     time = lax.broadcasted_iota(jnp.int32, (points, samples), 1)
     for n in range(width):
@@ -99,12 +100,15 @@
     return direct + jnp.where(lane < half, -sign * swapped, sign * swapped)
 
 
-def stream(kernel, held_kernel, arrived, prepare, one):
+def stream(kernel, held_kernel, arrived, row, prepare, one):
     groups = kernel.shape[1] // UNROLL
+    rows = pl.ds(row, held_kernel.shape[2])
 
     def fetch(i):
         part = pl.ds(i * UNROLL, UNROLL)
-        return pltpu.make_async_copy(kernel.at[:, part], held_kernel.at[:, part], arrived.at[i])
+        return pltpu.make_async_copy(
+            kernel.at[:, part, rows], held_kernel.at[:, part], arrived.at[i]
+        )
 
     for i in range(groups):
         fetch(i).start()
@@ -122,11 +126,6 @@
 def pack_body(*refs):
     for i, ref in enumerate(refs[:-1]):
         refs[-1][i] = ref[...]
-
-
-def pick_body(plus, minus, out_p, out_m):
-    out_p[...] = plus[0]
-    out_m[...] = minus[1]
 
 
 def unpack(refs, spec, places):
@@ -139,12 +138,13 @@
                 spec[:, places.pop(0)] = ref[i]
 
 
-def conv_body(source, *refs, spots, pieces):
+def conv_body(source, *refs, spots, pieces, dyh, slots):
     ins, outs, (spec, kernel, arrived) = refs[:pieces], refs[pieces:-3], refs[-3:]
     width, lanes = ins[0].shape[-2:]
-    order = [(s, dz) for s in range(2) for dz in range(NZ)]
-    firsts = [pl.multiple_of(rec_at(1 - s, dz) * width, width) for s, dz in order]
-    size = len(order) * width
+    size = NZ * width
+    z = lax.axis_index("z")
+    firsts = [pl.multiple_of(((z + dz) & (NZ - 1)) * width, width) for dz in range(NZ)]
+    row = pl.multiple_of(((lax.axis_index("yh") + dyh) & 1) * size, size)
 
     def prepare():
         unpack(ins, spec, [src_at(*spot) for spot in spots])
@@ -154,10 +154,15 @@
         rows = [kernel[c, kk, pl.ds(first, width), :] for c in range(2) for first in firsts]
         both = jnp.dot(jnp.concatenate(rows, axis=0), rhs, preferred_element_type=F32)
         out = cross(both[:size], both[size:], 1.0)
-        for j in range(len(order)):
-            outs[j][kk] = out[j * width : (j + 1) * width].astype(outs[j].dtype)
-
-    stream(source, kernel, arrived, prepare, one)
+        for ref, slot in zip(outs, slots):
+            for i, dz in enumerate(slot):
+                part = out[dz * width : (dz + 1) * width].astype(ref.dtype)
+                if len(slot) > 1:
+                    ref[i, kk] = part
+                else:
+                    ref[kk] = part
+
+    stream(source, kernel, arrived, row, prepare, one)
 
 
 def corr_body(source, *refs, spots, pieces):
@@ -179,15 +184,19 @@
             stay[j, kk] = total[u, near[j]]
             away[j, kk] = total[u, far[j]].astype(BF16)
 
-    stream(source, kernel, arrived, prepare, one)
-
-
-def hop_body(taken, share, out):
-    out[...] = (taken[...].astype(F32) + share[...]).astype(BF16)
-
-
-def meet_body(one_way, other_way, share, out):
-    out[...] = one_way[...].astype(F32) + other_way[...].astype(F32) + share[...]
+    stream(source, kernel, arrived, 0, prepare, one)
+
+
+def join_body(share, far, out):
+    out[...] = (share[...] + far[...].astype(F32)).astype(BF16)
+
+
+def hop_body(taken, share, far, out, *, at):
+    out[...] = (taken[...].astype(F32) + share[...] + far[at].astype(F32)).astype(BF16)
+
+
+def first_body(share, far, out, *, at):
+    out[...] = (share[...] + far[at].astype(F32)).astype(BF16)
 
 
 def held(stay, taken, s, b):
@@ -229,10 +238,8 @@
     limits_up = lax.dynamic_slice_in_dim(onset, (src * 2 * NZ + rec) * width, width, 1)
     limits_down = lax.dynamic_slice_in_dim(onset, (rec * 4 * NX + src) * width, width, 1)
     buf = pltpu.VMEM(one, F32)
-    bulk = [
-        pltpu.VMEM(kernel.shape, BF16),
-        pltpu.SemaphoreType.DMA((count // UNROLL,)),
-    ]
+    arrived = pltpu.SemaphoreType.DMA((count // UNROLL,))
+    half_kernel = (2, count, kernel.shape[2] // 2, kernel.shape[3])
 
     (own,) = local(spectra_body, [(one, BF16)], [forward, focusing], [buf])
     near = {(0, 0): own}
@@ -251,52 +258,57 @@
         pieces.append(move(packed, "c", 1))
     full = (len(spots), width, lanes)
 
-    leads = [(0, 4), (0, 5), (1, 3), (1, 4)]
-    order = [(s, dz) for s in range(2) for dz in range(NZ)]
-    outs = local(
-        functools.partial(conv_body, spots=spots, pieces=len(pieces)),
-        [(one, BF16 if key in leads else F32) for key in order],
-        pieces,
-        [pltpu.VMEM((count,) + full, BF16)] + bulk,
-        14,
-        kernel,
-    )
-    share = dict(zip(order, outs))
-    sums = {}
-    for s in range(2):
-        for sign, tag in ((1, "p"), (-1, "m")):
-            hops = NZ // 2 - (tag == "mp"[s])
-            value = share[s, sign * hops % NZ]
-            for i in range(1, hops + 1):
-                value = move(value, "z", sign)
-                if i < hops:
-                    left = share[s, sign * (hops - i) % NZ]
-                    (value,) = local(hop_body, [(one, BF16)], [value, left])
-            sums[s, tag] = value
-    (send,) = local(meet_body, [(one, F32)], [sums[0, "p"], sums[0, "m"], share[0, 0]])
-    taken = move(send, "yh", 1)
+    def conv(dyh, slots, dtype):
+        return local(
+            functools.partial(
+                conv_body, spots=spots, pieces=len(pieces), dyh=dyh, slots=slots
+            ),
+            [(((len(slot),) if len(slot) > 1 else ()) + one, dtype) for slot in slots],
+            pieces,
+            [pltpu.VMEM((count,) + full, BF16), pltpu.VMEM(half_kernel, BF16), arrived],
+            9,
+            kernel,
+        )
+
+    slots = [(4,), (3, 5), (2, 6), (0, 1, 7)]
+    far = [move(value, "yh", 1) for value in conv(1, slots, BF16)]
+    share = conv(0, [(dz,) for dz in range(NZ)], F32)
+    (plus,) = local(join_body, [(one, BF16)], [share[4], far[0]])
+    plus = move(plus, "z", 1)
+    first = functools.partial(first_body, at=1)
+    (minus,) = local(first, [(one, BF16)], [share[5], far[1]])
+    minus = move(minus, "z", -1)
+    for dz, group, at in ((3, 1, 0), (2, 2, 0), (1, 3, 1)):
+        body = functools.partial(hop_body, at=at)
+        (plus,) = local(body, [(one, BF16)], [plus, share[dz], far[group]])
+        plus = move(plus, "z", 1)
+    for dz, group, at in ((6, 2, 1), (7, 3, 2)):
+        body = functools.partial(hop_body, at=at)
+        (minus,) = local(body, [(one, BF16)], [minus, share[dz], far[group]])
+        minus = move(minus, "z", -1)
     upgoing, mine = local(
         middle_body,
         [(focusing.shape, F32), (one, BF16)],
-        [forward, inverse, limits_up, sums[1, "p"], sums[1, "m"], share[1, 0], taken],
+        [forward, inverse, limits_up, plus, minus, share[0], far[3]],
         [buf, buf],
     )
 
-    (pair,) = local(pack_body, [(two, BF16)], [mine, move(mine, "yh", 1)])
-    plus = minus = pair
-    pieces, spots = [pair], [(0, 0), (1, 0)]
+    pieces, spots = [mine, move(mine, "yh", 1)], [(0, 0), (1, 0)]
+    plus = minus = mine
     for i in range(1, NZ // 2):
         plus, minus = move(plus, "z", 1), move(minus, "z", -1)
-        pieces += [plus, minus]
-        spots += [(s, dz) for dz in (-i, i) for s in range(2)]
-    plus, minus = local(pick_body, [(one, BF16)] * 2, [plus, minus])
-    pieces += [move(plus, "z", 1), move(minus, "z", -1)]
+        (pair,) = local(pack_body, [(two, BF16)], [plus, minus])
+        pieces += [plus, minus, move(pair, "yh", 1)]
+        spots += [(s, dz) for s in range(2) for dz in (-i, i)]
+    plus = move(plus, "z", 1)
+    pieces += [plus, move(plus, "yh", 1)]
     spots += [(s, NZ // 2) for s in range(2)]
     away, stay = local(
         functools.partial(corr_body, spots=spots, pieces=len(pieces)),
         [((len(PAIRS),) + one, BF16), ((len(PAIRS),) + one, F32)],
         pieces,
-        [pltpu.VMEM((count,) + full, BF16), pltpu.VMEM((UNROLL,) + full, F32)] + bulk,
+        [pltpu.VMEM((count,) + full, BF16), pltpu.VMEM((UNROLL,) + full, F32)]
+        + [pltpu.VMEM(kernel.shape, BF16), arrived],
         18,
         kernel,
     )

time: 141 us -> 135 us (0.957); the launches traced: 141 us -> 132 us
  waiting for transfers between devices: 60.4 us -> 49.4 us
    ppermute x39 -> x38, waiting for transfers between devices: 60.4 us -> 49.4 us  [move(): lax.ppermute(value, axis, [(i, (i + step) % size) for i in range(size)])]
    pallas_call x23 -> x21, Pallas kernels: 15.2 us -> 16.6 us  [local(): pl.pallas_call(body, in_specs=[pl.BlockSpec(memory_space=pltpu.HBM)] * le...]
    ppermute x39 -> x38, starting transfers between devices: 59.9 us -> 61.1 us  [move(): lax.ppermute(value, axis, [(i, (i + step) % size) for i in range(size)])]
  transfers between devices with their start and end apart: 39 -> 38, of which waited for: 24 -> 22; matrix products, arithmetic and copies ran while one was open for 1% -> 1% of each run, Pallas kernels for 0% -> 3%
where the time goes in v1:
time: 135 us; the launch traced here: 132 us
  starting transfers between devices  61.1 us (45%)
  waiting for transfers between devices  49.4 us (37%)
  Pallas kernels  16.6 us (12%)
  local copies, waits for them, and re-layouts  4.26 us (3%)
    ppermute x38, starting transfers between devices, move(): lax.ppermute(value, axis, [(i, (i + step) % size) for i in range(size)])  61.1 us
    ppermute x38, waiting for transfers between devices, move(): lax.ppermute(value, axis, [(i, (i + step) % size) for i in range(size)])  49.4 us
    pallas_call x21, Pallas kernels, local(): pl.pallas_call(body, in_specs=[pl.BlockSpec(memory_space=pltpu.HBM)] * le...  16.6 us
    unnamed x14, local copies, waits for them, and re-layouts  3.41 us
  transfers between devices with their start and end apart: 38, of which 22 were waited for; matrix products, arithmetic and copies ran while one was open for 1% of the time, Pallas kernels for 3%

profile of v1, /device:TPU:32, one launch (start us, length us, event | category | flops | bytes accessed | tf_op | source)
XLA Modules:
  0.0 132.2 jit_solution(9449595279543155899)
XLA Ops:
  6.7 2.2 %collective-permute-done.2.refs_1_.refs_3_ = bf16[32,16,128]{2,1,0:T(8,128)(2,1)S(1)} collective-permute-done((bf16[32,16,128]{2,1,0:T(8,128)(2,1)S(1)}, bf16[32,16,128]{2,1,0:T(8,128)(2,1)S(1)}, u32[]{:S(2)}, u32[]{:S(2)}) %collective-permute-start.2) | collective-permute-done | bytes 131104 | tf_op jit(solution)/shard_map/ppermute | solution.py:226
  8.8 2.8 %collective-permute-start.4 = (bf16[32,16,128]{2,1,0:T(8,128)(2,1)S(1)}, bf16[32,16,128]{2,1,0:T(8,128)(2,1)S(1)}, u32[]{:S(2)}, u32[]{:S(2)}) collective-permute-start(bf16[32,16,128]{2,1,0:T(8,128)(2,1)S(1)} %collective-permute-done.2.refs_1_.refs_3_), channel_id=1, source_target_pairs={{0,96},{32,0},{64,32},{96,64},{1,97},{33,1},{65,33},{97,65},{2,98}... | collective-permute-start | bytes 393224 | tf_op jit(solution)/shard_map/ppermute | solution.py:226
  14.9 3.7 %collective-permute-start.6 = (bf16[32,16,128]{2,1,0:T(8,128)(2,1)S(1)}, bf16[32,16,128]{2,1,0:T(8,128)(2,1)S(1)}, u32[]{:S(2)}, u32[]{:S(2)}) collective-permute-start(bf16[32,16,128]{2,1,0:T(8,128)(2,1)S(1)} %collective-permute-done.4.refs_0_.refs_5_), channel_id=1, source_target_pairs={{0,96},{32,0},{64,32},{96,64},{1,97},{33,1},{65,33},{97,65},{2,98}... | collective-permute-start | bytes 393224 | tf_op jit(solution)/shard_map/ppermute | solution.py:226
  23.2 3.3 %shard_map.81 = (bf16[32,16,128]{2,1,0:T(8,128)(2,1)S(1)}, bf16[2,32,16,128]{3,2,1,0:T(8,128)(2,1)S(1)}, bf16[2,32,16,128]{3,2,1,0:T(8,128)(2,1)S(1)}, bf16[3,32,16,128]{3,2,1,0:T(8,128)(2,1)S(1)}) custom-call(bf16[2,32,256,256]{3,2,1,0:T(8,128)(2,1)} %source.5, bf16[32,16,128]{2,1,0:T(8,128)(2,1)S(1)} %shard_map.77.refs_0_, ...), custom_call_target="tpu_custom_call" | custom-call | tf_op jit(solution)/shard_map/pallas_call | solution.py:33
  26.4 3.3 %collective-permute-start.9 = (bf16[32,16,128]{2,1,0:T(8,128)(2,1)S(1)}, bf16[32,16,128]{2,1,0:T(8,128)(2,1)S(1)}, u32[]{:S(2)}, u32[]{:S(2)}) collective-permute-start(bf16[32,16,128]{2,1,0:T(8,128)(2,1)S(1)} %get-tuple-element.25), channel_id=1, source_target_pairs={{0,8},{8,0},{1,9},{9,1},{2,10},{10,2},{3,11},{11,3},{4,12},{12,4},... | collective-permute-start | bytes 393224 | tf_op jit(solution)/shard_map/ppermute | solution.py:226
  30.1 3.3 %shard_map.80 = (f32[32,16,128]{2,1,0:T(8,128)S(1)}, f32[32,16,128]{2,1,0:T(8,128)S(1)}, f32[32,16,128]{2,1,0:T(8,128)S(1)}, f32[32,16,128]{2,1,0:T(8,128)S(1)},...) custom-call(bf16[2,32,256,256]{3,2,1,0:T(8,128)(2,1)} %source.5, ...), custom_call_target="tpu_custom_call" | custom-call | tf_op jit(solution)/shard_map/pallas_call | solution.py:33
  33.6 2.0 %collective-permute-start.10 = (bf16[32,16,128]{2,1,0:T(8,128)(2,1)S(1)}, bf16[32,16,128]{2,1,0:T(8,128)(2,1)S(1)}, u32[]{:S(2)}, u32[]{:S(2)}) collective-permute-start(bf16[32,16,128]{2,1,0:T(8,128)(2,1)S(1)} %shard_map.82), channel_id=1, source_target_pairs={{0,1},{1,2},{2,3},{3,4},{4,5},{5,6},{6,7},{7,0},{8,9},{9,10},{10,1... | collective-permute-start | bytes 393224 | tf_op jit(solution)/shard_map/ppermute | solution.py:226
  35.6 4.0 %collective-permute-start.13 = (bf16[2,32,16,128]{3,2,1,0:T(8,128)(2,1)S(1)}, bf16[2,32,16,128]{3,2,1,0:T(8,128)(2,1)S(1)}, u32[]{:S(2)}, u32[]{:S(2)}) collective-permute-start(bf16[2,32,16,128]{3,2,1,0:T(8,128)(2,1)S(1)} %get-tuple-element.29), channel_id=1, source_target_pairs={{0,8},{8,0},{1,9},{9,1},{2,10},{10,2},{3,11},{11,3},{4,12},{12,4},... | collective-permute-start | bytes 786440 | tf_op jit(solution)/shard_map/ppermute | solution.py:226
  39.8 2.2 %collective-permute-start.12 = (bf16[32,16,128]{2,1,0:T(8,128)(2,1)S(1)}, bf16[32,16,128]{2,1,0:T(8,128)(2,1)S(1)}, u32[]{:S(2)}, u32[]{:S(2)}) collective-permute-start(bf16[32,16,128]{2,1,0:T(8,128)(2,1)S(1)} %shard_map.83), channel_id=1, source_target_pairs={{0,1},{1,2},{2,3},{3,4},{4,5},{5,6},{6,7},{7,0},{8,9},{9,10},{10,1... | collective-permute-start | bytes 393224 | tf_op jit(solution)/shard_map/ppermute | solution.py:226
  43.1 3.6 %collective-permute-done.13.far = bf16[2,32,16,128]{3,2,1,0:T(8,128)(2,1)S(1)} collective-permute-done((bf16[2,32,16,128]{3,2,1,0:T(8,128)(2,1)S(1)}, bf16[2,32,16,128]{3,2,1,0:T(8,128)(2,1)S(1)}, u32[]{:S(2)}, u32[]{:S(2)}) %collective-permute-start.13) | collective-permute-done | bytes 262176 | tf_op jit(solution)/shard_map/ppermute | solution.py:226
  46.8 2.0 %collective-permute-start.14 = (bf16[32,16,128]{2,1,0:T(8,128)(2,1)S(1)}, bf16[32,16,128]{2,1,0:T(8,128)(2,1)S(1)}, u32[]{:S(2)}, u32[]{:S(2)}) collective-permute-start(bf16[32,16,128]{2,1,0:T(8,128)(2,1)S(1)} %shard_map.84), channel_id=1, source_target_pairs={{0,1},{1,2},{2,3},{3,4},{4,5},{5,6},{6,7},{7,0},{8,9},{9,10},{10,1... | collective-permute-start | bytes 393224 | tf_op jit(solution)/shard_map/ppermute | solution.py:226
  49.9 3.4 %collective-permute-done.15.far = bf16[3,32,16,128]{3,2,1,0:T(8,128)(2,1)S(1)} collective-permute-done((bf16[3,32,16,128]{3,2,1,0:T(8,128)(2,1)S(1)}, bf16[3,32,16,128]{3,2,1,0:T(8,128)(2,1)S(1)}, u32[]{:S(2)}, u32[]{:S(2)}) %collective-permute-start.15) | collective-permute-done | bytes 393248 | tf_op jit(solution)/shard_map/ppermute | solution.py:226
  53.4 2.0 %collective-permute-start.16 = (bf16[32,16,128]{2,1,0:T(8,128)(2,1)S(1)}, bf16[32,16,128]{2,1,0:T(8,128)(2,1)S(1)}, u32[]{:S(2)}, u32[]{:S(2)}) collective-permute-start(bf16[32,16,128]{2,1,0:T(8,128)(2,1)S(1)} %shard_map.85), channel_id=1, source_target_pairs={{0,1},{1,2},{2,3},{3,4},{4,5},{5,6},{6,7},{7,0},{8,9},{9,10},{10,1... | collective-permute-start | bytes 393224 | tf_op jit(solution)/shard_map/ppermute | solution.py:226
  59.0 2.1 %collective-permute-done.19.minus = bf16[32,16,128]{2,1,0:T(8,128)(2,1)S(1)} collective-permute-done((bf16[32,16,128]{2,1,0:T(8,128)(2,1)S(1)}, bf16[32,16,128]{2,1,0:T(8,128)(2,1)S(1)}, u32[]{:S(2)}, u32[]{:S(2)}) %collective-permute-start.19) | collective-permute-done | bytes 131104 | tf_op jit(solution)/shard_map/ppermute | solution.py:226
  61.1 2.7 %shard_map.89 = (f32[64,16,128]{2,1,0:T(8,128)S(1)}, bf16[32,16,128]{2,1,0:T(8,128)(2,1)S(1)}) custom-call(f32[64,128]{1,0:T(8,128)S(1)} %copy-done.3, f32[64,128]{1,0:T(8,128)S(1)} %copy-done.5, s32[64,16]{1,0:T(8,128)S(1)} %get-tuple-element.47.onset, bf16[32,16,128]{2,1,0:T(8,128)(2,1)S(1)} %collective-permute-done.16.plus, ...), custom_call_target="tpu_custom_call" | custom-call | tf_op jit(solution)/shard_map/pallas_call | solution.py:33
  63.8 2.5 %collective-permute-start.21 = (bf16[32,16,128]{2,1,0:T(8,128)(2,1)S(1)}, bf16[32,16,128]{2,1,0:T(8,128)(2,1)S(1)}, u32[]{:S(2)}, u32[]{:S(2)}) collective-permute-start(bf16[32,16,128]{2,1,0:T(8,128)(2,1)S(1)} %get-tuple-element.37.refs_0_), channel_id=1, source_target_pairs={{0,1},{1,2},{2,3},{3,4},{4,5},{5,6},{6,7},{7,0},{8,9},{9,10},{10,1... | collective-permute-start | bytes 393224 | tf_op jit(solution)/shard_map/ppermute | solution.py:226
  66.3 2.6 %collective-permute-done.21.refs_0_.refs_2_ = bf16[32,16,128]{2,1,0:T(8,128)(2,1)S(1)} collective-permute-done((bf16[32,16,128]{2,1,0:T(8,128)(2,1)S(1)}, bf16[32,16,128]{2,1,0:T(8,128)(2,1)S(1)}, u32[]{:S(2)}, u32[]{:S(2)}) %collective-permute-start.21) | collective-permute-done | bytes 131104 | tf_op jit(solution)/shard_map/ppermute | solution.py:226
  68.8 4.1 %collective-permute-start.24 = (bf16[32,16,128]{2,1,0:T(8,128)(2,1)S(1)}, bf16[32,16,128]{2,1,0:T(8,128)(2,1)S(1)}, u32[]{:S(2)}, u32[]{:S(2)}) collective-permute-start(bf16[32,16,128]{2,1,0:T(8,128)(2,1)S(1)} %collective-permute-done.21.refs_0_.refs_2_), channel_id=1, source_target_pairs={{0,1},{1,2},{2,3},{3,4},{4,5},{5,6},{6,7},{7,0},{8,9},{9,10},{10,1... | collective-permute-start | bytes 393224 | tf_op jit(solution)/shard_map/ppermute | solution.py:226
  73.1 3.3 %collective-permute-done.24.refs_0_.refs_5_ = bf16[32,16,128]{2,1,0:T(8,128)(2,1)S(1)} collective-permute-done((bf16[32,16,128]{2,1,0:T(8,128)(2,1)S(1)}, bf16[32,16,128]{2,1,0:T(8,128)(2,1)S(1)}, u32[]{:S(2)}, u32[]{:S(2)}) %collective-permute-start.24) | collective-permute-done | bytes 131104 | tf_op jit(solution)/shard_map/ppermute | solution.py:226
  76.4 2.5 %collective-permute-start.27 = (bf16[32,16,128]{2,1,0:T(8,128)(2,1)S(1)}, bf16[32,16,128]{2,1,0:T(8,128)(2,1)S(1)}, u32[]{:S(2)}, u32[]{:S(2)}) collective-permute-start(bf16[32,16,128]{2,1,0:T(8,128)(2,1)S(1)} %collective-permute-done.24.refs_0_.refs_5_), channel_id=1, source_target_pairs={{0,1},{1,2},{2,3},{3,4},{4,5},{5,6},{6,7},{7,0},{8,9},{9,10},{10,1... | collective-permute-start | bytes 393224 | tf_op jit(solution)/shard_map/ppermute | solution.py:226
  79.4 3.7 %collective-permute-start.23 = (bf16[2,32,16,128]{3,2,1,0:T(8,128)(2,1)S(1)}, bf16[2,32,16,128]{3,2,1,0:T(8,128)(2,1)S(1)}, u32[]{:S(2)}, u32[]{:S(2)}) collective-permute-start(bf16[2,32,16,128]{3,2,1,0:T(8,128)(2,1)S(1)} %shard_map.90), channel_id=1, source_target_pairs={{0,8},{8,0},{1,9},{9,1},{2,10},{10,2},{3,11},{11,3},{4,12},{12,4},... | collective-permute-start | bytes 786440 | tf_op jit(solution)/shard_map/ppermute | solution.py:226
  83.2 2.1 %collective-permute-start.30 = (bf16[32,16,128]{2,1,0:T(8,128)(2,1)S(1)}, bf16[32,16,128]{2,1,0:T(8,128)(2,1)S(1)}, u32[]{:S(2)}, u32[]{:S(2)}) collective-permute-start(bf16[32,16,128]{2,1,0:T(8,128)(2,1)S(1)} %collective-permute-done.27.refs_0_.refs_8_), channel_id=1, source_target_pairs={{0,1},{1,2},{2,3},{3,4},{4,5},{5,6},{6,7},{7,0},{8,9},{9,10},{10,1... | collective-permute-start | bytes 393224 | tf_op jit(solution)/shard_map/ppermute | solution.py:226
  85.4 3.3 %collective-permute-start.29 = (bf16[2,32,16,128]{3,2,1,0:T(8,128)(2,1)S(1)}, bf16[2,32,16,128]{3,2,1,0:T(8,128)(2,1)S(1)}, u32[]{:S(2)}, u32[]{:S(2)}) collective-permute-start(bf16[2,32,16,128]{3,2,1,0:T(8,128)(2,1)S(1)} %shard_map.92), channel_id=1, source_target_pairs={{0,8},{8,0},{1,9},{9,1},{2,10},{10,2},{3,11},{11,3},{4,12},{12,4},... | collective-permute-start | bytes 786440 | tf_op jit(solution)/shard_map/ppermute | solution.py:226
  89.0 3.2 %collective-permute-start.31 = (bf16[32,16,128]{2,1,0:T(8,128)(2,1)S(1)}, bf16[32,16,128]{2,1,0:T(8,128)(2,1)S(1)}, u32[]{:S(2)}, u32[]{:S(2)}) collective-permute-start(bf16[32,16,128]{2,1,0:T(8,128)(2,1)S(1)} %collective-permute-done.30.refs_11_), channel_id=1, source_target_pairs={{0,8},{8,0},{1,9},{9,1},{2,10},{10,2},{3,11},{11,3},{4,12},{12,4},... | collective-permute-start | bytes 393224 | tf_op jit(solution)/shard_map/ppermute | solution.py:226
  92.2 7.4 %collective-permute-done.20.refs_1_ = bf16[32,16,128]{2,1,0:T(8,128)(2,1)S(1)} collective-permute-done((bf16[32,16,128]{2,1,0:T(8,128)(2,1)S(1)}, bf16[32,16,128]{2,1,0:T(8,128)(2,1)S(1)}, u32[]{:S(2)}, u32[]{:S(2)}) %collective-permute-start.20) | collective-permute-done | bytes 131104 | tf_op jit(solution)/shard_map/ppermute | solution.py:226
  101.0 4.4 %shard_map.93 = (bf16[8,32,16,128]{3,2,1,0:T(8,128)(2,1)S(1)}, f32[8,32,16,128]{3,2,1,0:T(8,128)S(1)}) custom-call(bf16[2,32,256,256]{3,2,1,0:T(8,128)(2,1)} %source.5, bf16[32,16,128]{2,1,0:T(8,128)(2,1)S(1)} %get-tuple-element.37.refs_0_, bf16[32,16,128]{2,1,0:T(8,128)(2,1)S(1)} %collective-permute-done.20.refs_1_, ...), custom_call_target="tpu_custom_call" | custom-call | tf_op jit(solution)/shard_map/pallas_call | solution.py:33
  105.5 2.6 %collective-permute-done.32.taken = bf16[8,32,16,128]{3,2,1,0:T(8,128)(2,1)S(1)} collective-permute-done((bf16[8,32,16,128]{3,2,1,0:T(8,128)(2,1)S(1)}, bf16[8,32,16,128]{3,2,1,0:T(8,128)(2,1)S(1)}, u32[]{:S(2)}, u32[]{:S(2)}) %collective-permute-start.32) | collective-permute-done | bytes 1048608 | tf_op jit(solution)/shard_map/ppermute | solution.py:226
  108.6 3.5 %collective-permute-start.34 = (bf16[32,16,128]{2,1,0:T(8,128)(2,1)S(1)}, bf16[32,16,128]{2,1,0:T(8,128)(2,1)S(1)}, u32[]{:S(2)}, u32[]{:S(2)}) collective-permute-start(bf16[32,16,128]{2,1,0:T(8,128)(2,1)S(1)} %get-tuple-element.41), channel_id=1, source_target_pairs={{0,96},{32,0},{64,32},{96,64},{1,97},{33,1},{65,33},{97,65},{2,98}... | collective-permute-start | bytes 393224 | tf_op jit(solution)/shard_map/ppermute | solution.py:226
  112.1 3.7 %collective-permute-done.33.plus = bf16[32,16,128]{2,1,0:T(8,128)(2,1)S(1)} collective-permute-done((bf16[32,16,128]{2,1,0:T(8,128)(2,1)S(1)}, bf16[32,16,128]{2,1,0:T(8,128)(2,1)S(1)}, u32[]{:S(2)}, u32[]{:S(2)}) %collective-permute-start.33) | collective-permute-done | bytes 131104 | tf_op jit(solution)/shard_map/ppermute | solution.py:226
  117.1 2.1 %collective-permute-start.36 = (bf16[2,32,16,128]{3,2,1,0:T(8,128)(2,1)S(1)}, bf16[2,32,16,128]{3,2,1,0:T(8,128)(2,1)S(1)}, u32[]{:S(2)}, u32[]{:S(2)}) collective-permute-start(bf16[2,32,16,128]{3,2,1,0:T(8,128)(2,1)S(1)} %get-tuple-element.43), channel_id=1, source_target_pairs={{0,96},{32,0},{64,32},{96,64},{1,97},{33,1},{65,33},{97,65},{2,98}... | collective-permute-start | bytes 786440 | tf_op jit(solution)/shard_map/ppermute | solution.py:226
  119.2 5.7 %collective-permute-done.35.plus = bf16[2,32,16,128]{3,2,1,0:T(8,128)(2,1)S(1)} collective-permute-done((bf16[2,32,16,128]{3,2,1,0:T(8,128)(2,1)S(1)}, bf16[2,32,16,128]{3,2,1,0:T(8,128)(2,1)S(1)}, u32[]{:S(2)}, u32[]{:S(2)}) %collective-permute-start.35) | collective-permute-done | bytes 262176 | tf_op jit(solution)/shard_map/ppermute | solution.py:226
  127.3 2.8 %collective-permute-done.37.taken = bf16[32,16,128]{2,1,0:T(8,128)(2,1)S(1)} collective-permute-done((bf16[32,16,128]{2,1,0:T(8,128)(2,1)S(1)}, bf16[32,16,128]{2,1,0:T(8,128)(2,1)S(1)}, u32[]{:S(2)}, u32[]{:S(2)}) %collective-permute-start.37) | collective-permute-done | bytes 131104 | tf_op jit(solution)/shard_map/ppermute | solution.py:226
  (80 shorter events, 29.4 us)
Async XLA Ops:
  5.2 8.4 %collective-permute-start = (bf16[32,16,128]{2,1,0:T(8,128)(2,1)S(1)}, bf16[32,16,128]{2,1,0:T(8,128)(2,1)S(1)}, u32[]{:S(2)}, u32[]{:S(2)}) collective-permute-start(bf16[32,16,128]{2,1,0:T(8,128)(2,1)S(1)} %shard_map.77.refs_0_), channel_id=1, source_target_pairs={{0,32},{32,64},{64,96},{96,0},{1,33},{33,65},{65,97},{97,1},{2,34}... | collective-permute-start | bytes 393224 | tf_op jit(solution)/shard_map/ppermute | solution.py:226
  8.8 6.1 %collective-permute-start.4 = (bf16[32,16,128]{2,1,0:T(8,128)(2,1)S(1)}, bf16[32,16,128]{2,1,0:T(8,128)(2,1)S(1)}, u32[]{:S(2)}, u32[]{:S(2)}) collective-permute-start(bf16[32,16,128]{2,1,0:T(8,128)(2,1)S(1)} %collective-permute-done.2.refs_1_.refs_3_), channel_id=1, source_target_pairs={{0,96},{32,0},{64,32},{96,64},{1,97},{33,1},{65,33},{97,65},{2,98}... | collective-permute-start | bytes 393224 | tf_op jit(solution)/shard_map/ppermute | solution.py:226
  11.6 7.0 %collective-permute-start.1 = (bf16[32,16,128]{2,1,0:T(8,128)(2,1)S(1)}, bf16[32,16,128]{2,1,0:T(8,128)(2,1)S(1)}, u32[]{:S(2)}, u32[]{:S(2)}) collective-permute-start(bf16[32,16,128]{2,1,0:T(8,128)(2,1)S(1)} %shard_map.77.refs_0_), channel_id=1, source_target_pairs={{0,96},{32,0},{64,32},{96,64},{1,97},{33,1},{65,33},{97,65},{2,98}... | collective-permute-start | bytes 393224 | tf_op jit(solution)/shard_map/ppermute | solution.py:226
  12.4 6.4 %collective-permute-start.5 = (bf16[32,16,128]{2,1,0:T(8,128)(2,1)S(1)}, bf16[32,16,128]{2,1,0:T(8,128)(2,1)S(1)}, u32[]{:S(2)}, u32[]{:S(2)}) collective-permute-start(bf16[32,16,128]{2,1,0:T(8,128)(2,1)S(1)} %collective-permute-done.2.refs_1_.refs_3_), channel_id=1, source_target_pairs={{0,32},{32,64},{64,96},{96,0},{1,33},{33,65},{65,97},{97,1},{2,34}... | collective-permute-start | bytes 393224 | tf_op jit(solution)/shard_map/ppermute | solution.py:226
  13.6 6.6 %collective-permute-start.3 = (bf16[32,16,128]{2,1,0:T(8,128)(2,1)S(1)}, bf16[32,16,128]{2,1,0:T(8,128)(2,1)S(1)}, u32[]{:S(2)}, u32[]{:S(2)}) collective-permute-start(bf16[32,16,128]{2,1,0:T(8,128)(2,1)S(1)} %collective-permute-done.refs_2_.refs_1_), channel_id=1, source_target_pairs={{0,32},{32,64},{64,96},{96,0},{1,33},{33,65},{65,97},{97,1},{2,34}... | collective-permute-start | bytes 393224 | tf_op jit(solution)/shard_map/ppermute | solution.py:226
  14.9 6.2 %collective-permute-start.6 = (bf16[32,16,128]{2,1,0:T(8,128)(2,1)S(1)}, bf16[32,16,128]{2,1,0:T(8,128)(2,1)S(1)}, u32[]{:S(2)}, u32[]{:S(2)}) collective-permute-start(bf16[32,16,128]{2,1,0:T(8,128)(2,1)S(1)} %collective-permute-done.4.refs_0_.refs_5_), channel_id=1, source_target_pairs={{0,96},{32,0},{64,32},{96,64},{1,97},{33,1},{65,33},{97,65},{2,98}... | collective-permute-start | bytes 393224 | tf_op jit(solution)/shard_map/ppermute | solution.py:226
  26.4 7.2 %collective-permute-start.9 = (bf16[32,16,128]{2,1,0:T(8,128)(2,1)S(1)}, bf16[32,16,128]{2,1,0:T(8,128)(2,1)S(1)}, u32[]{:S(2)}, u32[]{:S(2)}) collective-permute-start(bf16[32,16,128]{2,1,0:T(8,128)(2,1)S(1)} %get-tuple-element.25), channel_id=1, source_target_pairs={{0,8},{8,0},{1,9},{9,1},{2,10},{10,2},{3,11},{11,3},{4,12},{12,4},... | collective-permute-start | bytes 393224 | tf_op jit(solution)/shard_map/ppermute | solution.py:226
  29.7 10.1 %collective-permute-start.11 = (bf16[2,32,16,128]{3,2,1,0:T(8,128)(2,1)S(1)}, bf16[2,32,16,128]{3,2,1,0:T(8,128)(2,1)S(1)}, u32[]{:S(2)}, u32[]{:S(2)}) collective-permute-start(bf16[2,32,16,128]{3,2,1,0:T(8,128)(2,1)S(1)} %get-tuple-element.27), channel_id=1, source_target_pairs={{0,8},{8,0},{1,9},{9,1},{2,10},{10,2},{3,11},{11,3},{4,12},{12,4},... | collective-permute-start | bytes 786440 | tf_op jit(solution)/shard_map/ppermute | solution.py:226
  33.6 6.0 %collective-permute-start.10 = (bf16[32,16,128]{2,1,0:T(8,128)(2,1)S(1)}, bf16[32,16,128]{2,1,0:T(8,128)(2,1)S(1)}, u32[]{:S(2)}, u32[]{:S(2)}) collective-permute-start(bf16[32,16,128]{2,1,0:T(8,128)(2,1)S(1)} %shard_map.82), channel_id=1, source_target_pairs={{0,1},{1,2},{2,3},{3,4},{4,5},{5,6},{6,7},{7,0},{8,9},{9,10},{10,1... | collective-permute-start | bytes 393224 | tf_op jit(solution)/shard_map/ppermute | solution.py:226
  35.6 11.1 %collective-permute-start.13 = (bf16[2,32,16,128]{3,2,1,0:T(8,128)(2,1)S(1)}, bf16[2,32,16,128]{3,2,1,0:T(8,128)(2,1)S(1)}, u32[]{:S(2)}, u32[]{:S(2)}) collective-permute-start(bf16[2,32,16,128]{3,2,1,0:T(8,128)(2,1)S(1)} %get-tuple-element.29), channel_id=1, source_target_pairs={{0,8},{8,0},{1,9},{9,1},{2,10},{10,2},{3,11},{11,3},{4,12},{12,4},... | collective-permute-start | bytes 786440 | tf_op jit(solution)/shard_map/ppermute | solution.py:226
  39.6 13.7 %collective-permute-start.15 = (bf16[3,32,16,128]{3,2,1,0:T(8,128)(2,1)S(1)}, bf16[3,32,16,128]{3,2,1,0:T(8,128)(2,1)S(1)}, u32[]{:S(2)}, u32[]{:S(2)}) collective-permute-start(bf16[3,32,16,128]{3,2,1,0:T(8,128)(2,1)S(1)} %get-tuple-element.31), channel_id=1, source_target_pairs={{0,8},{8,0},{1,9},{9,1},{2,10},{10,2},{3,11},{11,3},{4,12},{12,4},... | collective-permute-start | bytes 1179656 | tf_op jit(solution)/shard_map/ppermute | solution.py:226
  39.8 7.0 %collective-permute-start.12 = (bf16[32,16,128]{2,1,0:T(8,128)(2,1)S(1)}, bf16[32,16,128]{2,1,0:T(8,128)(2,1)S(1)}, u32[]{:S(2)}, u32[]{:S(2)}) collective-permute-start(bf16[32,16,128]{2,1,0:T(8,128)(2,1)S(1)} %shard_map.83), channel_id=1, source_target_pairs={{0,1},{1,2},{2,3},{3,4},{4,5},{5,6},{6,7},{7,0},{8,9},{9,10},{10,1... | collective-permute-start | bytes 393224 | tf_op jit(solution)/shard_map/ppermute | solution.py:226
  42.0 6.8 %collective-permute-start.17 = (bf16[32,16,128]{2,1,0:T(8,128)(2,1)S(1)}, bf16[32,16,128]{2,1,0:T(8,128)(2,1)S(1)}, u32[]{:S(2)}, u32[]{:S(2)}) collective-permute-start(bf16[32,16,128]{2,1,0:T(8,128)(2,1)S(1)} %shard_map.86), channel_id=1, source_target_pairs={{0,7},{1,0},{2,1},{3,2},{4,3},{5,4},{6,5},{7,6},{8,15},{9,8},{10,9... | collective-permute-start | bytes 393224 | tf_op jit(solution)/shard_map/ppermute | solution.py:226
  46.8 6.5 %collective-permute-start.14 = (bf16[32,16,128]{2,1,0:T(8,128)(2,1)S(1)}, bf16[32,16,128]{2,1,0:T(8,128)(2,1)S(1)}, u32[]{:S(2)}, u32[]{:S(2)}) collective-permute-start(bf16[32,16,128]{2,1,0:T(8,128)(2,1)S(1)} %shard_map.84), channel_id=1, source_target_pairs={{0,1},{1,2},{2,3},{3,4},{4,5},{5,6},{6,7},{7,0},{8,9},{9,10},{10,1... | collective-permute-start | bytes 393224 | tf_op jit(solution)/shard_map/ppermute | solution.py:226
  48.9 6.5 %collective-permute-start.18 = (bf16[32,16,128]{2,1,0:T(8,128)(2,1)S(1)}, bf16[32,16,128]{2,1,0:T(8,128)(2,1)S(1)}, u32[]{:S(2)}, u32[]{:S(2)}) collective-permute-start(bf16[32,16,128]{2,1,0:T(8,128)(2,1)S(1)} %shard_map.87), channel_id=1, source_target_pairs={{0,7},{1,0},{2,1},{3,2},{4,3},{5,4},{6,5},{7,6},{8,15},{9,8},{10,9... | collective-permute-start | bytes 393224 | tf_op jit(solution)/shard_map/ppermute | solution.py:226
  53.4 5.6 %collective-permute-start.16 = (bf16[32,16,128]{2,1,0:T(8,128)(2,1)S(1)}, bf16[32,16,128]{2,1,0:T(8,128)(2,1)S(1)}, u32[]{:S(2)}, u32[]{:S(2)}) collective-permute-start(bf16[32,16,128]{2,1,0:T(8,128)(2,1)S(1)} %shard_map.85), channel_id=1, source_target_pairs={{0,1},{1,2},{2,3},{3,4},{4,5},{5,6},{6,7},{7,0},{8,9},{9,10},{10,1... | collective-permute-start | bytes 393224 | tf_op jit(solution)/shard_map/ppermute | solution.py:226
  55.4 5.7 %collective-permute-start.19 = (bf16[32,16,128]{2,1,0:T(8,128)(2,1)S(1)}, bf16[32,16,128]{2,1,0:T(8,128)(2,1)S(1)}, u32[]{:S(2)}, u32[]{:S(2)}) collective-permute-start(bf16[32,16,128]{2,1,0:T(8,128)(2,1)S(1)} %shard_map.88), channel_id=1, source_target_pairs={{0,7},{1,0},{2,1},{3,2},{4,3},{5,4},{6,5},{7,6},{8,15},{9,8},{10,9... | collective-permute-start | bytes 393224 | tf_op jit(solution)/shard_map/ppermute | solution.py:226
  66.3 6.9 %collective-permute-start.22 = (bf16[32,16,128]{2,1,0:T(8,128)(2,1)S(1)}, bf16[32,16,128]{2,1,0:T(8,128)(2,1)S(1)}, u32[]{:S(2)}, u32[]{:S(2)}) collective-permute-start(bf16[32,16,128]{2,1,0:T(8,128)(2,1)S(1)} %get-tuple-element.37.refs_0_), channel_id=1, source_target_pairs={{0,7},{1,0},{2,1},{3,2},{4,3},{5,4},{6,5},{7,6},{8,15},{9,8},{10,9... | collective-permute-start | bytes 393224 | tf_op jit(solution)/shard_map/ppermute | solution.py:226
  68.8 7.6 %collective-permute-start.24 = (bf16[32,16,128]{2,1,0:T(8,128)(2,1)S(1)}, bf16[32,16,128]{2,1,0:T(8,128)(2,1)S(1)}, u32[]{:S(2)}, u32[]{:S(2)}) collective-permute-start(bf16[32,16,128]{2,1,0:T(8,128)(2,1)S(1)} %collective-permute-done.21.refs_0_.refs_2_), channel_id=1, source_target_pairs={{0,1},{1,2},{2,3},{3,4},{4,5},{5,6},{6,7},{7,0},{8,9},{9,10},{10,1... | collective-permute-start | bytes 393224 | tf_op jit(solution)/shard_map/ppermute | solution.py:226
  73.1 6.2 %collective-permute-start.25 = (bf16[32,16,128]{2,1,0:T(8,128)(2,1)S(1)}, bf16[32,16,128]{2,1,0:T(8,128)(2,1)S(1)}, u32[]{:S(2)}, u32[]{:S(2)}) collective-permute-start(bf16[32,16,128]{2,1,0:T(8,128)(2,1)S(1)} %collective-permute-done.22.refs_1_.refs_3_), channel_id=1, source_target_pairs={{0,7},{1,0},{2,1},{3,2},{4,3},{5,4},{6,5},{7,6},{8,15},{9,8},{10,9... | collective-permute-start | bytes 393224 | tf_op jit(solution)/shard_map/ppermute | solution.py:226
  76.4 6.8 %collective-permute-start.27 = (bf16[32,16,128]{2,1,0:T(8,128)(2,1)S(1)}, bf16[32,16,128]{2,1,0:T(8,128)(2,1)S(1)}, u32[]{:S(2)}, u32[]{:S(2)}) collective-permute-start(bf16[32,16,128]{2,1,0:T(8,128)(2,1)S(1)} %collective-permute-done.24.refs_0_.refs_5_), channel_id=1, source_target_pairs={{0,1},{1,2},{2,3},{3,4},{4,5},{5,6},{6,7},{7,0},{8,9},{9,10},{10,1... | collective-permute-start | bytes 393224 | tf_op jit(solution)/shard_map/ppermute | solution.py:226
  79.4 6.0 %collective-permute-start.28 = (bf16[32,16,128]{2,1,0:T(8,128)(2,1)S(1)}, bf16[32,16,128]{2,1,0:T(8,128)(2,1)S(1)}, u32[]{:S(2)}, u32[]{:S(2)}) collective-permute-start(bf16[32,16,128]{2,1,0:T(8,128)(2,1)S(1)} %collective-permute-done.25.refs_1_.refs_6_), channel_id=1, source_target_pairs={{0,7},{1,0},{2,1},{3,2},{4,3},{5,4},{6,5},{7,6},{8,15},{9,8},{10,9... | collective-permute-start | bytes 393224 | tf_op jit(solution)/shard_map/ppermute | solution.py:226
  79.4 20.2 %collective-permute-start.23 = (bf16[2,32,16,128]{3,2,1,0:T(8,128)(2,1)S(1)}, bf16[2,32,16,128]{3,2,1,0:T(8,128)(2,1)S(1)}, u32[]{:S(2)}, u32[]{:S(2)}) collective-permute-start(bf16[2,32,16,128]{3,2,1,0:T(8,128)(2,1)S(1)} %shard_map.90), channel_id=1, source_target_pairs={{0,8},{8,0},{1,9},{9,1},{2,10},{10,2},{3,11},{11,3},{4,12},{12,4},... | collective-permute-start | bytes 786440 | tf_op jit(solution)/shard_map/ppermute | solution.py:226
  83.1 16.5 %collective-permute-start.26 = (bf16[2,32,16,128]{3,2,1,0:T(8,128)(2,1)S(1)}, bf16[2,32,16,128]{3,2,1,0:T(8,128)(2,1)S(1)}, u32[]{:S(2)}, u32[]{:S(2)}) collective-permute-start(bf16[2,32,16,128]{3,2,1,0:T(8,128)(2,1)S(1)} %shard_map.91), channel_id=1, source_target_pairs={{0,8},{8,0},{1,9},{9,1},{2,10},{10,2},{3,11},{11,3},{4,12},{12,4},... | collective-permute-start | bytes 786440 | tf_op jit(solution)/shard_map/ppermute | solution.py:226
  83.2 5.8 %collective-permute-start.30 = (bf16[32,16,128]{2,1,0:T(8,128)(2,1)S(1)}, bf16[32,16,128]{2,1,0:T(8,128)(2,1)S(1)}, u32[]{:S(2)}, u32[]{:S(2)}) collective-permute-start(bf16[32,16,128]{2,1,0:T(8,128)(2,1)S(1)} %collective-permute-done.27.refs_0_.refs_8_), channel_id=1, source_target_pairs={{0,1},{1,2},{2,3},{3,4},{4,5},{5,6},{6,7},{7,0},{8,9},{9,10},{10,1... | collective-permute-start | bytes 393224 | tf_op jit(solution)/shard_map/ppermute | solution.py:226
  85.4 14.2 %collective-permute-start.29 = (bf16[2,32,16,128]{3,2,1,0:T(8,128)(2,1)S(1)}, bf16[2,32,16,128]{3,2,1,0:T(8,128)(2,1)S(1)}, u32[]{:S(2)}, u32[]{:S(2)}) collective-permute-start(bf16[2,32,16,128]{3,2,1,0:T(8,128)(2,1)S(1)} %shard_map.92), channel_id=1, source_target_pairs={{0,8},{8,0},{1,9},{9,1},{2,10},{10,2},{3,11},{11,3},{4,12},{12,4},... | collective-permute-start | bytes 786440 | tf_op jit(solution)/shard_map/ppermute | solution.py:226
  88.7 10.9 %collective-permute-start.20 = (bf16[32,16,128]{2,1,0:T(8,128)(2,1)S(1)}, bf16[32,16,128]{2,1,0:T(8,128)(2,1)S(1)}, u32[]{:S(2)}, u32[]{:S(2)}) collective-permute-start(bf16[32,16,128]{2,1,0:T(8,128)(2,1)S(1)} %get-tuple-element.37.refs_0_), channel_id=1, source_target_pairs={{0,8},{8,0},{1,9},{9,1},{2,10},{10,2},{3,11},{11,3},{4,12},{12,4},... | collective-permute-start | bytes 393224 | tf_op jit(solution)/shard_map/ppermute | solution.py:226
  89.0 12.0 %collective-permute-start.31 = (bf16[32,16,128]{2,1,0:T(8,128)(2,1)S(1)}, bf16[32,16,128]{2,1,0:T(8,128)(2,1)S(1)}, u32[]{:S(2)}, u32[]{:S(2)}) collective-permute-start(bf16[32,16,128]{2,1,0:T(8,128)(2,1)S(1)} %collective-permute-done.30.refs_11_), channel_id=1, source_target_pairs={{0,8},{8,0},{1,9},{9,1},{2,10},{10,2},{3,11},{11,3},{4,12},{12,4},... | collective-permute-start | bytes 393224 | tf_op jit(solution)/shard_map/ppermute | solution.py:226
  108.2 7.5 %collective-permute-start.33 = (bf16[32,16,128]{2,1,0:T(8,128)(2,1)S(1)}, bf16[32,16,128]{2,1,0:T(8,128)(2,1)S(1)}, u32[]{:S(2)}, u32[]{:S(2)}) collective-permute-start(bf16[32,16,128]{2,1,0:T(8,128)(2,1)S(1)} %get-tuple-element.40), channel_id=1, source_target_pairs={{0,32},{32,64},{64,96},{96,0},{1,33},{33,65},{65,97},{97,1},{2,34}... | collective-permute-start | bytes 393224 | tf_op jit(solution)/shard_map/ppermute | solution.py:226
  108.6 7.2 %collective-permute-start.34 = (bf16[32,16,128]{2,1,0:T(8,128)(2,1)S(1)}, bf16[32,16,128]{2,1,0:T(8,128)(2,1)S(1)}, u32[]{:S(2)}, u32[]{:S(2)}) collective-permute-start(bf16[32,16,128]{2,1,0:T(8,128)(2,1)S(1)} %get-tuple-element.41), channel_id=1, source_target_pairs={{0,96},{32,0},{64,32},{96,64},{1,97},{33,1},{65,33},{97,65},{2,98}... | collective-permute-start | bytes 393224 | tf_op jit(solution)/shard_map/ppermute | solution.py:226
  115.9 9.1 %collective-permute-start.35 = (bf16[2,32,16,128]{3,2,1,0:T(8,128)(2,1)S(1)}, bf16[2,32,16,128]{3,2,1,0:T(8,128)(2,1)S(1)}, u32[]{:S(2)}, u32[]{:S(2)}) collective-permute-start(bf16[2,32,16,128]{3,2,1,0:T(8,128)(2,1)S(1)} %get-tuple-element.42), channel_id=1, source_target_pairs={{0,32},{32,64},{64,96},{96,0},{1,33},{33,65},{65,97},{97,1},{2,34}... | collective-permute-start | bytes 786440 | tf_op jit(solution)/shard_map/ppermute | solution.py:226
  117.1 7.9 %collective-permute-start.36 = (bf16[2,32,16,128]{3,2,1,0:T(8,128)(2,1)S(1)}, bf16[2,32,16,128]{3,2,1,0:T(8,128)(2,1)S(1)}, u32[]{:S(2)}, u32[]{:S(2)}) collective-permute-start(bf16[2,32,16,128]{3,2,1,0:T(8,128)(2,1)S(1)} %get-tuple-element.43), channel_id=1, source_target_pairs={{0,96},{32,0},{64,32},{96,64},{1,97},{33,1},{65,33},{97,65},{2,98}... | collective-permute-start | bytes 786440 | tf_op jit(solution)/shard_map/ppermute | solution.py:226
  (12 other events, 183.5 us)

commit v2 on v1

--- a/solution.py
+++ b/solution.py
@@ -64,15 +64,48 @@
     return lax.dot_general(stacked, inverse, dims, precision=HIGH, preferred_element_type=F32)
 
 
-def spectra_body(forward, traces, out, buf):
-    for n in range(traces.shape[1]):
+def spectra_body(forward_hbm, traces_hbm, out, forward, traces, buf, arrived):
+    width = traces.shape[1]
+    half = width // 2
+    fetches = [pltpu.make_async_copy(forward_hbm, forward, arrived.at[2])]
+    for i in range(2):
+        part = pl.ds(i * half, half)
+        fetches.append(
+            pltpu.make_async_copy(traces_hbm.at[:, part], traces.at[:, part], arrived.at[i])
+        )
+    for fetch in fetches:
+        fetch.start()
+    fetches[0].wait()
+    for n in range(width):
+        if n % half == 0:
+            fetches[1 + n // half].wait()
         buf[:, n, :] = to_spec(forward[...], traces[:, n, :])
     out[...] = buf[...].astype(BF16)
 
 
+def spectra(forward, traces):
+    count, lanes = forward.shape[0] // 2, 2 * traces.shape[0]
+    shape = (count, traces.shape[1], lanes)
+    hbm = pltpu.HBM
+    return pl.pallas_call(
+        spectra_body,
+        in_specs=[pl.BlockSpec(memory_space=hbm)] * 2,
+        out_specs=pl.BlockSpec(memory_space=pltpu.VMEM),
+        out_shape=pltpu.VMEM(shape, BF16),
+        scratch_shapes=[
+            pltpu.VMEM(forward.shape, F32),
+            pltpu.VMEM(traces.shape, F32),
+            pltpu.VMEM(shape, F32),
+            pltpu.SemaphoreType.DMA((3,)),
+        ],
+        compiler_params=pltpu.CompilerParams(vmem_limit_bytes=4 << 20),
+        name="spectra",
+    )(*[pltpu.with_memory_space_constraint(arg, hbm) for arg in (forward, traces)])
+
+
 def middle_body(forward, inverse, onset, plus, minus, share, far, upgoing, out, total, buf):
     ring = plus[...].astype(F32) + minus[...].astype(F32)
-    total[...] = ring + (share[...] + far[0].astype(F32))
+    total[...] = ring + (share[...] + far[...].astype(F32))
     points, width, samples = upgoing.shape
     time = lax.broadcasted_iota(jnp.int32, (points, samples), 1)
     for n in range(width):
@@ -241,7 +274,7 @@
     arrived = pltpu.SemaphoreType.DMA((count // UNROLL,))
     half_kernel = (2, count, kernel.shape[2] // 2, kernel.shape[3])
 
-    (own,) = local(spectra_body, [(one, BF16)], [forward, focusing], [buf])
+    own = spectra(forward, focusing)
     near = {(0, 0): own}
     near[0, -1] = move(own, "x", 1)
     near[0, 1] = move(own, "x", -1)
@@ -270,7 +303,7 @@
             kernel,
         )
 
-    slots = [(4,), (3, 5), (2, 6), (0, 1, 7)]
+    slots = [(4,), (3, 5), (2, 6), (1, 7), (0,)]
     far = [move(value, "yh", 1) for value in conv(1, slots, BF16)]
     share = conv(0, [(dz,) for dz in range(NZ)], F32)
     (plus,) = local(join_body, [(one, BF16)], [share[4], far[0]])
@@ -278,18 +311,18 @@
     first = functools.partial(first_body, at=1)
     (minus,) = local(first, [(one, BF16)], [share[5], far[1]])
     minus = move(minus, "z", -1)
-    for dz, group, at in ((3, 1, 0), (2, 2, 0), (1, 3, 1)):
+    for dz, group, at in ((3, 1, 0), (2, 2, 0), (1, 3, 0)):
         body = functools.partial(hop_body, at=at)
         (plus,) = local(body, [(one, BF16)], [plus, share[dz], far[group]])
         plus = move(plus, "z", 1)
-    for dz, group, at in ((6, 2, 1), (7, 3, 2)):
+    for dz, group, at in ((6, 2, 1), (7, 3, 1)):
         body = functools.partial(hop_body, at=at)
         (minus,) = local(body, [(one, BF16)], [minus, share[dz], far[group]])
         minus = move(minus, "z", -1)
     upgoing, mine = local(
         middle_body,
         [(focusing.shape, F32), (one, BF16)],
-        [forward, inverse, limits_up, plus, minus, share[0], far[3]],
+        [forward, inverse, limits_up, plus, minus, share[0], far[4]],
         [buf, buf],
     )
 

time: 135 us -> 135 us (level)
  the two profiles are of different devices: /device:TPU:32 before, /device:TPU:6 now
where the time goes in v2:
time: 135 us; the launch traced here: 134 us
  waiting for transfers between devices  57.2 us (42%)
  starting transfers between devices  56 us (41%)
  Pallas kernels  17.9 us (13%)
  local copies, waits for them, and re-layouts  2.47 us (2%)
    ppermute x39, waiting for transfers between devices, move(): lax.ppermute(value, axis, [(i, (i + step) % size) for i in range(size)])  57.2 us
    ppermute x39, starting transfers between devices, move(): lax.ppermute(value, axis, [(i, (i + step) % size) for i in range(size)])  56 us
    pallas_call x20, Pallas kernels, local(): pl.pallas_call(body, in_specs=[pl.BlockSpec(memory_space=pltpu.HBM)] * le...  15.5 us
  transfers between devices with their start and end apart: 39, of which 22 were waited for; matrix products, arithmetic and copies ran while one was open for 1% of the time, Pallas kernels for 3%

profile of v2, /device:TPU:6, one launch (start us, length us, event | category | flops | bytes accessed | tf_op | source)
XLA Modules:
  0.0 134.4 jit_solution(14885662678258723023)
XLA Ops:
  0.6 2.3 %spectra.1.refs_0_ = bf16[32,16,128]{2,1,0:T(8,128)(2,1)S(1)} custom-call(f32[64,128]{1,0:T(8,128)} %constant.46.clone.forward_hbm.forward, f32[64,16,128]{2,1,0:T(8,128)} %traces_hbm.1), custom_call_target="tpu_custom_call" | custom-call | tf_op jit(solution)/shard_map/spectra/pallas_call | solution.py:90
  5.3 3.0 %collective-permute-done.2.refs_1_.refs_3_ = bf16[32,16,128]{2,1,0:T(8,128)(2,1)S(1)} collective-permute-done((bf16[32,16,128]{2,1,0:T(8,128)(2,1)S(1)}, bf16[32,16,128]{2,1,0:T(8,128)(2,1)S(1)}, u32[]{:S(2)}, u32[]{:S(2)}) %collective-permute-start.2) | collective-permute-done | bytes 131104 | tf_op jit(solution)/shard_map/ppermute | solution.py:259
  9.6 2.7 %collective-permute-start.5 = (bf16[32,16,128]{2,1,0:T(8,128)(2,1)S(1)}, bf16[32,16,128]{2,1,0:T(8,128)(2,1)S(1)}, u32[]{:S(2)}, u32[]{:S(2)}) collective-permute-start(bf16[32,16,128]{2,1,0:T(8,128)(2,1)S(1)} %collective-permute-done.2.refs_1_.refs_3_), channel_id=1, source_target_pairs={{0,32},{32,64},{64,96},{96,0},{1,33},{33,65},{65,97},{97,1},{2,34}... | collective-permute-start | bytes 393224 | tf_op jit(solution)/shard_map/ppermute | solution.py:259
  17.4 4.0 %collective-permute-done.6.refs_3_.refs_7_ = bf16[32,16,128]{2,1,0:T(8,128)(2,1)S(1)} collective-permute-done((bf16[32,16,128]{2,1,0:T(8,128)(2,1)S(1)}, bf16[32,16,128]{2,1,0:T(8,128)(2,1)S(1)}, u32[]{:S(2)}, u32[]{:S(2)}) %collective-permute-start.6) | collective-permute-done | bytes 131104 | tf_op jit(solution)/shard_map/ppermute | solution.py:259
  23.5 3.3 %shard_map.80 = (bf16[32,16,128]{2,1,0:T(8,128)(2,1)S(1)}, bf16[2,32,16,128]{3,2,1,0:T(8,128)(2,1)S(1)}, bf16[2,32,16,128]{3,2,1,0:T(8,128)(2,1)S(1)}, bf16[2,32...) custom-call(bf16[2,32,256,256]{3,2,1,0:T(8,128)(2,1)} %source.5, bf16[32,16,128]{2,1,0:T(8,128)(2,1)S(1)} %spectra.1.refs_0_, ...), custom_call_target="tpu_custom_call" | custom-call | tf_op jit(solution)/shard_map/pallas_call | solution.py:33
  26.8 3.3 %collective-permute-start.9 = (bf16[32,16,128]{2,1,0:T(8,128)(2,1)S(1)}, bf16[32,16,128]{2,1,0:T(8,128)(2,1)S(1)}, u32[]{:S(2)}, u32[]{:S(2)}) collective-permute-start(bf16[32,16,128]{2,1,0:T(8,128)(2,1)S(1)} %get-tuple-element.26), channel_id=1, source_target_pairs={{0,8},{8,0},{1,9},{9,1},{2,10},{10,2},{3,11},{11,3},{4,12},{12,4},... | collective-permute-start | bytes 393224 | tf_op jit(solution)/shard_map/ppermute | solution.py:259
  30.4 3.3 %shard_map.79 = (f32[32,16,128]{2,1,0:T(8,128)S(1)}, f32[32,16,128]{2,1,0:T(8,128)S(1)}, f32[32,16,128]{2,1,0:T(8,128)S(1)}, f32[32,16,128]{2,1,0:T(8,128)S(1)},...) custom-call(bf16[2,32,256,256]{3,2,1,0:T(8,128)(2,1)} %source.5, ...), custom_call_target="tpu_custom_call" | custom-call | tf_op jit(solution)/shard_map/pallas_call | solution.py:33
  34.0 2.0 %collective-permute-start.10 = (bf16[32,16,128]{2,1,0:T(8,128)(2,1)S(1)}, bf16[32,16,128]{2,1,0:T(8,128)(2,1)S(1)}, u32[]{:S(2)}, u32[]{:S(2)}) collective-permute-start(bf16[32,16,128]{2,1,0:T(8,128)(2,1)S(1)} %shard_map.81), channel_id=1, source_target_pairs={{0,1},{1,2},{2,3},{3,4},{4,5},{5,6},{6,7},{7,0},{8,9},{9,10},{10,1... | collective-permute-start | bytes 393224 | tf_op jit(solution)/shard_map/ppermute | solution.py:259
  36.0 4.0 %collective-permute-start.13 = (bf16[2,32,16,128]{3,2,1,0:T(8,128)(2,1)S(1)}, bf16[2,32,16,128]{3,2,1,0:T(8,128)(2,1)S(1)}, u32[]{:S(2)}, u32[]{:S(2)}) collective-permute-start(bf16[2,32,16,128]{3,2,1,0:T(8,128)(2,1)S(1)} %get-tuple-element.30), channel_id=1, source_target_pairs={{0,8},{8,0},{1,9},{9,1},{2,10},{10,2},{3,11},{11,3},{4,12},{12,4},... | collective-permute-start | bytes 786440 | tf_op jit(solution)/shard_map/ppermute | solution.py:259
  40.0 3.0 %collective-permute-done.10.taken = bf16[32,16,128]{2,1,0:T(8,128)(2,1)S(1)} collective-permute-done((bf16[32,16,128]{2,1,0:T(8,128)(2,1)S(1)}, bf16[32,16,128]{2,1,0:T(8,128)(2,1)S(1)}, u32[]{:S(2)}, u32[]{:S(2)}) %collective-permute-start.10) | collective-permute-done | bytes 131104 | tf_op jit(solution)/shard_map/ppermute | solution.py:259
  43.1 4.2 %collective-permute-start.15 = (bf16[2,32,16,128]{3,2,1,0:T(8,128)(2,1)S(1)}, bf16[2,32,16,128]{3,2,1,0:T(8,128)(2,1)S(1)}, u32[]{:S(2)}, u32[]{:S(2)}) collective-permute-start(bf16[2,32,16,128]{3,2,1,0:T(8,128)(2,1)S(1)} %get-tuple-element.32), channel_id=1, source_target_pairs={{0,8},{8,0},{1,9},{9,1},{2,10},{10,2},{3,11},{11,3},{4,12},{12,4},... | collective-permute-start | bytes 786440 | tf_op jit(solution)/shard_map/ppermute | solution.py:259
  47.3 3.0 %collective-permute-start.17 = (bf16[32,16,128]{2,1,0:T(8,128)(2,1)S(1)}, bf16[32,16,128]{2,1,0:T(8,128)(2,1)S(1)}, u32[]{:S(2)}, u32[]{:S(2)}) collective-permute-start(bf16[32,16,128]{2,1,0:T(8,128)(2,1)S(1)} %shard_map.85), channel_id=1, source_target_pairs={{0,7},{1,0},{2,1},{3,2},{4,3},{5,4},{6,5},{7,6},{8,15},{9,8},{10,9... | collective-permute-start | bytes 393224 | tf_op jit(solution)/shard_map/ppermute | solution.py:259
  50.5 2.4 %collective-permute-done.17.taken = bf16[32,16,128]{2,1,0:T(8,128)(2,1)S(1)} collective-permute-done((bf16[32,16,128]{2,1,0:T(8,128)(2,1)S(1)}, bf16[32,16,128]{2,1,0:T(8,128)(2,1)S(1)}, u32[]{:S(2)}, u32[]{:S(2)}) %collective-permute-start.17) | collective-permute-done | bytes 131104 | tf_op jit(solution)/shard_map/ppermute | solution.py:259
  52.9 3.7 %collective-permute-start.18 = (bf16[32,16,128]{2,1,0:T(8,128)(2,1)S(1)}, bf16[32,16,128]{2,1,0:T(8,128)(2,1)S(1)}, u32[]{:S(2)}, u32[]{:S(2)}) collective-permute-start(bf16[32,16,128]{2,1,0:T(8,128)(2,1)S(1)} %shard_map.86), channel_id=1, source_target_pairs={{0,7},{1,0},{2,1},{3,2},{4,3},{5,4},{6,5},{7,6},{8,15},{9,8},{10,9... | collective-permute-start | bytes 393224 | tf_op jit(solution)/shard_map/ppermute | solution.py:259
  57.1 2.3 %collective-permute-done.18.taken = bf16[32,16,128]{2,1,0:T(8,128)(2,1)S(1)} collective-permute-done((bf16[32,16,128]{2,1,0:T(8,128)(2,1)S(1)}, bf16[32,16,128]{2,1,0:T(8,128)(2,1)S(1)}, u32[]{:S(2)}, u32[]{:S(2)}) %collective-permute-start.18) | collective-permute-done | bytes 131104 | tf_op jit(solution)/shard_map/ppermute | solution.py:259
  59.5 3.8 %collective-permute-start.19 = (bf16[32,16,128]{2,1,0:T(8,128)(2,1)S(1)}, bf16[32,16,128]{2,1,0:T(8,128)(2,1)S(1)}, u32[]{:S(2)}, u32[]{:S(2)}) collective-permute-start(bf16[32,16,128]{2,1,0:T(8,128)(2,1)S(1)} %shard_map.87), channel_id=1, source_target_pairs={{0,7},{1,0},{2,1},{3,2},{4,3},{5,4},{6,5},{7,6},{8,15},{9,8},{10,9... | collective-permute-start | bytes 393224 | tf_op jit(solution)/shard_map/ppermute | solution.py:259
  65.8 2.7 %shard_map.88 = (f32[64,16,128]{2,1,0:T(8,128)S(1)}, bf16[32,16,128]{2,1,0:T(8,128)(2,1)S(1)}) custom-call(f32[64,128]{1,0:T(8,128)S(1)} %copy-done.1, f32[64,128]{1,0:T(8,128)S(1)} %copy-done.3, s32[64,16]{1,0:T(8,128)S(1)} %get-tuple-element.49.onset, bf16[32,16,128]{2,1,0:T(8,128)(2,1)S(1)} %collective-permute-done.16.plus, ...), custom_call_target="tpu_custom_call" | custom-call | tf_op jit(solution)/shard_map/pallas_call | solution.py:33
  69.0 3.3 %collective-permute-start.23 = (bf16[32,16,128]{2,1,0:T(8,128)(2,1)S(1)}, bf16[32,16,128]{2,1,0:T(8,128)(2,1)S(1)}, u32[]{:S(2)}, u32[]{:S(2)}) collective-permute-start(bf16[32,16,128]{2,1,0:T(8,128)(2,1)S(1)} %get-tuple-element.39.refs_0_), channel_id=1, source_target_pairs={{0,7},{1,0},{2,1},{3,2},{4,3},{5,4},{6,5},{7,6},{8,15},{9,8},{10,9... | collective-permute-start | bytes 393224 | tf_op jit(solution)/shard_map/ppermute | solution.py:259
  72.3 3.2 %collective-permute-done.22.refs_0_.refs_2_ = bf16[32,16,128]{2,1,0:T(8,128)(2,1)S(1)} collective-permute-done((bf16[32,16,128]{2,1,0:T(8,128)(2,1)S(1)}, bf16[32,16,128]{2,1,0:T(8,128)(2,1)S(1)}, u32[]{:S(2)}, u32[]{:S(2)}) %collective-permute-start.22) | collective-permute-done | bytes 131104 | tf_op jit(solution)/shard_map/ppermute | solution.py:259
  75.5 3.2 %collective-permute-start.26 = (bf16[32,16,128]{2,1,0:T(8,128)(2,1)S(1)}, bf16[32,16,128]{2,1,0:T(8,128)(2,1)S(1)}, u32[]{:S(2)}, u32[]{:S(2)}) collective-permute-start(bf16[32,16,128]{2,1,0:T(8,128)(2,1)S(1)} %collective-permute-done.23.refs_1_.refs_3_), channel_id=1, source_target_pairs={{0,7},{1,0},{2,1},{3,2},{4,3},{5,4},{6,5},{7,6},{8,15},{9,8},{10,9... | collective-permute-start | bytes 393224 | tf_op jit(solution)/shard_map/ppermute | solution.py:259
  78.7 2.9 %collective-permute-done.25.refs_0_.refs_5_ = bf16[32,16,128]{2,1,0:T(8,128)(2,1)S(1)} collective-permute-done((bf16[32,16,128]{2,1,0:T(8,128)(2,1)S(1)}, bf16[32,16,128]{2,1,0:T(8,128)(2,1)S(1)}, u32[]{:S(2)}, u32[]{:S(2)}) %collective-permute-start.25) | collective-permute-done | bytes 131104 | tf_op jit(solution)/shard_map/ppermute | solution.py:259
  82.0 2.9 %collective-permute-start.29 = (bf16[32,16,128]{2,1,0:T(8,128)(2,1)S(1)}, bf16[32,16,128]{2,1,0:T(8,128)(2,1)S(1)}, u32[]{:S(2)}, u32[]{:S(2)}) collective-permute-start(bf16[32,16,128]{2,1,0:T(8,128)(2,1)S(1)} %collective-permute-done.26.refs_1_.refs_6_), channel_id=1, source_target_pairs={{0,7},{1,0},{2,1},{3,2},{4,3},{5,4},{6,5},{7,6},{8,15},{9,8},{10,9... | collective-permute-start | bytes 393224 | tf_op jit(solution)/shard_map/ppermute | solution.py:259
  85.7 3.1 %collective-permute-start.27 = (bf16[2,32,16,128]{3,2,1,0:T(8,128)(2,1)S(1)}, bf16[2,32,16,128]{3,2,1,0:T(8,128)(2,1)S(1)}, u32[]{:S(2)}, u32[]{:S(2)}) collective-permute-start(bf16[2,32,16,128]{3,2,1,0:T(8,128)(2,1)S(1)} %shard_map.90), channel_id=1, source_target_pairs={{0,8},{8,0},{1,9},{9,1},{2,10},{10,2},{3,11},{11,3},{4,12},{12,4},... | collective-permute-start | bytes 786440 | tf_op jit(solution)/shard_map/ppermute | solution.py:259
  89.7 2.8 %collective-permute-start.21 = (bf16[32,16,128]{2,1,0:T(8,128)(2,1)S(1)}, bf16[32,16,128]{2,1,0:T(8,128)(2,1)S(1)}, u32[]{:S(2)}, u32[]{:S(2)}) collective-permute-start(bf16[32,16,128]{2,1,0:T(8,128)(2,1)S(1)} %get-tuple-element.39.refs_0_), channel_id=1, source_target_pairs={{0,8},{8,0},{1,9},{9,1},{2,10},{10,2},{3,11},{11,3},{4,12},{12,4},... | collective-permute-start | bytes 393224 | tf_op jit(solution)/shard_map/ppermute | solution.py:259
  92.5 2.5 %collective-permute-done.31.refs_11_ = bf16[32,16,128]{2,1,0:T(8,128)(2,1)S(1)} collective-permute-done((bf16[32,16,128]{2,1,0:T(8,128)(2,1)S(1)}, bf16[32,16,128]{2,1,0:T(8,128)(2,1)S(1)}, u32[]{:S(2)}, u32[]{:S(2)}) %collective-permute-start.31) | collective-permute-done | bytes 131104 | tf_op jit(solution)/shard_map/ppermute | solution.py:259
  95.8 6.7 %collective-permute-done.21.refs_1_ = bf16[32,16,128]{2,1,0:T(8,128)(2,1)S(1)} collective-permute-done((bf16[32,16,128]{2,1,0:T(8,128)(2,1)S(1)}, bf16[32,16,128]{2,1,0:T(8,128)(2,1)S(1)}, u32[]{:S(2)}, u32[]{:S(2)}) %collective-permute-start.21) | collective-permute-done | bytes 131104 | tf_op jit(solution)/shard_map/ppermute | solution.py:259
  103.9 4.5 %shard_map.92 = (bf16[8,32,16,128]{3,2,1,0:T(8,128)(2,1)S(1)}, f32[8,32,16,128]{3,2,1,0:T(8,128)S(1)}) custom-call(bf16[2,32,256,256]{3,2,1,0:T(8,128)(2,1)} %source.5, bf16[32,16,128]{2,1,0:T(8,128)(2,1)S(1)} %get-tuple-element.39.refs_0_, bf16[32,16,128]{2,1,0:T(8,128)(2,1)S(1)} %collective-permute-done.21.refs_1_, ...), custom_call_target="tpu_custom_call" | custom-call | tf_op jit(solution)/shard_map/pallas_call | solution.py:33
  108.5 2.6 %collective-permute-done.33.taken = bf16[8,32,16,128]{3,2,1,0:T(8,128)(2,1)S(1)} collective-permute-done((bf16[8,32,16,128]{3,2,1,0:T(8,128)(2,1)S(1)}, bf16[8,32,16,128]{3,2,1,0:T(8,128)(2,1)S(1)}, u32[]{:S(2)}, u32[]{:S(2)}) %collective-permute-start.33) | collective-permute-done | bytes 1048608 | tf_op jit(solution)/shard_map/ppermute | solution.py:259
  111.2 2.0 %collective-permute-start.35 = (bf16[32,16,128]{2,1,0:T(8,128)(2,1)S(1)}, bf16[32,16,128]{2,1,0:T(8,128)(2,1)S(1)}, u32[]{:S(2)}, u32[]{:S(2)}) collective-permute-start(bf16[32,16,128]{2,1,0:T(8,128)(2,1)S(1)} %get-tuple-element.43), channel_id=1, source_target_pairs={{0,96},{32,0},{64,32},{96,64},{1,97},{33,1},{65,33},{97,65},{2,98}... | collective-permute-start | bytes 393224 | tf_op jit(solution)/shard_map/ppermute | solution.py:259
  113.3 3.5 %collective-permute-done.34.plus = bf16[32,16,128]{2,1,0:T(8,128)(2,1)S(1)} collective-permute-done((bf16[32,16,128]{2,1,0:T(8,128)(2,1)S(1)}, bf16[32,16,128]{2,1,0:T(8,128)(2,1)S(1)}, u32[]{:S(2)}, u32[]{:S(2)}) %collective-permute-start.34) | collective-permute-done | bytes 131104 | tf_op jit(solution)/shard_map/ppermute | solution.py:259
  120.3 5.5 %collective-permute-done.36.plus = bf16[2,32,16,128]{3,2,1,0:T(8,128)(2,1)S(1)} collective-permute-done((bf16[2,32,16,128]{3,2,1,0:T(8,128)(2,1)S(1)}, bf16[2,32,16,128]{3,2,1,0:T(8,128)(2,1)S(1)}, u32[]{:S(2)}, u32[]{:S(2)}) %collective-permute-start.36) | collective-permute-done | bytes 262176 | tf_op jit(solution)/shard_map/ppermute | solution.py:259
  128.7 3.6 %collective-permute-done.38.taken = bf16[32,16,128]{2,1,0:T(8,128)(2,1)S(1)} collective-permute-done((bf16[32,16,128]{2,1,0:T(8,128)(2,1)S(1)}, bf16[32,16,128]{2,1,0:T(8,128)(2,1)S(1)}, u32[]{:S(2)}, u32[]{:S(2)}) %collective-permute-start.38) | collective-permute-done | bytes 131104 | tf_op jit(solution)/shard_map/ppermute | solution.py:259
  (78 shorter events, 28.2 us)
Async XLA Ops:
  4.6 7.7 %collective-permute-start = (bf16[32,16,128]{2,1,0:T(8,128)(2,1)S(1)}, bf16[32,16,128]{2,1,0:T(8,128)(2,1)S(1)}, u32[]{:S(2)}, u32[]{:S(2)}) collective-permute-start(bf16[32,16,128]{2,1,0:T(8,128)(2,1)S(1)} %spectra.1.refs_0_), channel_id=1, source_target_pairs={{0,32},{32,64},{64,96},{96,0},{1,33},{33,65},{65,97},{97,1},{2,34}... | collective-permute-start | bytes 393224 | tf_op jit(solution)/shard_map/ppermute | solution.py:259
  8.3 7.0 %collective-permute-start.4 = (bf16[32,16,128]{2,1,0:T(8,128)(2,1)S(1)}, bf16[32,16,128]{2,1,0:T(8,128)(2,1)S(1)}, u32[]{:S(2)}, u32[]{:S(2)}) collective-permute-start(bf16[32,16,128]{2,1,0:T(8,128)(2,1)S(1)} %collective-permute-done.2.refs_1_.refs_3_), channel_id=1, source_target_pairs={{0,96},{32,0},{64,32},{96,64},{1,97},{33,1},{65,33},{97,65},{2,98}... | collective-permute-start | bytes 393224 | tf_op jit(solution)/shard_map/ppermute | solution.py:259
  9.1 8.2 %collective-permute-start.1 = (bf16[32,16,128]{2,1,0:T(8,128)(2,1)S(1)}, bf16[32,16,128]{2,1,0:T(8,128)(2,1)S(1)}, u32[]{:S(2)}, u32[]{:S(2)}) collective-permute-start(bf16[32,16,128]{2,1,0:T(8,128)(2,1)S(1)} %spectra.1.refs_0_), channel_id=1, source_target_pairs={{0,96},{32,0},{64,32},{96,64},{1,97},{33,1},{65,33},{97,65},{2,98}... | collective-permute-start | bytes 393224 | tf_op jit(solution)/shard_map/ppermute | solution.py:259
  9.6 7.8 %collective-permute-start.5 = (bf16[32,16,128]{2,1,0:T(8,128)(2,1)S(1)}, bf16[32,16,128]{2,1,0:T(8,128)(2,1)S(1)}, u32[]{:S(2)}, u32[]{:S(2)}) collective-permute-start(bf16[32,16,128]{2,1,0:T(8,128)(2,1)S(1)} %collective-permute-done.2.refs_1_.refs_3_), channel_id=1, source_target_pairs={{0,32},{32,64},{64,96},{96,0},{1,33},{33,65},{65,97},{97,1},{2,34}... | collective-permute-start | bytes 393224 | tf_op jit(solution)/shard_map/ppermute | solution.py:259
  15.3 6.2 %collective-permute-start.6 = (bf16[32,16,128]{2,1,0:T(8,128)(2,1)S(1)}, bf16[32,16,128]{2,1,0:T(8,128)(2,1)S(1)}, u32[]{:S(2)}, u32[]{:S(2)}) collective-permute-start(bf16[32,16,128]{2,1,0:T(8,128)(2,1)S(1)} %collective-permute-done.4.refs_0_.refs_5_), channel_id=1, source_target_pairs={{0,96},{32,0},{64,32},{96,64},{1,97},{33,1},{65,33},{97,65},{2,98}... | collective-permute-start | bytes 393224 | tf_op jit(solution)/shard_map/ppermute | solution.py:259
  26.8 7.2 %collective-permute-start.9 = (bf16[32,16,128]{2,1,0:T(8,128)(2,1)S(1)}, bf16[32,16,128]{2,1,0:T(8,128)(2,1)S(1)}, u32[]{:S(2)}, u32[]{:S(2)}) collective-permute-start(bf16[32,16,128]{2,1,0:T(8,128)(2,1)S(1)} %get-tuple-element.26), channel_id=1, source_target_pairs={{0,8},{8,0},{1,9},{9,1},{2,10},{10,2},{3,11},{11,3},{4,12},{12,4},... | collective-permute-start | bytes 393224 | tf_op jit(solution)/shard_map/ppermute | solution.py:259
  30.1 12.9 %collective-permute-start.11 = (bf16[2,32,16,128]{3,2,1,0:T(8,128)(2,1)S(1)}, bf16[2,32,16,128]{3,2,1,0:T(8,128)(2,1)S(1)}, u32[]{:S(2)}, u32[]{:S(2)}) collective-permute-start(bf16[2,32,16,128]{3,2,1,0:T(8,128)(2,1)S(1)} %get-tuple-element.28), channel_id=1, source_target_pairs={{0,8},{8,0},{1,9},{9,1},{2,10},{10,2},{3,11},{11,3},{4,12},{12,4},... | collective-permute-start | bytes 786440 | tf_op jit(solution)/shard_map/ppermute | solution.py:259
  34.0 8.9 %collective-permute-start.10 = (bf16[32,16,128]{2,1,0:T(8,128)(2,1)S(1)}, bf16[32,16,128]{2,1,0:T(8,128)(2,1)S(1)}, u32[]{:S(2)}, u32[]{:S(2)}) collective-permute-start(bf16[32,16,128]{2,1,0:T(8,128)(2,1)S(1)} %shard_map.81), channel_id=1, source_target_pairs={{0,1},{1,2},{2,3},{3,4},{4,5},{5,6},{6,7},{7,0},{8,9},{9,10},{10,1... | collective-permute-start | bytes 393224 | tf_op jit(solution)/shard_map/ppermute | solution.py:259
  36.0 14.3 %collective-permute-start.13 = (bf16[2,32,16,128]{3,2,1,0:T(8,128)(2,1)S(1)}, bf16[2,32,16,128]{3,2,1,0:T(8,128)(2,1)S(1)}, u32[]{:S(2)}, u32[]{:S(2)}) collective-permute-start(bf16[2,32,16,128]{3,2,1,0:T(8,128)(2,1)S(1)} %get-tuple-element.30), channel_id=1, source_target_pairs={{0,8},{8,0},{1,9},{9,1},{2,10},{10,2},{3,11},{11,3},{4,12},{12,4},... | collective-permute-start | bytes 786440 | tf_op jit(solution)/shard_map/ppermute | solution.py:259
  43.0 7.4 %collective-permute-start.12 = (bf16[32,16,128]{2,1,0:T(8,128)(2,1)S(1)}, bf16[32,16,128]{2,1,0:T(8,128)(2,1)S(1)}, u32[]{:S(2)}, u32[]{:S(2)}) collective-permute-start(bf16[32,16,128]{2,1,0:T(8,128)(2,1)S(1)} %shard_map.82), channel_id=1, source_target_pairs={{0,1},{1,2},{2,3},{3,4},{4,5},{5,6},{6,7},{7,0},{8,9},{9,10},{10,1... | collective-permute-start | bytes 393224 | tf_op jit(solution)/shard_map/ppermute | solution.py:259
  43.1 13.9 %collective-permute-start.15 = (bf16[2,32,16,128]{3,2,1,0:T(8,128)(2,1)S(1)}, bf16[2,32,16,128]{3,2,1,0:T(8,128)(2,1)S(1)}, u32[]{:S(2)}, u32[]{:S(2)}) collective-permute-start(bf16[2,32,16,128]{3,2,1,0:T(8,128)(2,1)S(1)} %get-tuple-element.32), channel_id=1, source_target_pairs={{0,8},{8,0},{1,9},{9,1},{2,10},{10,2},{3,11},{11,3},{4,12},{12,4},... | collective-permute-start | bytes 786440 | tf_op jit(solution)/shard_map/ppermute | solution.py:259
  50.4 6.6 %collective-permute-start.14 = (bf16[32,16,128]{2,1,0:T(8,128)(2,1)S(1)}, bf16[32,16,128]{2,1,0:T(8,128)(2,1)S(1)}, u32[]{:S(2)}, u32[]{:S(2)}) collective-permute-start(bf16[32,16,128]{2,1,0:T(8,128)(2,1)S(1)} %shard_map.83), channel_id=1, source_target_pairs={{0,1},{1,2},{2,3},{3,4},{4,5},{5,6},{6,7},{7,0},{8,9},{9,10},{10,1... | collective-permute-start | bytes 393224 | tf_op jit(solution)/shard_map/ppermute | solution.py:259
  52.9 6.5 %collective-permute-start.18 = (bf16[32,16,128]{2,1,0:T(8,128)(2,1)S(1)}, bf16[32,16,128]{2,1,0:T(8,128)(2,1)S(1)}, u32[]{:S(2)}, u32[]{:S(2)}) collective-permute-start(bf16[32,16,128]{2,1,0:T(8,128)(2,1)S(1)} %shard_map.86), channel_id=1, source_target_pairs={{0,7},{1,0},{2,1},{3,2},{4,3},{5,4},{6,5},{7,6},{8,15},{9,8},{10,9... | collective-permute-start | bytes 393224 | tf_op jit(solution)/shard_map/ppermute | solution.py:259
  56.6 7.5 %collective-permute-start.20 = (bf16[32,16,128]{2,1,0:T(8,128)(2,1)S(1)}, bf16[32,16,128]{2,1,0:T(8,128)(2,1)S(1)}, u32[]{:S(2)}, u32[]{:S(2)}) collective-permute-start(bf16[32,16,128]{2,1,0:T(8,128)(2,1)S(1)} %get-tuple-element.37), channel_id=1, source_target_pairs={{0,8},{8,0},{1,9},{9,1},{2,10},{10,2},{3,11},{11,3},{4,12},{12,4},... | collective-permute-start | bytes 393224 | tf_op jit(solution)/shard_map/ppermute | solution.py:259
  57.0 7.1 %collective-permute-start.16 = (bf16[32,16,128]{2,1,0:T(8,128)(2,1)S(1)}, bf16[32,16,128]{2,1,0:T(8,128)(2,1)S(1)}, u32[]{:S(2)}, u32[]{:S(2)}) collective-permute-start(bf16[32,16,128]{2,1,0:T(8,128)(2,1)S(1)} %shard_map.84), channel_id=1, source_target_pairs={{0,1},{1,2},{2,3},{3,4},{4,5},{5,6},{6,7},{7,0},{8,9},{9,10},{10,1... | collective-permute-start | bytes 393224 | tf_op jit(solution)/shard_map/ppermute | solution.py:259
  59.5 6.3 %collective-permute-start.19 = (bf16[32,16,128]{2,1,0:T(8,128)(2,1)S(1)}, bf16[32,16,128]{2,1,0:T(8,128)(2,1)S(1)}, u32[]{:S(2)}, u32[]{:S(2)}) collective-permute-start(bf16[32,16,128]{2,1,0:T(8,128)(2,1)S(1)} %shard_map.87), channel_id=1, source_target_pairs={{0,7},{1,0},{2,1},{3,2},{4,3},{5,4},{6,5},{7,6},{8,15},{9,8},{10,9... | collective-permute-start | bytes 393224 | tf_op jit(solution)/shard_map/ppermute | solution.py:259
  68.4 7.0 %collective-permute-start.22 = (bf16[32,16,128]{2,1,0:T(8,128)(2,1)S(1)}, bf16[32,16,128]{2,1,0:T(8,128)(2,1)S(1)}, u32[]{:S(2)}, u32[]{:S(2)}) collective-permute-start(bf16[32,16,128]{2,1,0:T(8,128)(2,1)S(1)} %get-tuple-element.39.refs_0_), channel_id=1, source_target_pairs={{0,1},{1,2},{2,3},{3,4},{4,5},{5,6},{6,7},{7,0},{8,9},{9,10},{10,1... | collective-permute-start | bytes 393224 | tf_op jit(solution)/shard_map/ppermute | solution.py:259
  69.0 6.5 %collective-permute-start.23 = (bf16[32,16,128]{2,1,0:T(8,128)(2,1)S(1)}, bf16[32,16,128]{2,1,0:T(8,128)(2,1)S(1)}, u32[]{:S(2)}, u32[]{:S(2)}) collective-permute-start(bf16[32,16,128]{2,1,0:T(8,128)(2,1)S(1)} %get-tuple-element.39.refs_0_), channel_id=1, source_target_pairs={{0,7},{1,0},{2,1},{3,2},{4,3},{5,4},{6,5},{7,6},{8,15},{9,8},{10,9... | collective-permute-start | bytes 393224 | tf_op jit(solution)/shard_map/ppermute | solution.py:259
  75.5 6.2 %collective-permute-start.25 = (bf16[32,16,128]{2,1,0:T(8,128)(2,1)S(1)}, bf16[32,16,128]{2,1,0:T(8,128)(2,1)S(1)}, u32[]{:S(2)}, u32[]{:S(2)}) collective-permute-start(bf16[32,16,128]{2,1,0:T(8,128)(2,1)S(1)} %collective-permute-done.22.refs_0_.refs_2_), channel_id=1, source_target_pairs={{0,1},{1,2},{2,3},{3,4},{4,5},{5,6},{6,7},{7,0},{8,9},{9,10},{10,1... | collective-permute-start | bytes 393224 | tf_op jit(solution)/shard_map/ppermute | solution.py:259
  75.5 6.5 %collective-permute-start.26 = (bf16[32,16,128]{2,1,0:T(8,128)(2,1)S(1)}, bf16[32,16,128]{2,1,0:T(8,128)(2,1)S(1)}, u32[]{:S(2)}, u32[]{:S(2)}) collective-permute-start(bf16[32,16,128]{2,1,0:T(8,128)(2,1)S(1)} %collective-permute-done.23.refs_1_.refs_3_), channel_id=1, source_target_pairs={{0,7},{1,0},{2,1},{3,2},{4,3},{5,4},{6,5},{7,6},{8,15},{9,8},{10,9... | collective-permute-start | bytes 393224 | tf_op jit(solution)/shard_map/ppermute | solution.py:259
  81.7 7.2 %collective-permute-start.28 = (bf16[32,16,128]{2,1,0:T(8,128)(2,1)S(1)}, bf16[32,16,128]{2,1,0:T(8,128)(2,1)S(1)}, u32[]{:S(2)}, u32[]{:S(2)}) collective-permute-start(bf16[32,16,128]{2,1,0:T(8,128)(2,1)S(1)} %collective-permute-done.25.refs_0_.refs_5_), channel_id=1, source_target_pairs={{0,1},{1,2},{2,3},{3,4},{4,5},{5,6},{6,7},{7,0},{8,9},{9,10},{10,1... | collective-permute-start | bytes 393224 | tf_op jit(solution)/shard_map/ppermute | solution.py:259
  82.0 6.9 %collective-permute-start.29 = (bf16[32,16,128]{2,1,0:T(8,128)(2,1)S(1)}, bf16[32,16,128]{2,1,0:T(8,128)(2,1)S(1)}, u32[]{:S(2)}, u32[]{:S(2)}) collective-permute-start(bf16[32,16,128]{2,1,0:T(8,128)(2,1)S(1)} %collective-permute-done.26.refs_1_.refs_6_), channel_id=1, source_target_pairs={{0,7},{1,0},{2,1},{3,2},{4,3},{5,4},{6,5},{7,6},{8,15},{9,8},{10,9... | collective-permute-start | bytes 393224 | tf_op jit(solution)/shard_map/ppermute | solution.py:259
  84.9 17.6 %collective-permute-start.24 = (bf16[2,32,16,128]{3,2,1,0:T(8,128)(2,1)S(1)}, bf16[2,32,16,128]{3,2,1,0:T(8,128)(2,1)S(1)}, u32[]{:S(2)}, u32[]{:S(2)}) collective-permute-start(bf16[2,32,16,128]{3,2,1,0:T(8,128)(2,1)S(1)} %shard_map.89), channel_id=1, source_target_pairs={{0,8},{8,0},{1,9},{9,1},{2,10},{10,2},{3,11},{11,3},{4,12},{12,4},... | collective-permute-start | bytes 786440 | tf_op jit(solution)/shard_map/ppermute | solution.py:259
  85.7 16.8 %collective-permute-start.27 = (bf16[2,32,16,128]{3,2,1,0:T(8,128)(2,1)S(1)}, bf16[2,32,16,128]{3,2,1,0:T(8,128)(2,1)S(1)}, u32[]{:S(2)}, u32[]{:S(2)}) collective-permute-start(bf16[2,32,16,128]{3,2,1,0:T(8,128)(2,1)S(1)} %shard_map.90), channel_id=1, source_target_pairs={{0,8},{8,0},{1,9},{9,1},{2,10},{10,2},{3,11},{11,3},{4,12},{12,4},... | collective-permute-start | bytes 786440 | tf_op jit(solution)/shard_map/ppermute | solution.py:259
  88.9 6.2 %collective-permute-start.31 = (bf16[32,16,128]{2,1,0:T(8,128)(2,1)S(1)}, bf16[32,16,128]{2,1,0:T(8,128)(2,1)S(1)}, u32[]{:S(2)}, u32[]{:S(2)}) collective-permute-start(bf16[32,16,128]{2,1,0:T(8,128)(2,1)S(1)} %collective-permute-done.28.refs_0_.refs_8_), channel_id=1, source_target_pairs={{0,1},{1,2},{2,3},{3,4},{4,5},{5,6},{6,7},{7,0},{8,9},{9,10},{10,1... | collective-permute-start | bytes 393224 | tf_op jit(solution)/shard_map/ppermute | solution.py:259
  88.9 13.6 %collective-permute-start.30 = (bf16[2,32,16,128]{3,2,1,0:T(8,128)(2,1)S(1)}, bf16[2,32,16,128]{3,2,1,0:T(8,128)(2,1)S(1)}, u32[]{:S(2)}, u32[]{:S(2)}) collective-permute-start(bf16[2,32,16,128]{3,2,1,0:T(8,128)(2,1)S(1)} %shard_map.91), channel_id=1, source_target_pairs={{0,8},{8,0},{1,9},{9,1},{2,10},{10,2},{3,11},{11,3},{4,12},{12,4},... | collective-permute-start | bytes 786440 | tf_op jit(solution)/shard_map/ppermute | solution.py:259
  89.7 12.8 %collective-permute-start.21 = (bf16[32,16,128]{2,1,0:T(8,128)(2,1)S(1)}, bf16[32,16,128]{2,1,0:T(8,128)(2,1)S(1)}, u32[]{:S(2)}, u32[]{:S(2)}) collective-permute-start(bf16[32,16,128]{2,1,0:T(8,128)(2,1)S(1)} %get-tuple-element.39.refs_0_), channel_id=1, source_target_pairs={{0,8},{8,0},{1,9},{9,1},{2,10},{10,2},{3,11},{11,3},{4,12},{12,4},... | collective-permute-start | bytes 393224 | tf_op jit(solution)/shard_map/ppermute | solution.py:259
  95.0 8.8 %collective-permute-start.32 = (bf16[32,16,128]{2,1,0:T(8,128)(2,1)S(1)}, bf16[32,16,128]{2,1,0:T(8,128)(2,1)S(1)}, u32[]{:S(2)}, u32[]{:S(2)}) collective-permute-start(bf16[32,16,128]{2,1,0:T(8,128)(2,1)S(1)} %collective-permute-done.31.refs_11_), channel_id=1, source_target_pairs={{0,8},{8,0},{1,9},{9,1},{2,10},{10,2},{3,11},{11,3},{4,12},{12,4},... | collective-permute-start | bytes 393224 | tf_op jit(solution)/shard_map/ppermute | solution.py:259
  111.2 5.6 %collective-permute-start.34 = (bf16[32,16,128]{2,1,0:T(8,128)(2,1)S(1)}, bf16[32,16,128]{2,1,0:T(8,128)(2,1)S(1)}, u32[]{:S(2)}, u32[]{:S(2)}) collective-permute-start(bf16[32,16,128]{2,1,0:T(8,128)(2,1)S(1)} %get-tuple-element.42), channel_id=1, source_target_pairs={{0,32},{32,64},{64,96},{96,0},{1,33},{33,65},{65,97},{97,1},{2,34}... | collective-permute-start | bytes 393224 | tf_op jit(solution)/shard_map/ppermute | solution.py:259
  111.2 6.8 %collective-permute-start.35 = (bf16[32,16,128]{2,1,0:T(8,128)(2,1)S(1)}, bf16[32,16,128]{2,1,0:T(8,128)(2,1)S(1)}, u32[]{:S(2)}, u32[]{:S(2)}) collective-permute-start(bf16[32,16,128]{2,1,0:T(8,128)(2,1)S(1)} %get-tuple-element.43), channel_id=1, source_target_pairs={{0,96},{32,0},{64,32},{96,64},{1,97},{33,1},{65,33},{97,65},{2,98}... | collective-permute-start | bytes 393224 | tf_op jit(solution)/shard_map/ppermute | solution.py:259
  118.2 7.6 %collective-permute-start.36 = (bf16[2,32,16,128]{3,2,1,0:T(8,128)(2,1)S(1)}, bf16[2,32,16,128]{3,2,1,0:T(8,128)(2,1)S(1)}, u32[]{:S(2)}, u32[]{:S(2)}) collective-permute-start(bf16[2,32,16,128]{3,2,1,0:T(8,128)(2,1)S(1)} %get-tuple-element.44), channel_id=1, source_target_pairs={{0,32},{32,64},{64,96},{96,0},{1,33},{33,65},{65,97},{97,1},{2,34}... | collective-permute-start | bytes 786440 | tf_op jit(solution)/shard_map/ppermute | solution.py:259
  118.5 8.7 %collective-permute-start.37 = (bf16[2,32,16,128]{3,2,1,0:T(8,128)(2,1)S(1)}, bf16[2,32,16,128]{3,2,1,0:T(8,128)(2,1)S(1)}, u32[]{:S(2)}, u32[]{:S(2)}) collective-permute-start(bf16[2,32,16,128]{3,2,1,0:T(8,128)(2,1)S(1)} %get-tuple-element.45), channel_id=1, source_target_pairs={{0,96},{32,0},{64,32},{96,64},{1,97},{33,1},{65,33},{97,65},{2,98}... | collective-permute-start | bytes 786440 | tf_op jit(solution)/shard_map/ppermute | solution.py:259
  (11 other events, 194.9 us)

commit v3 on v2

--- a/solution.py
+++ b/solution.py
@@ -105,7 +105,7 @@
 
 def middle_body(forward, inverse, onset, plus, minus, share, far, upgoing, out, total, buf):
     ring = plus[...].astype(F32) + minus[...].astype(F32)
-    total[...] = ring + (share[...] + far[...].astype(F32))
+    total[...] = ring + (share[...] + far[1].astype(F32))
     points, width, samples = upgoing.shape
     time = lax.broadcasted_iota(jnp.int32, (points, samples), 1)
     for n in range(width):
@@ -116,14 +116,44 @@
     out[...] = buf[...].astype(BF16)
 
 
-def last_body(inverse, onset, first, kept, taken, downgoing, total):
+def last_body(inverse, onset, first, kept, taken, out_hbm, downgoing, total, sent):
     total[...] = kept[...] + taken[...].astype(F32)
     points, width, samples = downgoing.shape
+    half = width // 2
     time = lax.broadcasted_iota(jnp.int32, (points, samples), 1)
+    stores = []
     for n in range(width):
         trace = from_spec(total[:, n, :], inverse[...])
         trace = jnp.where(time < onset[:, n : n + 1], trace, 0.0)
         downgoing[:, n, :] = first[:, n, :] - trace
+        if n % half == half - 1:
+            part = pl.ds(n + 1 - half, half)
+            stores.append(
+                pltpu.make_async_copy(
+                    downgoing.at[:, part], out_hbm.at[:, part], sent.at[n // half]
+                )
+            )
+            stores[-1].start()
+    for store in stores:
+        store.wait()
+
+
+def last(*args):
+    vmem = pl.BlockSpec(memory_space=pltpu.VMEM)
+    shape, spectrum = args[2].shape, args[3].shape
+    return pl.pallas_call(
+        last_body,
+        in_specs=[vmem] * len(args),
+        out_specs=pl.BlockSpec(memory_space=pltpu.HBM),
+        out_shape=pltpu.HBM(shape, F32),
+        scratch_shapes=[
+            pltpu.VMEM(shape, F32),
+            pltpu.VMEM(spectrum, F32),
+            pltpu.SemaphoreType.DMA((2,)),
+        ],
+        compiler_params=pltpu.CompilerParams(vmem_limit_bytes=4 << 20),
+        name="last",
+    )(*[pltpu.with_memory_space_constraint(arg, pltpu.VMEM) for arg in args])
 
 
 def cross(direct, turned, sign):
@@ -226,10 +256,6 @@
 
 def hop_body(taken, share, far, out, *, at):
     out[...] = (taken[...].astype(F32) + share[...] + far[at].astype(F32)).astype(BF16)
-
-
-def first_body(share, far, out, *, at):
-    out[...] = (share[...] + far[at].astype(F32)).astype(BF16)
 
 
 def held(stay, taken, s, b):
@@ -303,15 +329,14 @@
             kernel,
         )
 
-    slots = [(4,), (3, 5), (2, 6), (1, 7), (0,)]
+    slots = [(4,), (5,), (3, 6), (2, 7), (1, 0)]
     far = [move(value, "yh", 1) for value in conv(1, slots, BF16)]
     share = conv(0, [(dz,) for dz in range(NZ)], F32)
     (plus,) = local(join_body, [(one, BF16)], [share[4], far[0]])
     plus = move(plus, "z", 1)
-    first = functools.partial(first_body, at=1)
-    (minus,) = local(first, [(one, BF16)], [share[5], far[1]])
+    (minus,) = local(join_body, [(one, BF16)], [share[5], far[1]])
     minus = move(minus, "z", -1)
-    for dz, group, at in ((3, 1, 0), (2, 2, 0), (1, 3, 0)):
+    for dz, group, at in ((3, 2, 0), (2, 3, 0), (1, 4, 0)):
         body = functools.partial(hop_body, at=at)
         (plus,) = local(body, [(one, BF16)], [plus, share[dz], far[group]])
         plus = move(plus, "z", 1)
@@ -351,12 +376,8 @@
     plus, minus = local(turn_x_body, [(two, BF16)] * 2, [plus, minus, stay, taken])
     plus, minus = move(plus, "x", 1), move(minus, "x", -1)
     send, keep = local(meet_x_body, [(one, BF16), (one, F32)], [plus, minus, stay, taken])
-    (downgoing,) = local(
-        last_body,
-        [(focusing.shape, F32)],
-        [rinverse, limits_down, first_arrival, keep, move(send, "yl", 1)],
-        [buf],
-    )
+    taken = move(send, "yl", 1)
+    downgoing = last(rinverse, limits_down, first_arrival, keep, taken)
     return upgoing, downgoing
 
 

time: 135 us -> 138 us (1.022)
  starting transfers between devices: 56 us -> 59.5 us
    ppermute x39, starting transfers between devices: 56 us -> 59.5 us  [move(): lax.ppermute(value, axis, [(i, (i + step) % size) for i in range(size)])]
    pallas_call x0 -> x1, Pallas kernels: none -> 1.97 us  [last(): pl.pallas_call(last_body, in_specs=[vmem] * len(args), out_specs=pl.Block...]
    pallas_call x20 -> x19, Pallas kernels: 15.5 us -> 14.3 us  [local(): pl.pallas_call(body, in_specs=[pl.BlockSpec(memory_space=pltpu.HBM)] * le...]
  transfers between devices with their start and end apart: 39 -> 39, of which waited for: 22 -> 20; matrix products, arithmetic and copies ran while one was open for 1% -> 1% of each run, Pallas kernels for 3% -> 3%
where the time goes in v3:
time: 138 us
  starting transfers between devices  59.5 us (43%)
  waiting for transfers between devices  57 us (41%)
  Pallas kernels  18.6 us (13%)
  local copies, waits for them, and re-layouts  1.68 us (1%)
    ppermute x39, starting transfers between devices, move(): lax.ppermute(value, axis, [(i, (i + step) % size) for i in range(size)])  59.5 us
    ppermute x39, waiting for transfers between devices, move(): lax.ppermute(value, axis, [(i, (i + step) % size) for i in range(size)])  57 us
    pallas_call x19, Pallas kernels, local(): pl.pallas_call(body, in_specs=[pl.BlockSpec(memory_space=pltpu.HBM)] * le...  14.3 us
  transfers between devices with their start and end apart: 39, of which 20 were waited for; matrix products, arithmetic and copies ran while one was open for 1% of the time, Pallas kernels for 3%

profile of v3, /device:TPU:6, one launch (start us, length us, event | category | flops | bytes accessed | tf_op | source)
XLA Modules:
  0.0 137.8 jit_solution(7874553755888545488)
XLA Ops:
  0.6 2.3 %spectra.1.refs_0_ = bf16[32,16,128]{2,1,0:T(8,128)(2,1)S(1)} custom-call(f32[64,128]{1,0:T(8,128)} %constant.46.clone.forward_hbm.forward, f32[64,16,128]{2,1,0:T(8,128)} %traces_hbm.1), custom_call_target="tpu_custom_call" | custom-call | tf_op jit(solution)/shard_map/spectra/pallas_call | solution.py:90
  5.3 3.0 %collective-permute-done.2.refs_1_.refs_3_ = bf16[32,16,128]{2,1,0:T(8,128)(2,1)S(1)} collective-permute-done((bf16[32,16,128]{2,1,0:T(8,128)(2,1)S(1)}, bf16[32,16,128]{2,1,0:T(8,128)(2,1)S(1)}, u32[]{:S(2)}, u32[]{:S(2)}) %collective-permute-start.2) | collective-permute-done | bytes 131104 | tf_op jit(solution)/shard_map/ppermute | solution.py:285
  9.6 2.7 %collective-permute-start.5 = (bf16[32,16,128]{2,1,0:T(8,128)(2,1)S(1)}, bf16[32,16,128]{2,1,0:T(8,128)(2,1)S(1)}, u32[]{:S(2)}, u32[]{:S(2)}) collective-permute-start(bf16[32,16,128]{2,1,0:T(8,128)(2,1)S(1)} %collective-permute-done.2.refs_1_.refs_3_), channel_id=1, source_target_pairs={{0,32},{32,64},{64,96},{96,0},{1,33},{33,65},{65,97},{97,1},{2,34}... | collective-permute-start | bytes 393224 | tf_op jit(solution)/shard_map/ppermute | solution.py:285
  17.4 4.0 %collective-permute-done.6.refs_3_.refs_7_ = bf16[32,16,128]{2,1,0:T(8,128)(2,1)S(1)} collective-permute-done((bf16[32,16,128]{2,1,0:T(8,128)(2,1)S(1)}, bf16[32,16,128]{2,1,0:T(8,128)(2,1)S(1)}, u32[]{:S(2)}, u32[]{:S(2)}) %collective-permute-start.6) | collective-permute-done | bytes 131104 | tf_op jit(solution)/shard_map/ppermute | solution.py:285
  23.5 3.3 %shard_map.80 = (bf16[32,16,128]{2,1,0:T(8,128)(2,1)S(1)}, bf16[32,16,128]{2,1,0:T(8,128)(2,1)S(1)}, bf16[2,32,16,128]{3,2,1,0:T(8,128)(2,1)S(1)}, bf16[2,32,16,...) custom-call(bf16[2,32,256,256]{3,2,1,0:T(8,128)(2,1)} %source.5, bf16[32,16,128]{2,1,0:T(8,128)(2,1)S(1)} %spectra.1.refs_0_, ...), custom_call_target="tpu_custom_call" | custom-call | tf_op jit(solution)/shard_map/pallas_call | solution.py:33
  26.8 3.3 %collective-permute-start.9 = (bf16[32,16,128]{2,1,0:T(8,128)(2,1)S(1)}, bf16[32,16,128]{2,1,0:T(8,128)(2,1)S(1)}, u32[]{:S(2)}, u32[]{:S(2)}) collective-permute-start(bf16[32,16,128]{2,1,0:T(8,128)(2,1)S(1)} %get-tuple-element.26), channel_id=1, source_target_pairs={{0,8},{8,0},{1,9},{9,1},{2,10},{10,2},{3,11},{11,3},{4,12},{12,4},... | collective-permute-start | bytes 393224 | tf_op jit(solution)/shard_map/ppermute | solution.py:285
  30.4 3.2 %collective-permute-start.17 = (bf16[32,16,128]{2,1,0:T(8,128)(2,1)S(1)}, bf16[32,16,128]{2,1,0:T(8,128)(2,1)S(1)}, u32[]{:S(2)}, u32[]{:S(2)}) collective-permute-start(bf16[32,16,128]{2,1,0:T(8,128)(2,1)S(1)} %get-tuple-element.34), channel_id=1, source_target_pairs={{0,8},{8,0},{1,9},{9,1},{2,10},{10,2},{3,11},{11,3},{4,12},{12,4},... | collective-permute-start | bytes 393224 | tf_op jit(solution)/shard_map/ppermute | solution.py:285
  33.6 3.3 %shard_map.79 = (f32[32,16,128]{2,1,0:T(8,128)S(1)}, f32[32,16,128]{2,1,0:T(8,128)S(1)}, f32[32,16,128]{2,1,0:T(8,128)S(1)}, f32[32,16,128]{2,1,0:T(8,128)S(1)},...) custom-call(bf16[2,32,256,256]{3,2,1,0:T(8,128)(2,1)} %source.5, ...), custom_call_target="tpu_custom_call" | custom-call | tf_op jit(solution)/shard_map/pallas_call | solution.py:33
  40.0 2.9 %collective-permute-done.17.far = bf16[32,16,128]{2,1,0:T(8,128)(2,1)S(1)} collective-permute-done((bf16[32,16,128]{2,1,0:T(8,128)(2,1)S(1)}, bf16[32,16,128]{2,1,0:T(8,128)(2,1)S(1)}, u32[]{:S(2)}, u32[]{:S(2)}) %collective-permute-start.17) | collective-permute-done | bytes 131104 | tf_op jit(solution)/shard_map/ppermute | solution.py:285
  42.9 6.8 %collective-permute-start.18 = (bf16[32,16,128]{2,1,0:T(8,128)(2,1)S(1)}, bf16[32,16,128]{2,1,0:T(8,128)(2,1)S(1)}, u32[]{:S(2)}, u32[]{:S(2)}) collective-permute-start(bf16[32,16,128]{2,1,0:T(8,128)(2,1)S(1)} %shard_map.85), channel_id=1, source_target_pairs={{0,7},{1,0},{2,1},{3,2},{4,3},{5,4},{6,5},{7,6},{8,15},{9,8},{10,9... | collective-permute-start | bytes 393224 | tf_op jit(solution)/shard_map/ppermute | solution.py:285
  49.8 2.9 %collective-permute-start.15 = (bf16[2,32,16,128]{3,2,1,0:T(8,128)(2,1)S(1)}, bf16[2,32,16,128]{3,2,1,0:T(8,128)(2,1)S(1)}, u32[]{:S(2)}, u32[]{:S(2)}) collective-permute-start(bf16[2,32,16,128]{3,2,1,0:T(8,128)(2,1)S(1)} %get-tuple-element.32), channel_id=1, source_target_pairs={{0,8},{8,0},{1,9},{9,1},{2,10},{10,2},{3,11},{11,3},{4,12},{12,4},... | collective-permute-start | bytes 786440 | tf_op jit(solution)/shard_map/ppermute | solution.py:285
  52.8 3.2 %collective-permute-start.19 = (bf16[32,16,128]{2,1,0:T(8,128)(2,1)S(1)}, bf16[32,16,128]{2,1,0:T(8,128)(2,1)S(1)}, u32[]{:S(2)}, u32[]{:S(2)}) collective-permute-start(bf16[32,16,128]{2,1,0:T(8,128)(2,1)S(1)} %shard_map.86), channel_id=1, source_target_pairs={{0,7},{1,0},{2,1},{3,2},{4,3},{5,4},{6,5},{7,6},{8,15},{9,8},{10,9... | collective-permute-start | bytes 393224 | tf_op jit(solution)/shard_map/ppermute | solution.py:285
  56.1 2.4 %collective-permute-done.19.taken = bf16[32,16,128]{2,1,0:T(8,128)(2,1)S(1)} collective-permute-done((bf16[32,16,128]{2,1,0:T(8,128)(2,1)S(1)}, bf16[32,16,128]{2,1,0:T(8,128)(2,1)S(1)}, u32[]{:S(2)}, u32[]{:S(2)}) %collective-permute-start.19) | collective-permute-done | bytes 131104 | tf_op jit(solution)/shard_map/ppermute | solution.py:285
  58.6 3.7 %collective-permute-start.20 = (bf16[32,16,128]{2,1,0:T(8,128)(2,1)S(1)}, bf16[32,16,128]{2,1,0:T(8,128)(2,1)S(1)}, u32[]{:S(2)}, u32[]{:S(2)}) collective-permute-start(bf16[32,16,128]{2,1,0:T(8,128)(2,1)S(1)} %shard_map.87), channel_id=1, source_target_pairs={{0,7},{1,0},{2,1},{3,2},{4,3},{5,4},{6,5},{7,6},{8,15},{9,8},{10,9... | collective-permute-start | bytes 393224 | tf_op jit(solution)/shard_map/ppermute | solution.py:285
  64.8 3.8 %collective-permute-done.16.plus = bf16[32,16,128]{2,1,0:T(8,128)(2,1)S(1)} collective-permute-done((bf16[32,16,128]{2,1,0:T(8,128)(2,1)S(1)}, bf16[32,16,128]{2,1,0:T(8,128)(2,1)S(1)}, u32[]{:S(2)}, u32[]{:S(2)}) %collective-permute-start.16) | collective-permute-done | bytes 131104 | tf_op jit(solution)/shard_map/ppermute | solution.py:285
  68.6 2.7 %shard_map.88 = (f32[64,16,128]{2,1,0:T(8,128)S(1)}, bf16[32,16,128]{2,1,0:T(8,128)(2,1)S(1)}) custom-call(f32[64,128]{1,0:T(8,128)S(1)} %copy-done.1, f32[64,128]{1,0:T(8,128)S(1)} %copy-done.2, s32[64,16]{1,0:T(8,128)S(1)} %get-tuple-element.49.onset, bf16[32,16,128]{2,1,0:T(8,128)(2,1)S(1)} %collective-permute-done.16.plus, ...), custom_call_target="tpu_custom_call" | custom-call | tf_op jit(solution)/shard_map/pallas_call | solution.py:33
  71.4 3.2 %collective-permute-start.23 = (bf16[32,16,128]{2,1,0:T(8,128)(2,1)S(1)}, bf16[32,16,128]{2,1,0:T(8,128)(2,1)S(1)}, u32[]{:S(2)}, u32[]{:S(2)}) collective-permute-start(bf16[32,16,128]{2,1,0:T(8,128)(2,1)S(1)} %get-tuple-element.39.refs_0_), channel_id=1, source_target_pairs={{0,7},{1,0},{2,1},{3,2},{4,3},{5,4},{6,5},{7,6},{8,15},{9,8},{10,9... | collective-permute-start | bytes 393224 | tf_op jit(solution)/shard_map/ppermute | solution.py:285
  74.6 3.7 %collective-permute-done.22.refs_0_.refs_2_ = bf16[32,16,128]{2,1,0:T(8,128)(2,1)S(1)} collective-permute-done((bf16[32,16,128]{2,1,0:T(8,128)(2,1)S(1)}, bf16[32,16,128]{2,1,0:T(8,128)(2,1)S(1)}, u32[]{:S(2)}, u32[]{:S(2)}) %collective-permute-start.22) | collective-permute-done | bytes 131104 | tf_op jit(solution)/shard_map/ppermute | solution.py:285
  78.3 3.2 %collective-permute-start.26 = (bf16[32,16,128]{2,1,0:T(8,128)(2,1)S(1)}, bf16[32,16,128]{2,1,0:T(8,128)(2,1)S(1)}, u32[]{:S(2)}, u32[]{:S(2)}) collective-permute-start(bf16[32,16,128]{2,1,0:T(8,128)(2,1)S(1)} %collective-permute-done.23.refs_1_.refs_3_), channel_id=1, source_target_pairs={{0,7},{1,0},{2,1},{3,2},{4,3},{5,4},{6,5},{7,6},{8,15},{9,8},{10,9... | collective-permute-start | bytes 393224 | tf_op jit(solution)/shard_map/ppermute | solution.py:285
  81.6 2.9 %collective-permute-done.25.refs_0_.refs_5_ = bf16[32,16,128]{2,1,0:T(8,128)(2,1)S(1)} collective-permute-done((bf16[32,16,128]{2,1,0:T(8,128)(2,1)S(1)}, bf16[32,16,128]{2,1,0:T(8,128)(2,1)S(1)}, u32[]{:S(2)}, u32[]{:S(2)}) %collective-permute-start.25) | collective-permute-done | bytes 131104 | tf_op jit(solution)/shard_map/ppermute | solution.py:285
  84.5 3.2 %collective-permute-start.29 = (bf16[32,16,128]{2,1,0:T(8,128)(2,1)S(1)}, bf16[32,16,128]{2,1,0:T(8,128)(2,1)S(1)}, u32[]{:S(2)}, u32[]{:S(2)}) collective-permute-start(bf16[32,16,128]{2,1,0:T(8,128)(2,1)S(1)} %collective-permute-done.26.refs_1_.refs_6_), channel_id=1, source_target_pairs={{0,7},{1,0},{2,1},{3,2},{4,3},{5,4},{6,5},{7,6},{8,15},{9,8},{10,9... | collective-permute-start | bytes 393224 | tf_op jit(solution)/shard_map/ppermute | solution.py:285
  87.8 2.6 %collective-permute-start.24 = (bf16[2,32,16,128]{3,2,1,0:T(8,128)(2,1)S(1)}, bf16[2,32,16,128]{3,2,1,0:T(8,128)(2,1)S(1)}, u32[]{:S(2)}, u32[]{:S(2)}) collective-permute-start(bf16[2,32,16,128]{3,2,1,0:T(8,128)(2,1)S(1)} %shard_map.89), channel_id=1, source_target_pairs={{0,8},{8,0},{1,9},{9,1},{2,10},{10,2},{3,11},{11,3},{4,12},{12,4},... | collective-permute-start | bytes 786440 | tf_op jit(solution)/shard_map/ppermute | solution.py:285
  91.8 2.6 %collective-permute-start.30 = (bf16[2,32,16,128]{3,2,1,0:T(8,128)(2,1)S(1)}, bf16[2,32,16,128]{3,2,1,0:T(8,128)(2,1)S(1)}, u32[]{:S(2)}, u32[]{:S(2)}) collective-permute-start(bf16[2,32,16,128]{3,2,1,0:T(8,128)(2,1)S(1)} %shard_map.91), channel_id=1, source_target_pairs={{0,8},{8,0},{1,9},{9,1},{2,10},{10,2},{3,11},{11,3},{4,12},{12,4},... | collective-permute-start | bytes 786440 | tf_op jit(solution)/shard_map/ppermute | solution.py:285
  95.4 2.5 %collective-permute-done.31.refs_11_ = bf16[32,16,128]{2,1,0:T(8,128)(2,1)S(1)} collective-permute-done((bf16[32,16,128]{2,1,0:T(8,128)(2,1)S(1)}, bf16[32,16,128]{2,1,0:T(8,128)(2,1)S(1)}, u32[]{:S(2)}, u32[]{:S(2)}) %collective-permute-start.31) | collective-permute-done | bytes 131104 | tf_op jit(solution)/shard_map/ppermute | solution.py:285
  97.9 2.5 %collective-permute-start.32 = (bf16[32,16,128]{2,1,0:T(8,128)(2,1)S(1)}, bf16[32,16,128]{2,1,0:T(8,128)(2,1)S(1)}, u32[]{:S(2)}, u32[]{:S(2)}) collective-permute-start(bf16[32,16,128]{2,1,0:T(8,128)(2,1)S(1)} %collective-permute-done.31.refs_11_), channel_id=1, source_target_pairs={{0,8},{8,0},{1,9},{9,1},{2,10},{10,2},{3,11},{11,3},{4,12},{12,4},... | collective-permute-start | bytes 393224 | tf_op jit(solution)/shard_map/ppermute | solution.py:285
  100.4 5.4 %collective-permute-done.21.refs_1_ = bf16[32,16,128]{2,1,0:T(8,128)(2,1)S(1)} collective-permute-done((bf16[32,16,128]{2,1,0:T(8,128)(2,1)S(1)}, bf16[32,16,128]{2,1,0:T(8,128)(2,1)S(1)}, u32[]{:S(2)}, u32[]{:S(2)}) %collective-permute-start.21) | collective-permute-done | bytes 131104 | tf_op jit(solution)/shard_map/ppermute | solution.py:285
  107.2 4.5 %shard_map.92 = (bf16[8,32,16,128]{3,2,1,0:T(8,128)(2,1)S(1)}, f32[8,32,16,128]{3,2,1,0:T(8,128)S(1)}) custom-call(bf16[2,32,256,256]{3,2,1,0:T(8,128)(2,1)} %source.5, bf16[32,16,128]{2,1,0:T(8,128)(2,1)S(1)} %get-tuple-element.39.refs_0_, bf16[32,16,128]{2,1,0:T(8,128)(2,1)S(1)} %collective-permute-done.21.refs_1_, ...), custom_call_target="tpu_custom_call" | custom-call | tf_op jit(solution)/shard_map/pallas_call | solution.py:33
  111.7 2.6 %collective-permute-done.33.taken = bf16[8,32,16,128]{3,2,1,0:T(8,128)(2,1)S(1)} collective-permute-done((bf16[8,32,16,128]{3,2,1,0:T(8,128)(2,1)S(1)}, bf16[8,32,16,128]{3,2,1,0:T(8,128)(2,1)S(1)}, u32[]{:S(2)}, u32[]{:S(2)}) %collective-permute-start.33) | collective-permute-done | bytes 1048608 | tf_op jit(solution)/shard_map/ppermute | solution.py:285
  114.5 2.0 %collective-permute-start.35 = (bf16[32,16,128]{2,1,0:T(8,128)(2,1)S(1)}, bf16[32,16,128]{2,1,0:T(8,128)(2,1)S(1)}, u32[]{:S(2)}, u32[]{:S(2)}) collective-permute-start(bf16[32,16,128]{2,1,0:T(8,128)(2,1)S(1)} %get-tuple-element.43), channel_id=1, source_target_pairs={{0,96},{32,0},{64,32},{96,64},{1,97},{33,1},{65,33},{97,65},{2,98}... | collective-permute-start | bytes 393224 | tf_op jit(solution)/shard_map/ppermute | solution.py:285
  116.5 3.5 %collective-permute-done.34.plus = bf16[32,16,128]{2,1,0:T(8,128)(2,1)S(1)} collective-permute-done((bf16[32,16,128]{2,1,0:T(8,128)(2,1)S(1)}, bf16[32,16,128]{2,1,0:T(8,128)(2,1)S(1)}, u32[]{:S(2)}, u32[]{:S(2)}) %collective-permute-start.34) | collective-permute-done | bytes 131104 | tf_op jit(solution)/shard_map/ppermute | solution.py:285
  123.6 5.5 %collective-permute-done.36.plus = bf16[2,32,16,128]{3,2,1,0:T(8,128)(2,1)S(1)} collective-permute-done((bf16[2,32,16,128]{3,2,1,0:T(8,128)(2,1)S(1)}, bf16[2,32,16,128]{3,2,1,0:T(8,128)(2,1)S(1)}, u32[]{:S(2)}, u32[]{:S(2)}) %collective-permute-start.36) | collective-permute-done | bytes 262176 | tf_op jit(solution)/shard_map/ppermute | solution.py:285
  132.2 3.5 %collective-permute-done.38.taken = bf16[32,16,128]{2,1,0:T(8,128)(2,1)S(1)} collective-permute-done((bf16[32,16,128]{2,1,0:T(8,128)(2,1)S(1)}, bf16[32,16,128]{2,1,0:T(8,128)(2,1)S(1)}, u32[]{:S(2)}, u32[]{:S(2)}) %collective-permute-start.38) | collective-permute-done | bytes 131104 | tf_op jit(solution)/shard_map/ppermute | solution.py:285
  (77 shorter events, 29.9 us)
Async XLA Ops:
  4.6 7.7 %collective-permute-start = (bf16[32,16,128]{2,1,0:T(8,128)(2,1)S(1)}, bf16[32,16,128]{2,1,0:T(8,128)(2,1)S(1)}, u32[]{:S(2)}, u32[]{:S(2)}) collective-permute-start(bf16[32,16,128]{2,1,0:T(8,128)(2,1)S(1)} %spectra.1.refs_0_), channel_id=1, source_target_pairs={{0,32},{32,64},{64,96},{96,0},{1,33},{33,65},{65,97},{97,1},{2,34}... | collective-permute-start | bytes 393224 | tf_op jit(solution)/shard_map/ppermute | solution.py:285
  8.3 7.0 %collective-permute-start.4 = (bf16[32,16,128]{2,1,0:T(8,128)(2,1)S(1)}, bf16[32,16,128]{2,1,0:T(8,128)(2,1)S(1)}, u32[]{:S(2)}, u32[]{:S(2)}) collective-permute-start(bf16[32,16,128]{2,1,0:T(8,128)(2,1)S(1)} %collective-permute-done.2.refs_1_.refs_3_), channel_id=1, source_target_pairs={{0,96},{32,0},{64,32},{96,64},{1,97},{33,1},{65,33},{97,65},{2,98}... | collective-permute-start | bytes 393224 | tf_op jit(solution)/shard_map/ppermute | solution.py:285
  9.1 8.2 %collective-permute-start.1 = (bf16[32,16,128]{2,1,0:T(8,128)(2,1)S(1)}, bf16[32,16,128]{2,1,0:T(8,128)(2,1)S(1)}, u32[]{:S(2)}, u32[]{:S(2)}) collective-permute-start(bf16[32,16,128]{2,1,0:T(8,128)(2,1)S(1)} %spectra.1.refs_0_), channel_id=1, source_target_pairs={{0,96},{32,0},{64,32},{96,64},{1,97},{33,1},{65,33},{97,65},{2,98}... | collective-permute-start | bytes 393224 | tf_op jit(solution)/shard_map/ppermute | solution.py:285
  9.6 7.8 %collective-permute-start.5 = (bf16[32,16,128]{2,1,0:T(8,128)(2,1)S(1)}, bf16[32,16,128]{2,1,0:T(8,128)(2,1)S(1)}, u32[]{:S(2)}, u32[]{:S(2)}) collective-permute-start(bf16[32,16,128]{2,1,0:T(8,128)(2,1)S(1)} %collective-permute-done.2.refs_1_.refs_3_), channel_id=1, source_target_pairs={{0,32},{32,64},{64,96},{96,0},{1,33},{33,65},{65,97},{97,1},{2,34}... | collective-permute-start | bytes 393224 | tf_op jit(solution)/shard_map/ppermute | solution.py:285
  15.3 6.2 %collective-permute-start.6 = (bf16[32,16,128]{2,1,0:T(8,128)(2,1)S(1)}, bf16[32,16,128]{2,1,0:T(8,128)(2,1)S(1)}, u32[]{:S(2)}, u32[]{:S(2)}) collective-permute-start(bf16[32,16,128]{2,1,0:T(8,128)(2,1)S(1)} %collective-permute-done.4.refs_0_.refs_5_), channel_id=1, source_target_pairs={{0,96},{32,0},{64,32},{96,64},{1,97},{33,1},{65,33},{97,65},{2,98}... | collective-permute-start | bytes 393224 | tf_op jit(solution)/shard_map/ppermute | solution.py:285
  26.8 10.1 %collective-permute-start.9 = (bf16[32,16,128]{2,1,0:T(8,128)(2,1)S(1)}, bf16[32,16,128]{2,1,0:T(8,128)(2,1)S(1)}, u32[]{:S(2)}, u32[]{:S(2)}) collective-permute-start(bf16[32,16,128]{2,1,0:T(8,128)(2,1)S(1)} %get-tuple-element.26), channel_id=1, source_target_pairs={{0,8},{8,0},{1,9},{9,1},{2,10},{10,2},{3,11},{11,3},{4,12},{12,4},... | collective-permute-start | bytes 393224 | tf_op jit(solution)/shard_map/ppermute | solution.py:285
  30.1 19.6 %collective-permute-start.11 = (bf16[2,32,16,128]{3,2,1,0:T(8,128)(2,1)S(1)}, bf16[2,32,16,128]{3,2,1,0:T(8,128)(2,1)S(1)}, u32[]{:S(2)}, u32[]{:S(2)}) collective-permute-start(bf16[2,32,16,128]{3,2,1,0:T(8,128)(2,1)S(1)} %get-tuple-element.28), channel_id=1, source_target_pairs={{0,8},{8,0},{1,9},{9,1},{2,10},{10,2},{3,11},{11,3},{4,12},{12,4},... | collective-permute-start | bytes 786440 | tf_op jit(solution)/shard_map/ppermute | solution.py:285
  30.4 12.5 %collective-permute-start.17 = (bf16[32,16,128]{2,1,0:T(8,128)(2,1)S(1)}, bf16[32,16,128]{2,1,0:T(8,128)(2,1)S(1)}, u32[]{:S(2)}, u32[]{:S(2)}) collective-permute-start(bf16[32,16,128]{2,1,0:T(8,128)(2,1)S(1)} %get-tuple-element.34), channel_id=1, source_target_pairs={{0,8},{8,0},{1,9},{9,1},{2,10},{10,2},{3,11},{11,3},{4,12},{12,4},... | collective-permute-start | bytes 393224 | tf_op jit(solution)/shard_map/ppermute | solution.py:285
  36.9 12.8 %collective-permute-start.10 = (bf16[32,16,128]{2,1,0:T(8,128)(2,1)S(1)}, bf16[32,16,128]{2,1,0:T(8,128)(2,1)S(1)}, u32[]{:S(2)}, u32[]{:S(2)}) collective-permute-start(bf16[32,16,128]{2,1,0:T(8,128)(2,1)S(1)} %shard_map.81), channel_id=1, source_target_pairs={{0,1},{1,2},{2,3},{3,4},{4,5},{5,6},{6,7},{7,0},{8,9},{9,10},{10,1... | collective-permute-start | bytes 393224 | tf_op jit(solution)/shard_map/ppermute | solution.py:285
  38.9 17.1 %collective-permute-start.13 = (bf16[2,32,16,128]{3,2,1,0:T(8,128)(2,1)S(1)}, bf16[2,32,16,128]{3,2,1,0:T(8,128)(2,1)S(1)}, u32[]{:S(2)}, u32[]{:S(2)}) collective-permute-start(bf16[2,32,16,128]{3,2,1,0:T(8,128)(2,1)S(1)} %get-tuple-element.30), channel_id=1, source_target_pairs={{0,8},{8,0},{1,9},{9,1},{2,10},{10,2},{3,11},{11,3},{4,12},{12,4},... | collective-permute-start | bytes 786440 | tf_op jit(solution)/shard_map/ppermute | solution.py:285
  42.9 9.8 %collective-permute-start.18 = (bf16[32,16,128]{2,1,0:T(8,128)(2,1)S(1)}, bf16[32,16,128]{2,1,0:T(8,128)(2,1)S(1)}, u32[]{:S(2)}, u32[]{:S(2)}) collective-permute-start(bf16[32,16,128]{2,1,0:T(8,128)(2,1)S(1)} %shard_map.85), channel_id=1, source_target_pairs={{0,7},{1,0},{2,1},{3,2},{4,3},{5,4},{6,5},{7,6},{8,15},{9,8},{10,9... | collective-permute-start | bytes 393224 | tf_op jit(solution)/shard_map/ppermute | solution.py:285
  49.7 6.3 %collective-permute-start.12 = (bf16[32,16,128]{2,1,0:T(8,128)(2,1)S(1)}, bf16[32,16,128]{2,1,0:T(8,128)(2,1)S(1)}, u32[]{:S(2)}, u32[]{:S(2)}) collective-permute-start(bf16[32,16,128]{2,1,0:T(8,128)(2,1)S(1)} %shard_map.82), channel_id=1, source_target_pairs={{0,1},{1,2},{2,3},{3,4},{4,5},{5,6},{6,7},{7,0},{8,9},{9,10},{10,1... | collective-permute-start | bytes 393224 | tf_op jit(solution)/shard_map/ppermute | solution.py:285
  49.8 12.5 %collective-permute-start.15 = (bf16[2,32,16,128]{3,2,1,0:T(8,128)(2,1)S(1)}, bf16[2,32,16,128]{3,2,1,0:T(8,128)(2,1)S(1)}, u32[]{:S(2)}, u32[]{:S(2)}) collective-permute-start(bf16[2,32,16,128]{3,2,1,0:T(8,128)(2,1)S(1)} %get-tuple-element.32), channel_id=1, source_target_pairs={{0,8},{8,0},{1,9},{9,1},{2,10},{10,2},{3,11},{11,3},{4,12},{12,4},... | collective-permute-start | bytes 786440 | tf_op jit(solution)/shard_map/ppermute | solution.py:285
  52.8 5.7 %collective-permute-start.19 = (bf16[32,16,128]{2,1,0:T(8,128)(2,1)S(1)}, bf16[32,16,128]{2,1,0:T(8,128)(2,1)S(1)}, u32[]{:S(2)}, u32[]{:S(2)}) collective-permute-start(bf16[32,16,128]{2,1,0:T(8,128)(2,1)S(1)} %shard_map.86), channel_id=1, source_target_pairs={{0,7},{1,0},{2,1},{3,2},{4,3},{5,4},{6,5},{7,6},{8,15},{9,8},{10,9... | collective-permute-start | bytes 393224 | tf_op jit(solution)/shard_map/ppermute | solution.py:285
  56.1 6.3 %collective-permute-start.14 = (bf16[32,16,128]{2,1,0:T(8,128)(2,1)S(1)}, bf16[32,16,128]{2,1,0:T(8,128)(2,1)S(1)}, u32[]{:S(2)}, u32[]{:S(2)}) collective-permute-start(bf16[32,16,128]{2,1,0:T(8,128)(2,1)S(1)} %shard_map.83), channel_id=1, source_target_pairs={{0,1},{1,2},{2,3},{3,4},{4,5},{5,6},{6,7},{7,0},{8,9},{9,10},{10,1... | collective-permute-start | bytes 393224 | tf_op jit(solution)/shard_map/ppermute | solution.py:285
  58.6 6.3 %collective-permute-start.20 = (bf16[32,16,128]{2,1,0:T(8,128)(2,1)S(1)}, bf16[32,16,128]{2,1,0:T(8,128)(2,1)S(1)}, u32[]{:S(2)}, u32[]{:S(2)}) collective-permute-start(bf16[32,16,128]{2,1,0:T(8,128)(2,1)S(1)} %shard_map.87), channel_id=1, source_target_pairs={{0,7},{1,0},{2,1},{3,2},{4,3},{5,4},{6,5},{7,6},{8,15},{9,8},{10,9... | collective-permute-start | bytes 393224 | tf_op jit(solution)/shard_map/ppermute | solution.py:285
  62.4 6.3 %collective-permute-start.16 = (bf16[32,16,128]{2,1,0:T(8,128)(2,1)S(1)}, bf16[32,16,128]{2,1,0:T(8,128)(2,1)S(1)}, u32[]{:S(2)}, u32[]{:S(2)}) collective-permute-start(bf16[32,16,128]{2,1,0:T(8,128)(2,1)S(1)} %shard_map.84), channel_id=1, source_target_pairs={{0,1},{1,2},{2,3},{3,4},{4,5},{5,6},{6,7},{7,0},{8,9},{9,10},{10,1... | collective-permute-start | bytes 393224 | tf_op jit(solution)/shard_map/ppermute | solution.py:285
  71.3 7.0 %collective-permute-start.22 = (bf16[32,16,128]{2,1,0:T(8,128)(2,1)S(1)}, bf16[32,16,128]{2,1,0:T(8,128)(2,1)S(1)}, u32[]{:S(2)}, u32[]{:S(2)}) collective-permute-start(bf16[32,16,128]{2,1,0:T(8,128)(2,1)S(1)} %get-tuple-element.39.refs_0_), channel_id=1, source_target_pairs={{0,1},{1,2},{2,3},{3,4},{4,5},{5,6},{6,7},{7,0},{8,9},{9,10},{10,1... | collective-permute-start | bytes 393224 | tf_op jit(solution)/shard_map/ppermute | solution.py:285
  71.4 7.0 %collective-permute-start.23 = (bf16[32,16,128]{2,1,0:T(8,128)(2,1)S(1)}, bf16[32,16,128]{2,1,0:T(8,128)(2,1)S(1)}, u32[]{:S(2)}, u32[]{:S(2)}) collective-permute-start(bf16[32,16,128]{2,1,0:T(8,128)(2,1)S(1)} %get-tuple-element.39.refs_0_), channel_id=1, source_target_pairs={{0,7},{1,0},{2,1},{3,2},{4,3},{5,4},{6,5},{7,6},{8,15},{9,8},{10,9... | collective-permute-start | bytes 393224 | tf_op jit(solution)/shard_map/ppermute | solution.py:285
  78.3 6.2 %collective-permute-start.25 = (bf16[32,16,128]{2,1,0:T(8,128)(2,1)S(1)}, bf16[32,16,128]{2,1,0:T(8,128)(2,1)S(1)}, u32[]{:S(2)}, u32[]{:S(2)}) collective-permute-start(bf16[32,16,128]{2,1,0:T(8,128)(2,1)S(1)} %collective-permute-done.22.refs_0_.refs_2_), channel_id=1, source_target_pairs={{0,1},{1,2},{2,3},{3,4},{4,5},{5,6},{6,7},{7,0},{8,9},{9,10},{10,1... | collective-permute-start | bytes 393224 | tf_op jit(solution)/shard_map/ppermute | solution.py:285
  78.3 6.2 %collective-permute-start.26 = (bf16[32,16,128]{2,1,0:T(8,128)(2,1)S(1)}, bf16[32,16,128]{2,1,0:T(8,128)(2,1)S(1)}, u32[]{:S(2)}, u32[]{:S(2)}) collective-permute-start(bf16[32,16,128]{2,1,0:T(8,128)(2,1)S(1)} %collective-permute-done.23.refs_1_.refs_3_), channel_id=1, source_target_pairs={{0,7},{1,0},{2,1},{3,2},{4,3},{5,4},{6,5},{7,6},{8,15},{9,8},{10,9... | collective-permute-start | bytes 393224 | tf_op jit(solution)/shard_map/ppermute | solution.py:285
  84.5 7.2 %collective-permute-start.28 = (bf16[32,16,128]{2,1,0:T(8,128)(2,1)S(1)}, bf16[32,16,128]{2,1,0:T(8,128)(2,1)S(1)}, u32[]{:S(2)}, u32[]{:S(2)}) collective-permute-start(bf16[32,16,128]{2,1,0:T(8,128)(2,1)S(1)} %collective-permute-done.25.refs_0_.refs_5_), channel_id=1, source_target_pairs={{0,1},{1,2},{2,3},{3,4},{4,5},{5,6},{6,7},{7,0},{8,9},{9,10},{10,1... | collective-permute-start | bytes 393224 | tf_op jit(solution)/shard_map/ppermute | solution.py:285
  84.5 7.2 %collective-permute-start.29 = (bf16[32,16,128]{2,1,0:T(8,128)(2,1)S(1)}, bf16[32,16,128]{2,1,0:T(8,128)(2,1)S(1)}, u32[]{:S(2)}, u32[]{:S(2)}) collective-permute-start(bf16[32,16,128]{2,1,0:T(8,128)(2,1)S(1)} %collective-permute-done.26.refs_1_.refs_6_), channel_id=1, source_target_pairs={{0,7},{1,0},{2,1},{3,2},{4,3},{5,4},{6,5},{7,6},{8,15},{9,8},{10,9... | collective-permute-start | bytes 393224 | tf_op jit(solution)/shard_map/ppermute | solution.py:285
  87.8 18.0 %collective-permute-start.24 = (bf16[2,32,16,128]{3,2,1,0:T(8,128)(2,1)S(1)}, bf16[2,32,16,128]{3,2,1,0:T(8,128)(2,1)S(1)}, u32[]{:S(2)}, u32[]{:S(2)}) collective-permute-start(bf16[2,32,16,128]{3,2,1,0:T(8,128)(2,1)S(1)} %shard_map.89), channel_id=1, source_target_pairs={{0,8},{8,0},{1,9},{9,1},{2,10},{10,2},{3,11},{11,3},{4,12},{12,4},... | collective-permute-start | bytes 786440 | tf_op jit(solution)/shard_map/ppermute | solution.py:285
  90.4 15.4 %collective-permute-start.27 = (bf16[2,32,16,128]{3,2,1,0:T(8,128)(2,1)S(1)}, bf16[2,32,16,128]{3,2,1,0:T(8,128)(2,1)S(1)}, u32[]{:S(2)}, u32[]{:S(2)}) collective-permute-start(bf16[2,32,16,128]{3,2,1,0:T(8,128)(2,1)S(1)} %shard_map.90), channel_id=1, source_target_pairs={{0,8},{8,0},{1,9},{9,1},{2,10},{10,2},{3,11},{11,3},{4,12},{12,4},... | collective-permute-start | bytes 786440 | tf_op jit(solution)/shard_map/ppermute | solution.py:285
  91.7 6.2 %collective-permute-start.31 = (bf16[32,16,128]{2,1,0:T(8,128)(2,1)S(1)}, bf16[32,16,128]{2,1,0:T(8,128)(2,1)S(1)}, u32[]{:S(2)}, u32[]{:S(2)}) collective-permute-start(bf16[32,16,128]{2,1,0:T(8,128)(2,1)S(1)} %collective-permute-done.28.refs_0_.refs_8_), channel_id=1, source_target_pairs={{0,1},{1,2},{2,3},{3,4},{4,5},{5,6},{6,7},{7,0},{8,9},{9,10},{10,1... | collective-permute-start | bytes 393224 | tf_op jit(solution)/shard_map/ppermute | solution.py:285
  91.8 14.0 %collective-permute-start.30 = (bf16[2,32,16,128]{3,2,1,0:T(8,128)(2,1)S(1)}, bf16[2,32,16,128]{3,2,1,0:T(8,128)(2,1)S(1)}, u32[]{:S(2)}, u32[]{:S(2)}) collective-permute-start(bf16[2,32,16,128]{3,2,1,0:T(8,128)(2,1)S(1)} %shard_map.91), channel_id=1, source_target_pairs={{0,8},{8,0},{1,9},{9,1},{2,10},{10,2},{3,11},{11,3},{4,12},{12,4},... | collective-permute-start | bytes 786440 | tf_op jit(solution)/shard_map/ppermute | solution.py:285
  94.4 11.4 %collective-permute-start.21 = (bf16[32,16,128]{2,1,0:T(8,128)(2,1)S(1)}, bf16[32,16,128]{2,1,0:T(8,128)(2,1)S(1)}, u32[]{:S(2)}, u32[]{:S(2)}) collective-permute-start(bf16[32,16,128]{2,1,0:T(8,128)(2,1)S(1)} %get-tuple-element.39.refs_0_), channel_id=1, source_target_pairs={{0,8},{8,0},{1,9},{9,1},{2,10},{10,2},{3,11},{11,3},{4,12},{12,4},... | collective-permute-start | bytes 393224 | tf_op jit(solution)/shard_map/ppermute | solution.py:285
  97.9 9.3 %collective-permute-start.32 = (bf16[32,16,128]{2,1,0:T(8,128)(2,1)S(1)}, bf16[32,16,128]{2,1,0:T(8,128)(2,1)S(1)}, u32[]{:S(2)}, u32[]{:S(2)}) collective-permute-start(bf16[32,16,128]{2,1,0:T(8,128)(2,1)S(1)} %collective-permute-done.31.refs_11_), channel_id=1, source_target_pairs={{0,8},{8,0},{1,9},{9,1},{2,10},{10,2},{3,11},{11,3},{4,12},{12,4},... | collective-permute-start | bytes 393224 | tf_op jit(solution)/shard_map/ppermute | solution.py:285
  114.5 6.8 %collective-permute-start.35 = (bf16[32,16,128]{2,1,0:T(8,128)(2,1)S(1)}, bf16[32,16,128]{2,1,0:T(8,128)(2,1)S(1)}, u32[]{:S(2)}, u32[]{:S(2)}) collective-permute-start(bf16[32,16,128]{2,1,0:T(8,128)(2,1)S(1)} %get-tuple-element.43), channel_id=1, source_target_pairs={{0,96},{32,0},{64,32},{96,64},{1,97},{33,1},{65,33},{97,65},{2,98}... | collective-permute-start | bytes 393224 | tf_op jit(solution)/shard_map/ppermute | solution.py:285
  121.5 7.6 %collective-permute-start.36 = (bf16[2,32,16,128]{3,2,1,0:T(8,128)(2,1)S(1)}, bf16[2,32,16,128]{3,2,1,0:T(8,128)(2,1)S(1)}, u32[]{:S(2)}, u32[]{:S(2)}) collective-permute-start(bf16[2,32,16,128]{3,2,1,0:T(8,128)(2,1)S(1)} %get-tuple-element.44), channel_id=1, source_target_pairs={{0,32},{32,64},{64,96},{96,0},{1,33},{33,65},{65,97},{97,1},{2,34}... | collective-permute-start | bytes 786440 | tf_op jit(solution)/shard_map/ppermute | solution.py:285
  121.8 8.7 %collective-permute-start.37 = (bf16[2,32,16,128]{3,2,1,0:T(8,128)(2,1)S(1)}, bf16[2,32,16,128]{3,2,1,0:T(8,128)(2,1)S(1)}, u32[]{:S(2)}, u32[]{:S(2)}) collective-permute-start(bf16[2,32,16,128]{3,2,1,0:T(8,128)(2,1)S(1)} %get-tuple-element.45), channel_id=1, source_target_pairs={{0,96},{32,0},{64,32},{96,64},{1,97},{33,1},{65,33},{97,65},{2,98}... | collective-permute-start | bytes 786440 | tf_op jit(solution)/shard_map/ppermute | solution.py:285
  (11 other events, 201.6 us)
